TPU v7x, 32 devices: a whole 2x2x4 slice. The times are simulated.
32 devices in a mesh: blk: 8 (over y, x, core), table: 4 (over z).
Axes of the slice: x: 2, y: 2, z: 4, core: 2. Of those that a mesh axis runs over, the one named last changes fastest.
Arguments:
- queries: bfloat16 [16384, 256], P(('blk', 'table')), may hold values from -20 to 20
- items: bfloat16 [16384, 256], P(('blk', 'table')), may hold values from -4.8 to 4.8
- positives: int32 [16384], P(('blk', 'table')), may hold values from 0 to 511
- item_owner: int32 [16384, 1], P(('blk', 'table')), may hold values from 0 to 31; in each aligned block of 512 rows (0 to 511, 512 to 1023, ...) at most 48 rows name the same one
- item_row: int32 [16384], P(('blk', 'table')), may hold values from 0 to 16383
Outputs:
- query_grad: bfloat16 [16384, 256], P(('blk', 'table'))
- item_grad: bfloat16 [16384, 256], P(('blk', 'table'))
- table_grad: bfloat16 [524288, 256], P(('blk', 'table'))
Inputs may be any that keep to these rules, and one draw needn't show every extreme that they name: `item_owner`: among the rows of one device, no owner is named more than 48 times, a bound that some block reaches.
All inputs are finite; a program needn't handle non-finite values.
Results may differ from a plain program's by a relative error of at most 0.0034.
Values may be sent and summed in bfloat16 or wider, within the bound.
No kernel may reach another device: no remote copies, remote signals or barrier semaphores. Data moves between devices by JAX's collectives and lax.ppermute only.
A program may use at most 64 MiB of HBM per device.

v0:
```python
import functools
import math

import jax
import jax.numpy as jnp
from jax import lax
from jax.experimental import pallas as pl
from jax.experimental.pallas import tpu as pltpu
from jax.sharding import PartitionSpec as P


ROWS_DEV = 16384
LANES = 128
SUB = 256
LOG2E = math.log2(math.e)
NT = (((1,), (1,)), ((), ()))
TN = (((0,), (0,)), ((), ()))


def moved(block, axis, target_of):
    count = lax.axis_size(axis)
    return lax.ppermute(block, axis, [(i, target_of(i) % count) for i in range(count)])


def vmem():
    return pl.BlockSpec(memory_space=pltpu.VMEM)


def params(mib):
    return pltpu.CompilerParams(vmem_limit_bytes=mib * 2**20)


def call(body, out_shape, args, flops=0, trans=0, mib=12):
    moved_bytes = sum(a.size * a.dtype.itemsize for a in args)
    outs = out_shape if isinstance(out_shape, (tuple, list)) else (out_shape,)
    moved_bytes += sum(math.prod(o.shape) * o.dtype.itemsize for o in outs)
    specs = [vmem() for _ in outs]
    return pl.pallas_call(
        body,
        out_shape=out_shape,
        in_specs=[vmem() for _ in args],
        out_specs=specs if isinstance(out_shape, (tuple, list)) else specs[0],
        cost_estimate=pl.CostEstimate(flops=flops, bytes_accessed=moved_bytes, transcendentals=trans),
        compiler_params=params(mib),
    )(*args)


def iota(shape, dim, dtype=jnp.int32):
    value = lax.broadcasted_iota(jnp.int32, shape, dim)
    return value if dtype == jnp.int32 else value.astype(dtype)


def column(row):
    wide = jnp.broadcast_to(row, (LANES, LANES))
    return jnp.transpose(wide)


def one_hot(shape, row, base):
    there = (iota(shape, 0) + base).astype(jnp.int16)
    return jnp.where(there == row.astype(jnp.int16), jnp.bfloat16(1), jnp.bfloat16(0))


def route_kernel(devices, capacity, owner_ref, row_ref, slot_ref, ids_ref):
    size = owner_ref.shape[1]
    owner = owner_ref[...]
    rank = jnp.zeros((1, size), jnp.float32)
    for base in range(0, size, LANES):
        col = column(owner[:, base : base + LANES])
        col = jnp.concatenate([col] * (size // LANES), axis=1)
        here = iota((LANES, size), 0) + base
        hit = (col == owner) & (here < iota((LANES, size), 1))
        rank = rank + jnp.sum(jnp.where(hit, 1.0, 0.0), axis=0, keepdims=True)
    rank = rank.astype(jnp.int32)
    slot_ref[...] = owner * capacity + rank
    row = row_ref[...]
    high = (lax.shift_right_logical(row, 7) + 1).astype(jnp.float32)
    low = (row & 127).astype(jnp.float32)
    mine = iota((devices, size), 0) == owner
    place = one_hot((LANES, size), rank, 0)
    high = jnp.where(mine, high, 0.0).astype(jnp.bfloat16)
    low = jnp.where(mine, low, 0.0).astype(jnp.bfloat16)
    high = lax.dot_general(high, place, NT, preferred_element_type=jnp.float32)
    low = lax.dot_general(low, place, NT, preferred_element_type=jnp.float32)
    value = jnp.where(high > 0.5, (high - 1.0) * 128.0 + low, float(ROWS_DEV))
    ids_ref[...] = value.astype(jnp.int32)


def order_kernel(capacity, group, ids_ref, rank_ref, sorted_ref, count_ref):
    devices = ids_ref.shape[0]
    slots = devices * capacity
    chunks = slots // LANES
    ids = ids_ref[...]
    lane = iota((1, LANES), 1)
    rolled = {}
    rows = [jnp.zeros((1, LANES), jnp.int32) for _ in range(chunks)]
    for s in range(devices):
        at, off = divmod(s * capacity, LANES)
        if off not in rolled:
            rolled[off] = pltpu.roll(ids, off, 1) if off else ids
        piece = rolled[off][s : s + 1, :]
        rows[at] = jnp.where((lane >= off) & (lane < off + capacity), piece, rows[at])
        if off + capacity > LANES:
            rows[at + 1] = jnp.where(lane < off + capacity - LANES, piece, rows[at + 1])
    edges = lane * group
    count = jnp.zeros((1, LANES), jnp.float32)
    ranks = [jnp.zeros((1, LANES), jnp.float32) for _ in range(chunks)]
    earlier = iota((LANES, LANES), 0) < iota((LANES, LANES), 1)
    for j in range(chunks):
        col = column(rows[j])
        count = count + jnp.sum(jnp.where(col < edges, 1.0, 0.0), axis=0, keepdims=True)
        for i in range(chunks):
            if j < i:
                hit = col <= rows[i]
            elif j > i:
                hit = col < rows[i]
            else:
                hit = (col < rows[i]) | ((col == rows[i]) & earlier)
            ranks[i] = ranks[i] + jnp.sum(jnp.where(hit, 1.0, 0.0), axis=0, keepdims=True)
    count_ref[...] = count.astype(jnp.int32)
    rank = jnp.concatenate(ranks, axis=1).astype(jnp.int32)
    rank_ref[...] = rank
    row = jnp.concatenate(rows, axis=1)
    high = jnp.broadcast_to(lax.shift_right_logical(row, 7).astype(jnp.float32), (8, slots)).astype(jnp.bfloat16)
    low = jnp.broadcast_to((row & 127).astype(jnp.float32), (8, slots)).astype(jnp.bfloat16)
    for c in range(chunks):
        pick = one_hot((LANES, slots), rank, c * LANES)
        up = lax.dot_general(high, pick, NT, preferred_element_type=jnp.float32)
        down = lax.dot_general(low, pick, NT, preferred_element_type=jnp.float32)
        sorted_ref[c : c + 1, :] = (up * 128.0 + down)[0:1, :].astype(jnp.int32)


def stats_kernel(scale, blocks, olds, *refs):
    q_ref = refs[0]
    k_refs = refs[1 : 1 + blocks]
    old = refs[1 + blocks : 1 + blocks + olds]
    top_ref, total_ref = refs[-2:]
    size = q_ref.shape[0]
    for base in range(0, size, SUB):
        q = q_ref[base : base + SUB, :]
        at = slice(base, base + SUB)
        top = old[0][:, at] if old else None
        total = old[1][:, at] if old else None
        for k in k_refs:
            scores = scale * lax.dot_general(k[...], q, NT, preferred_element_type=jnp.float32)
            high = jnp.max(scores, axis=0, keepdims=True)
            high = high if top is None else jnp.maximum(top, high)
            part = jnp.sum(jnp.exp2(scores - high), axis=0, keepdims=True)
            total = part if top is None else total * jnp.exp2(top - high) + part
            top = high
        top_ref[:, at] = top + jnp.log2(total) if old else top
        total_ref[:, at] = total


def query_kernel(scale, blocks, q_ref, lse_ref, pos_ref, *refs):
    k_refs, out_ref = refs[:blocks], refs[-1]
    size = q_ref.shape[0]
    for base in range(0, size, SUB):
        at = slice(base, base + SUB)
        q = q_ref[at, :]
        total = None
        for m, k in enumerate(k_refs):
            scores = (scale * LOG2E) * lax.dot_general(k[...], q, NT, preferred_element_type=jnp.float32)
            weights = jnp.exp2(scores - lse_ref[:, at])
            if m == 0:
                weights = weights - jnp.where(iota((size, SUB), 0) == pos_ref[:, at], 1.0, 0.0)
            part = lax.dot_general(weights.astype(jnp.bfloat16), k[...], TN, preferred_element_type=jnp.float32)
            total = part if total is None else total + part
        out_ref[at, :] = (scale * total).astype(jnp.bfloat16)


def item_kernel(scale, blocks, k_ref, slot_ref, pos_ref, *refs):
    q_refs, lse_refs = refs[:blocks], refs[blocks : 2 * blocks]
    out_ref, send_ref = refs[-2:]
    size = k_ref.shape[0]
    keys = k_ref[...]
    total = None
    for m in range(blocks):
        for base in range(0, size, SUB):
            at = slice(base, base + SUB)
            q = q_refs[m][at, :]
            scores = (scale * LOG2E) * lax.dot_general(keys, q, NT, preferred_element_type=jnp.float32)
            weights = jnp.exp2(scores - lse_refs[m][:, at])
            if m == 0:
                weights = weights - jnp.where(iota((size, SUB), 0) == pos_ref[:, at], 1.0, 0.0)
            part = jnp.dot(weights.astype(jnp.bfloat16), q, preferred_element_type=jnp.float32)
            total = part if total is None else total + part
    grad = (scale * total).astype(jnp.bfloat16)
    out_ref[...] = grad
    for base in range(0, send_ref.shape[0], SUB):
        pick = one_hot((SUB, size), slot_ref[...], base)
        part = jnp.dot(pick, grad, preferred_element_type=jnp.float32)
        send_ref[base : base + SUB, :] = part.astype(jnp.bfloat16)


def table_kernel(groups, count_ref, rows_ref, rank_ref, sorted_ref, out_ref, pick, arranged, total):
    step = pl.program_id(0)
    chunks = arranged.shape[0] // LANES
    width = rows_ref.shape[1]

    @pl.when(step == 0)
    def _():
        for at in range(0, chunks * LANES, SUB):
            pick[at : at + SUB, :] = one_hot((SUB, chunks * LANES), rank_ref[...], at)
        arranged[...] = jnp.dot(pick[...], rows_ref[...], preferred_element_type=jnp.float32).astype(jnp.bfloat16)

    def spread(chunk, base):
        at = pl.multiple_of(chunk * LANES, LANES)
        ids = jnp.concatenate([sorted_ref[pl.ds(chunk, 1), :], sorted_ref[pl.ds(chunk + 1, 1), :]], axis=1)
        hot = one_hot((SUB, 2 * LANES), ids - base, 0)
        return jnp.dot(hot, arranged[pl.ds(at, 2 * LANES), :], preferred_element_type=jnp.float32)

    firsts = [jnp.minimum(count_ref[step * groups + g] // LANES, chunks - 2) for g in range(groups)]
    overs = [count_ref[step * groups + g + 1] > (firsts[g] + 2) * LANES for g in range(groups)]
    for g in range(groups):
        out_ref[g * SUB : (g + 1) * SUB, :] = spread(firsts[g], (step * groups + g) * SUB).astype(jnp.bfloat16)

    @pl.when(functools.reduce(jnp.logical_or, overs))
    def _():
        def group(g, carry):
            base = (step * groups + g) * SUB
            total[...] = jnp.zeros((SUB, width), jnp.float32)

            def more(pair, inner):
                total[...] += spread(2 * pair, base)
                return inner

            lax.fori_loop(0, chunks // 2, more, 0)
            out_ref[pl.ds(pl.multiple_of(g * SUB, SUB), SUB), :] = total[...].astype(jnp.bfloat16)
            return carry

        lax.fori_loop(0, groups, group, 0)


def local(queries, items, positives, item_owner, item_row):
    size, width = queries.shape
    scale = 3.0 / math.sqrt(width)
    blk_count = lax.axis_size("blk")
    window = blk_count // 2
    devices = blk_count * lax.axis_size("table")
    capacity = -(-(3 * size // devices) // 8) * 8
    slots = devices * capacity
    f32 = functools.partial(jax.ShapeDtypeStruct, dtype=jnp.float32)
    b16 = functools.partial(jax.ShapeDtypeStruct, dtype=jnp.bfloat16)
    i32 = functools.partial(jax.ShapeDtypeStruct, dtype=jnp.int32)

    owner_row = item_owner.reshape(1, size)
    row_row = item_row.reshape(1, size)
    pos_row = positives.reshape(1, size)

    pair = 2 * size * size * width
    twos = range(1, window // 2)
    k_two = [moved(items, "blk", lambda i, j=j: i + 2 * j) for j in twos]
    k_odd = moved(items, "blk", lambda i: i + window - 1 if i % 2 else i + 1)
    q_two = [moved(queries, "blk", lambda i, j=j: i - 2 * j) for j in twos]
    q_odd = moved(queries, "blk", lambda i: i - 1 if i % 2 else i - (window - 1))
    slot, ids = call(
        functools.partial(route_kernel, devices, capacity),
        (i32((1, size)), i32((devices, LANES))),
        (owner_row, row_row),
        flops=4 * devices * LANES * size,
    )
    got_ids = lax.all_to_all(
        ids.reshape(devices, 1, LANES), ("blk", "table"), split_axis=0, concat_axis=0, tiled=True
    ).reshape(devices, LANES)
    top, total = call(
        functools.partial(stats_kernel, scale * LOG2E, 1, 0),
        (f32((1, size)), f32((1, size))),
        (queries, items),
        flops=pair,
        trans=size * size,
    )
    k_two, q_two, got_ids = lax.optimization_barrier((k_two, q_two, got_ids))
    k_swap = [moved(k, "blk", lambda i: i ^ 1) for k in k_two]
    q_swap = [moved(q, "blk", lambda i: i ^ 1) for q in q_two]
    k_all = [k_odd, *k_two, *k_swap]
    q_all = [q_odd, *q_two, *q_swap]
    table_groups = ROWS_DEV // SUB
    lse, _ = call(
        functools.partial(stats_kernel, scale * LOG2E, len(k_all), 2),
        (f32((1, size)), f32((1, size))),
        (queries, *k_all, top, total),
        flops=pair * len(k_all),
        trans=size * size * len(k_all),
    )
    got_rank, got_sorted, got_count = call(
        functools.partial(order_kernel, capacity, SUB),
        (i32((1, slots)), i32((slots // LANES, LANES)), i32((1, LANES))),
        (got_ids,),
        flops=32 * slots * slots,
    )
    lse_odd = moved(lse, "blk", lambda i: i - 1 if i % 2 else i - (window - 1))
    lse_two = [moved(lse, "blk", lambda i, j=j: i - 2 * j) for j in twos]
    lse_swap = [moved(lse, "blk", lambda i, j=j: (i ^ 1) - 2 * j) for j in twos]
    lse_all = [lse_odd, *lse_two, *lse_swap]

    query_grad = call(
        functools.partial(query_kernel, scale, window),
        b16((size, width)),
        (queries, lse, pos_row, items, *k_all),
        flops=2 * pair * window,
        trans=size * size * window,
    )
    item_grad, send_rows = call(
        functools.partial(item_kernel, scale, window),
        (b16((size, width)), b16((slots, width))),
        (items, slot, pos_row, queries, *q_all, lse, *lse_all),
        flops=2 * pair * window + 2 * slots * size * width,
        trans=size * size * window,
    )
    got_rows = lax.all_to_all(
        send_rows.reshape(devices, capacity, width), ("blk", "table"), split_axis=0, concat_axis=0, tiled=True
    ).reshape(slots, width)
    groups = 8
    table_grad = pl.pallas_call(
        functools.partial(table_kernel, groups),
        out_shape=b16((ROWS_DEV, width)),
        grid_spec=pltpu.PrefetchScalarGridSpec(
            num_scalar_prefetch=1,
            grid=(table_groups // groups,),
            in_specs=[vmem(), vmem(), vmem()],
            out_specs=pl.BlockSpec((groups * SUB, width), lambda i, count: (i, 0)),
            scratch_shapes=[pltpu.VMEM((slots, slots), jnp.bfloat16), pltpu.VMEM((slots, width), jnp.bfloat16), pltpu.VMEM((SUB, width), jnp.float32)],
        ),
        compiler_params=params(24),
        cost_estimate=pl.CostEstimate(
            flops=2 * slots * slots * width, bytes_accessed=2 * ROWS_DEV * width, transcendentals=0
        ),
    )(got_count.reshape(LANES), got_rows, got_rank, got_sorted)
    return (query_grad, item_grad, table_grad)


def solution(mesh):
    both = P(("blk", "table"), None)
    flat = P(("blk", "table"))
    return jax.shard_map(
        local, mesh=mesh, in_specs=(both, both, flat, both, flat), out_specs=(both, both, both), check_vma=False
    )
```

profile of v0, /device:TPU:1, one launch (start us, length us, event | category | flops | bytes accessed | tf_op | source)
XLA Modules:
  0.0 66.2 jit_solution(10139107353487477742)
XLA Ops:
  0.6 0.0 copy-start.8
  0.6 2.1 %collective-permute-start.1 = (bf16[512,256]{1,0:T(8,128)(2,1)}, bf16[512,256]{1,0:T(8,128)(2,1)S(1)}, u32[]{:S(2)}, u32[]{:S(2)}) collective-permute-start(bf16[512,256]{1,0:T(8,128)(2,1)} %k_ref.1), channel_id=1, source_target_pairs={{0,8},{4,12},{8,16},{12,20},{16,24},{20,28},{24,0},{28,4},{1,9},{5... | collective-permute-start | bytes 786440 | tf_op jit(solution)/shard_map/ppermute | solution.py:22
  2.7 1.0 %collective-permute-start.2 = (bf16[512,256]{1,0:T(8,128)(2,1)}, bf16[512,256]{1,0:T(8,128)(2,1)S(1)}, u32[]{:S(2)}, u32[]{:S(2)}) collective-permute-start(bf16[512,256]{1,0:T(8,128)(2,1)} %refs_0_.7), channel_id=1, source_target_pairs={{0,24},{4,28},{8,0},{12,4},{16,8},{20,12},{24,16},{28,20},{1,25},{... | collective-permute-start | bytes 786440 | tf_op jit(solution)/shard_map/ppermute | solution.py:22
  3.7 0.7 %copy-done.5 = s32[512,1]{0,1:T(1,128)S(1)} copy-done((s32[512,1]{0,1:T(1,128)S(1)}, s32[512,1]{0,1:T(1,128)}, u32[]{:S(2)}) %copy-start.5) | copy-done | bytes 2072
  4.4 0.7 %copy-done.6 = s32[512]{0:T(512)S(1)} copy-done((s32[512]{0:T(512)S(1)}, s32[512]{0:T(512)}, u32[]{:S(2)}) %copy-start.6) | copy-done | bytes 2072
  5.1 0.9 %shard_map.76 = (s32[1,512]{1,0:T(1,128)S(1)}, s32[32,128]{1,0:T(8,128)}) custom-call(s32[1,512]{1,0:T(1,128)S(1)} %bitcast.13, s32[1,512]{1,0:T(1,128)S(1)} %bitcast.14), custom_call_target="tpu_custom_call" | custom-call | flops 8388608 | bytes 22528 | tf_op jit(solution)/shard_map/pallas_call | solution.py:38
  6.0 6.1 %all-to-all-start = ((s32[32,1,128]{2,1,0:T(1,128)}), s32[32,1,128]{2,1,0:T(1,128)S(1)}, u32[]{:S(2)}, u32[]{:S(2)}) async-start(s32[32,1,128]{2,1,0:T(1,128)} %bitcast.3), calls=%async_computation | async-start | bytes 32768 | tf_op jit(solution)/shard_map/all_to_all | solution.py:262
  12.1 1.7 %collective-permute-start = (bf16[512,256]{1,0:T(8,128)(2,1)}, bf16[512,256]{1,0:T(8,128)(2,1)S(1)}, u32[]{:S(2)}, u32[]{:S(2)}) collective-permute-start(bf16[512,256]{1,0:T(8,128)(2,1)} %k_ref.1), channel_id=1, source_target_pairs={{0,4},{4,16},{8,12},{12,24},{16,20},{20,0},{24,28},{28,8},{1,5},{5... | collective-permute-start | bytes 786440 | tf_op jit(solution)/shard_map/ppermute | solution.py:22
  13.8 5.0 %all-to-all-done = s32[32,1,128]{2,1,0:T(1,128)S(1)} async-done(((s32[32,1,128]{2,1,0:T(1,128)}), s32[32,1,128]{2,1,0:T(1,128)S(1)}, u32[]{:S(2)}, u32[]{:S(2)}) %all-to-all-start) | async-done | bytes 16416 | tf_op jit(solution)/shard_map/all_to_all | solution.py:262
  18.8 0.7 %collective-permute-start.3 = (bf16[512,256]{1,0:T(8,128)(2,1)S(1)}, bf16[512,256]{1,0:T(8,128)(2,1)S(1)}, u32[]{:S(2)}, u32[]{:S(2)}) collective-permute-start(bf16[512,256]{1,0:T(8,128)(2,1)S(1)} %collective-permute-done.1.refs_2_), channel_id=1, source_target_pairs={{0,4},{4,0},{8,12},{12,8},{16,20},{20,16},{24,28},{28,24},{1,5},{5... | collective-permute-start | bytes 786440 | tf_op jit(solution)/shard_map/ppermute | solution.py:22
  19.5 0.1 collective-permute-start.4
  19.6 0.6 collective-permute-start.5
  20.2 0.9 %copy-done = bf16[512,256]{1,0:T(8,128)(2,1)S(1)} copy-done((bf16[512,256]{1,0:T(8,128)(2,1)S(1)}, bf16[512,256]{1,0:T(8,128)(2,1)}, u32[]{:S(2)}) %copy-start) | copy-done | bytes 262168
  21.2 0.9 %copy-done.2 = bf16[512,256]{1,0:T(8,128)(2,1)S(1)} copy-done((bf16[512,256]{1,0:T(8,128)(2,1)S(1)}, bf16[512,256]{1,0:T(8,128)(2,1)}, u32[]{:S(2)}) %copy-start.2) | copy-done | bytes 262168
  22.1 0.5 shard_map.77
  22.7 1.6 %shard_map.78 = (f32[1,512]{1,0:T(1,128)S(1)}, f32[1,512]{1,0:T(1,128)}) custom-call(bf16[512,256]{1,0:T(8,128)(2,1)S(1)} %copy-done, bf16[512,256]{1,0:T(8,128)(2,1)S(1)} %collective-permute-done.refs_1_, bf16[512,256]{1,0:T(8,128)(2,1)S(1)} %collective-permute-done.1.refs_2_, bf16[512,256]{1,0:T(8,128)(2,1)S(1)} %collective-permute-done.3.refs_3_, ...), custom_call_target="tpu_custom_call" | custom-call | flops 402653184 | bytes 1056768 | tf_op jit(solution)/shard_map/pallas_call | solution.py:38
  24.3 1.1 %collective-permute-start.8 = (f32[1,512]{1,0:T(1,128)S(1)}, f32[1,512]{1,0:T(1,128)S(1)}, u32[]{:S(2)}, u32[]{:S(2)}) collective-permute-start(f32[1,512]{1,0:T(1,128)S(1)} %get-tuple-element.20.lse_ref.refs_4_), channel_id=1, source_target_pairs={{0,28},{4,24},{8,4},{12,0},{16,12},{20,8},{24,20},{28,16},{1,29},{... | collective-permute-start | bytes 6152 | tf_op jit(solution)/shard_map/ppermute | solution.py:22
  25.5 1.1 %collective-permute-start.7 = (f32[1,512]{1,0:T(1,128)S(1)}, f32[1,512]{1,0:T(1,128)S(1)}, u32[]{:S(2)}, u32[]{:S(2)}) collective-permute-start(f32[1,512]{1,0:T(1,128)S(1)} %get-tuple-element.20.lse_ref.refs_4_), channel_id=1, source_target_pairs={{0,24},{4,28},{8,0},{12,4},{16,8},{20,12},{24,16},{28,20},{1,25},{... | collective-permute-start | bytes 6152 | tf_op jit(solution)/shard_map/ppermute | solution.py:22
  26.6 0.8 %collective-permute-start.6 = (f32[1,512]{1,0:T(1,128)S(1)}, f32[1,512]{1,0:T(1,128)S(1)}, u32[]{:S(2)}, u32[]{:S(2)}) collective-permute-start(f32[1,512]{1,0:T(1,128)S(1)} %get-tuple-element.20.lse_ref.refs_4_), channel_id=1, source_target_pairs={{0,20},{4,0},{8,28},{12,8},{16,4},{20,16},{24,12},{28,24},{1,21},{... | collective-permute-start | bytes 6152 | tf_op jit(solution)/shard_map/ppermute | solution.py:22
  27.3 0.0 collective-permute-done.4.refs_1_
  27.3 0.0 collective-permute-done.5.refs_3_
  27.3 0.6 collective-permute-done.7.refs_6_
  27.9 1.7 %collective-permute-done.6.refs_5_ = f32[1,512]{1,0:T(1,128)S(1)} collective-permute-done((f32[1,512]{1,0:T(1,128)S(1)}, f32[1,512]{1,0:T(1,128)S(1)}, u32[]{:S(2)}, u32[]{:S(2)}) %collective-permute-start.6) | collective-permute-done | bytes 2080 | tf_op jit(solution)/shard_map/ppermute | solution.py:22
  29.6 0.9 %copy-done.3 = bf16[512,256]{1,0:T(8,128)(2,1)S(1)} copy-done((bf16[512,256]{1,0:T(8,128)(2,1)S(1)}, bf16[512,256]{1,0:T(8,128)(2,1)}, u32[]{:S(2)}) %copy-start.3) | copy-done | bytes 262168
  30.5 0.7 %copy-done.7 = s32[512]{0:T(512)S(1)} copy-done((s32[512]{0:T(512)S(1)}, s32[512]{0:T(512)}, u32[]{:S(2)}) %copy-start.7) | copy-done | bytes 2072
  31.2 3.0 %shard_map.80 = (bf16[512,256]{1,0:T(8,128)(2,1)}, bf16[1536,256]{1,0:T(8,128)(2,1)}) custom-call(bf16[512,256]{1,0:T(8,128)(2,1)S(1)} %copy-done.3, s32[1,512]{1,0:T(1,128)S(1)} %get-tuple-element.21.slot_ref, s32[1,512]{1,0:T(1,128)S(1)} %bitcast.15, bf16[512,256]{1,0:T(8,128)(2,1)S(1)} %copy-done, bf16[512,256]{1,0:T(8,128)(2,1)S(1)} %collective-permute-done.4.refs_1_, ...), custom_call_target="tpu_custom_call" | custom-call | flops 1476395008 | bytes 2371584 | tf_op jit(solution)/shard_map/pallas_call | solution.py:38
  34.2 3.1 %all-to-all-start.1 = ((bf16[32,48,256]{2,1,0:T(8,128)(2,1)}), bf16[32,48,256]{2,1,0:T(8,128)(2,1)S(1)}, u32[]{:S(2)}, u32[]{:S(2)}) async-start(bf16[32,48,256]{2,1,0:T(8,128)(2,1)} %bitcast.7), calls=%async_computation.1 | async-start | bytes 1572864 | tf_op jit(solution)/shard_map/all_to_all | solution.py:310
  37.3 3.9 %shard_map.81 = (s32[1,1536]{1,0:T(1,128)S(1)}, s32[12,128]{1,0:T(8,128)S(1)}, s32[1,128]{1,0:T(1,128)S(1)}) custom-call(s32[32,128]{1,0:T(8,128)S(1)} %bitcast.11), custom_call_target="tpu_custom_call" | custom-call | flops 75497472 | bytes 29184 | tf_op jit(solution)/shard_map/pallas_call | solution.py:38
  41.2 0.0 copy-done.4
  41.2 2.4 %shard_map.79 = bf16[512,256]{1,0:T(8,128)(2,1)} custom-call(bf16[512,256]{1,0:T(8,128)(2,1)S(1)} %copy-done.1, f32[1,512]{1,0:T(1,128)S(1)} %get-tuple-element.20.lse_ref.refs_4_, s32[1,512]{1,0:T(1,128)S(1)} %bitcast.16, bf16[512,256]{1,0:T(8,128)(2,1)S(1)} %copy-done.4, bf16[512,256]{1,0:T(8,128)(2,1)S(1)} %collective-permute-done.refs_1_, ...), custom_call_target="tpu_custom_call" | custom-call | flops 1073741824 | bytes 1576960 | tf_op jit(solution)/shard_map/pallas_call | solution.py:38
  43.6 14.5 %all-to-all-done.1 = bf16[32,48,256]{2,1,0:T(8,128)(2,1)S(1)} async-done(((bf16[32,48,256]{2,1,0:T(8,128)(2,1)}), bf16[32,48,256]{2,1,0:T(8,128)(2,1)S(1)}, u32[]{:S(2)}, u32[]{:S(2)}) %all-to-all-start.1) | async-done | bytes 786464 | tf_op jit(solution)/shard_map/all_to_all | solution.py:310
  58.1 8.1 %shard_map.82 = bf16[16384,256]{1,0:T(8,128)(2,1)} custom-call(s32[128]{0:T(128)S(1)} %bitcast.12, bf16[1536,256]{1,0:T(8,128)(2,1)S(1)} %bitcast.10, s32[1,1536]{1,0:T(1,128)S(1)} %get-tuple-element.27.rank_ref, s32[12,128]{1,0:T(8,128)S(1)} %get-tuple-element.28.sorted_ref), custom_call_target="tpu_custom_call" | custom-call | flops 1207959552 | bytes 8388608 | tf_op jit(solution)/shard_map/pallas_call | solution.py:314
  (15 shorter events, 0.0 us)
Async XLA Ops:
  0.6 40.6 %copy-start.8 = (s32[512]{0:T(512)S(1)}, s32[512]{0:T(512)}, u32[]{:S(2)}) copy-start(s32[512]{0:T(512)} %param.7) | copy-start | bytes 6148
  0.6 18.1 %collective-permute-start.1 = (bf16[512,256]{1,0:T(8,128)(2,1)}, bf16[512,256]{1,0:T(8,128)(2,1)S(1)}, u32[]{:S(2)}, u32[]{:S(2)}) collective-permute-start(bf16[512,256]{1,0:T(8,128)(2,1)} %k_ref.1), channel_id=1, source_target_pairs={{0,8},{4,12},{8,16},{12,20},{16,24},{20,28},{24,0},{28,4},{1,9},{5... | collective-permute-start | bytes 786440 | tf_op jit(solution)/shard_map/ppermute | solution.py:22
  2.7 16.0 %collective-permute-start.2 = (bf16[512,256]{1,0:T(8,128)(2,1)}, bf16[512,256]{1,0:T(8,128)(2,1)S(1)}, u32[]{:S(2)}, u32[]{:S(2)}) collective-permute-start(bf16[512,256]{1,0:T(8,128)(2,1)} %refs_0_.7), channel_id=1, source_target_pairs={{0,24},{4,28},{8,0},{12,4},{16,8},{20,12},{24,16},{28,20},{1,25},{... | collective-permute-start | bytes 786440 | tf_op jit(solution)/shard_map/ppermute | solution.py:22
  3.7 0.7 %copy-start.5 = (s32[512,1]{0,1:T(1,128)S(1)}, s32[512,1]{0,1:T(1,128)}, u32[]{:S(2)}) copy-start(s32[512,1]{0,1:T(1,128)} %param.8) | copy-start | bytes 6148
  4.4 0.7 %copy-start.6 = (s32[512]{0:T(512)S(1)}, s32[512]{0:T(512)}, u32[]{:S(2)}) copy-start(s32[512]{0:T(512)} %param.9) | copy-start | bytes 6148
  6.0 12.7 %all-to-all-start = ((s32[32,1,128]{2,1,0:T(1,128)}), s32[32,1,128]{2,1,0:T(1,128)S(1)}, u32[]{:S(2)}, u32[]{:S(2)}) async-start(s32[32,1,128]{2,1,0:T(1,128)} %bitcast.3), calls=%async_computation | async-start | bytes 32768 | tf_op jit(solution)/shard_map/all_to_all | solution.py:262
  12.1 10.5 %collective-permute-start = (bf16[512,256]{1,0:T(8,128)(2,1)}, bf16[512,256]{1,0:T(8,128)(2,1)S(1)}, u32[]{:S(2)}, u32[]{:S(2)}) collective-permute-start(bf16[512,256]{1,0:T(8,128)(2,1)} %k_ref.1), channel_id=1, source_target_pairs={{0,4},{4,16},{8,12},{12,24},{16,20},{20,0},{24,28},{28,8},{1,5},{5... | collective-permute-start | bytes 786440 | tf_op jit(solution)/shard_map/ppermute | solution.py:22
  18.8 3.9 %collective-permute-start.3 = (bf16[512,256]{1,0:T(8,128)(2,1)S(1)}, bf16[512,256]{1,0:T(8,128)(2,1)S(1)}, u32[]{:S(2)}, u32[]{:S(2)}) collective-permute-start(bf16[512,256]{1,0:T(8,128)(2,1)S(1)} %collective-permute-done.1.refs_2_), channel_id=1, source_target_pairs={{0,4},{4,0},{8,12},{12,8},{16,20},{20,16},{24,28},{28,24},{1,5},{5... | collective-permute-start | bytes 786440 | tf_op jit(solution)/shard_map/ppermute | solution.py:22
  19.5 7.8 %collective-permute-start.4 = (bf16[512,256]{1,0:T(8,128)(2,1)}, bf16[512,256]{1,0:T(8,128)(2,1)S(1)}, u32[]{:S(2)}, u32[]{:S(2)}) collective-permute-start(bf16[512,256]{1,0:T(8,128)(2,1)} %refs_0_.7), channel_id=1, source_target_pairs={{0,20},{4,0},{8,28},{12,8},{16,4},{20,16},{24,12},{28,24},{1,21},{... | collective-permute-start | bytes 786440 | tf_op jit(solution)/shard_map/ppermute | solution.py:22
  19.6 7.8 %collective-permute-start.5 = (bf16[512,256]{1,0:T(8,128)(2,1)S(1)}, bf16[512,256]{1,0:T(8,128)(2,1)S(1)}, u32[]{:S(2)}, u32[]{:S(2)}) collective-permute-start(bf16[512,256]{1,0:T(8,128)(2,1)S(1)} %collective-permute-done.2.refs_2_), channel_id=1, source_target_pairs={{0,4},{4,0},{8,12},{12,8},{16,20},{20,16},{24,28},{28,24},{1,5},{5... | collective-permute-start | bytes 786440 | tf_op jit(solution)/shard_map/ppermute | solution.py:22
  20.2 0.9 %copy-start = (bf16[512,256]{1,0:T(8,128)(2,1)S(1)}, bf16[512,256]{1,0:T(8,128)(2,1)}, u32[]{:S(2)}) copy-start(bf16[512,256]{1,0:T(8,128)(2,1)} %refs_0_.7) | copy-start | bytes 786436
  21.2 0.9 %copy-start.2 = (bf16[512,256]{1,0:T(8,128)(2,1)S(1)}, bf16[512,256]{1,0:T(8,128)(2,1)}, u32[]{:S(2)}) copy-start(bf16[512,256]{1,0:T(8,128)(2,1)} %k_ref.1) | copy-start | bytes 786436
  22.1 19.1 %copy-start.1 = (bf16[512,256]{1,0:T(8,128)(2,1)S(1)}, bf16[512,256]{1,0:T(8,128)(2,1)}, u32[]{:S(2)}) copy-start(bf16[512,256]{1,0:T(8,128)(2,1)} %refs_0_.7) | copy-start | bytes 786436
  22.1 19.1 %copy-start.4 = (bf16[512,256]{1,0:T(8,128)(2,1)S(1)}, bf16[512,256]{1,0:T(8,128)(2,1)}, u32[]{:S(2)}) copy-start(bf16[512,256]{1,0:T(8,128)(2,1)} %k_ref.1) | copy-start | bytes 786436
  24.3 3.0 %collective-permute-start.8 = (f32[1,512]{1,0:T(1,128)S(1)}, f32[1,512]{1,0:T(1,128)S(1)}, u32[]{:S(2)}, u32[]{:S(2)}) collective-permute-start(f32[1,512]{1,0:T(1,128)S(1)} %get-tuple-element.20.lse_ref.refs_4_), channel_id=1, source_target_pairs={{0,28},{4,24},{8,4},{12,0},{16,12},{20,8},{24,20},{28,16},{1,29},{... | collective-permute-start | bytes 6152 | tf_op jit(solution)/shard_map/ppermute | solution.py:22
  25.5 2.4 %collective-permute-start.7 = (f32[1,512]{1,0:T(1,128)S(1)}, f32[1,512]{1,0:T(1,128)S(1)}, u32[]{:S(2)}, u32[]{:S(2)}) collective-permute-start(f32[1,512]{1,0:T(1,128)S(1)} %get-tuple-element.20.lse_ref.refs_4_), channel_id=1, source_target_pairs={{0,24},{4,28},{8,0},{12,4},{16,8},{20,12},{24,16},{28,20},{1,25},{... | collective-permute-start | bytes 6152 | tf_op jit(solution)/shard_map/ppermute | solution.py:22
  26.6 3.0 %collective-permute-start.6 = (f32[1,512]{1,0:T(1,128)S(1)}, f32[1,512]{1,0:T(1,128)S(1)}, u32[]{:S(2)}, u32[]{:S(2)}) collective-permute-start(f32[1,512]{1,0:T(1,128)S(1)} %get-tuple-element.20.lse_ref.refs_4_), channel_id=1, source_target_pairs={{0,20},{4,0},{8,28},{12,8},{16,4},{20,16},{24,12},{28,24},{1,21},{... | collective-permute-start | bytes 6152 | tf_op jit(solution)/shard_map/ppermute | solution.py:22
  29.6 1.0 %copy-start.3 = (bf16[512,256]{1,0:T(8,128)(2,1)S(1)}, bf16[512,256]{1,0:T(8,128)(2,1)}, u32[]{:S(2)}) copy-start(bf16[512,256]{1,0:T(8,128)(2,1)} %k_ref.1) | copy-start | bytes 786436
  30.5 0.7 %copy-start.7 = (s32[512]{0:T(512)S(1)}, s32[512]{0:T(512)}, u32[]{:S(2)}) copy-start(s32[512]{0:T(512)} %param.7) | copy-start | bytes 6148
  34.2 24.0 %all-to-all-start.1 = ((bf16[32,48,256]{2,1,0:T(8,128)(2,1)}), bf16[32,48,256]{2,1,0:T(8,128)(2,1)S(1)}, u32[]{:S(2)}, u32[]{:S(2)}) async-start(bf16[32,48,256]{2,1,0:T(8,128)(2,1)} %bitcast.7), calls=%async_computation.1 | async-start | bytes 1572864 | tf_op jit(solution)/shard_map/all_to_all | solution.py:310
where the time goes:
time: 66.6 us; the launch traced here: 66.2 us
  waiting for transfers between devices  21.7 us (33%)
  Pallas kernels  20.4 us (31%)
  starting transfers between devices  18.5 us (28%)
  local copies, waits for them, and re-layouts  4.91 us (7%)
  between operations  0.72 us (1%)
    all_to_all x1, waiting for transfers between devices, local(): lax.all_to_all(send_rows.reshape(devices, capacity, width), ('blk', 'tabl...  14.5 us
    pallas_call x6, Pallas kernels, call(): pl.pallas_call(body, out_shape=out_shape, in_specs=[vmem() for _ in args]...  12.3 us
    ppermute x9, starting transfers between devices, moved(): lax.ppermute(block, axis, [(i, target_of(i) % count) for i in range(count)])  9.25 us
    pallas_call x1, Pallas kernels, local(): pl.pallas_call(functools.partial(table_kernel, groups), out_shape=b16((RO...  8.12 us
    all_to_all x1, starting transfers between devices, local(): lax.all_to_all(ids.reshape(devices, 1, LANES), ('blk', 'table'), split_ax...  6.06 us
    all_to_all x1, waiting for transfers between devices, local(): lax.all_to_all(ids.reshape(devices, 1, LANES), ('blk', 'table'), split_ax...  4.95 us
    unnamed x18, local copies, waits for them, and re-layouts  4.91 us
    all_to_all x1, starting transfers between devices, local(): lax.all_to_all(send_rows.reshape(devices, capacity, width), ('blk', 'tabl...  3.15 us
  transfers between devices with their start and end apart: 11, of which 4 were waited for; matrix products, arithmetic and copies ran while one was open for 0% of the time, Pallas kernels for 14%

commit v1 on v0

--- a/solution.py
+++ b/solution.py
@@ -60,7 +60,23 @@
     return jnp.where(there == row.astype(jnp.int16), jnp.bfloat16(1), jnp.bfloat16(0))
 
 
-def route_kernel(devices, capacity, owner_ref, row_ref, slot_ref, ids_ref):
+def first_kernel(scale, devices, capacity, *refs):
+    sources, results, (owner_ref, row_ref, done) = refs[:5], refs[5:12], refs[12:]
+    slot_ref, ids_ref, top_ref, total_ref, pos_ref, q_ref, k_ref = results
+    targets = (owner_ref, row_ref, k_ref, q_ref, pos_ref)
+    copies = [pltpu.make_async_copy(a, b, done.at[i]) for i, (a, b) in enumerate(zip(sources, targets))]
+    for copy in copies:
+        copy.start()
+    copies[0].wait()
+    copies[1].wait()
+    route(devices, capacity, owner_ref, row_ref, slot_ref, ids_ref)
+    copies[2].wait()
+    copies[3].wait()
+    stats_kernel(scale, 1, 0, q_ref, k_ref, top_ref, total_ref)
+    copies[4].wait()
+
+
+def route(devices, capacity, owner_ref, row_ref, slot_ref, ids_ref):
     size = owner_ref.shape[1]
     owner = owner_ref[...]
     rank = jnp.zeros((1, size), jnp.float32)
@@ -253,23 +269,30 @@
     k_odd = moved(items, "blk", lambda i: i + window - 1 if i % 2 else i + 1)
     q_two = [moved(queries, "blk", lambda i, j=j: i - 2 * j) for j in twos]
     q_odd = moved(queries, "blk", lambda i: i - 1 if i % 2 else i - (window - 1))
-    slot, ids = call(
-        functools.partial(route_kernel, devices, capacity),
-        (i32((1, size)), i32((devices, LANES))),
-        (owner_row, row_row),
-        flops=4 * devices * LANES * size,
-    )
+    slot, ids, top, total, pos_row, queries, items = pl.pallas_call(
+        functools.partial(first_kernel, scale * LOG2E, devices, capacity),
+        out_shape=(
+            i32((1, size)),
+            i32((devices, LANES)),
+            f32((1, size)),
+            f32((1, size)),
+            i32((1, size)),
+            b16((size, width)),
+            b16((size, width)),
+        ),
+        in_specs=[pl.BlockSpec(memory_space=pltpu.HBM) for _ in range(5)],
+        out_specs=tuple(vmem() for _ in range(7)),
+        scratch_shapes=[
+            pltpu.VMEM((1, size), jnp.int32),
+            pltpu.VMEM((1, size), jnp.int32),
+            pltpu.SemaphoreType.DMA((5,)),
+        ],
+        compiler_params=params(12),
+        cost_estimate=pl.CostEstimate(flops=pair, bytes_accessed=4 * size * width, transcendentals=size * size),
+    )(*[pltpu.with_memory_space_constraint(x, pltpu.HBM) for x in (owner_row, row_row, items, queries, pos_row)])
     got_ids = lax.all_to_all(
         ids.reshape(devices, 1, LANES), ("blk", "table"), split_axis=0, concat_axis=0, tiled=True
     ).reshape(devices, LANES)
-    top, total = call(
-        functools.partial(stats_kernel, scale * LOG2E, 1, 0),
-        (f32((1, size)), f32((1, size))),
-        (queries, items),
-        flops=pair,
-        trans=size * size,
-    )
-    k_two, q_two, got_ids = lax.optimization_barrier((k_two, q_two, got_ids))
     k_swap = [moved(k, "blk", lambda i: i ^ 1) for k in k_two]
     q_swap = [moved(q, "blk", lambda i: i ^ 1) for q in q_two]
     k_all = [k_odd, *k_two, *k_swap]

time: 66.6 us -> 67.7 us (1.017)
  local copies, waits for them, and re-layouts: 4.91 us -> 0 us
  waiting for transfers between devices: 21.7 us -> 25.5 us
  starting transfers between devices: 18.5 us -> 20 us
  Pallas kernels: 20.4 us -> 21.2 us
    ppermute x9, waiting for transfers between devices: 2.26 us -> 7.2 us  [moved(): lax.ppermute(block, axis, [(i, target_of(i) % count) for i in range(count)])]
    unnamed x18 -> x0, local copies, waits for them, and re-layouts: 4.91 us -> none
    pallas_call x0 -> x1, Pallas kernels: none -> 2.25 us  [local(): pl.pallas_call(functools.partial(first_kernel, scale * LOG2E, devices, ca...]
    ppermute x9, starting transfers between devices: 9.25 us -> 11.1 us  [moved(): lax.ppermute(block, axis, [(i, target_of(i) % count) for i in range(count)])]
    pallas_call x6 -> x4, Pallas kernels: 12.3 us -> 10.9 us  [call(): pl.pallas_call(body, out_shape=out_shape, in_specs=[vmem() for _ in args]...]
    all_to_all x1, waiting for transfers between devices: 4.95 us -> 3.61 us  [local(): lax.all_to_all(ids.reshape(devices, 1, LANES), ('blk', 'table'), split_ax...]
  transfers between devices with their start and end apart: 11 -> 11, of which waited for: 4 -> 4; matrix products, arithmetic and copies ran while one was open for 0% -> 0% of each run, Pallas kernels for 14% -> 19%
where the time goes in v1:
time: 67.7 us; the launch traced here: 67.5 us
  waiting for transfers between devices  25.5 us (38%)
  Pallas kernels  21.2 us (31%)
  starting transfers between devices  20 us (30%)
  between operations  0.72 us (1%)
    all_to_all x1, waiting for transfers between devices, local(): lax.all_to_all(send_rows.reshape(devices, capacity, width), ('blk', 'tabl...  14.7 us
    ppermute x9, starting transfers between devices, moved(): lax.ppermute(block, axis, [(i, target_of(i) % count) for i in range(count)])  11.1 us
    pallas_call x4, Pallas kernels, call(): pl.pallas_call(body, out_shape=out_shape, in_specs=[vmem() for _ in args]...  10.9 us
    pallas_call x1, Pallas kernels, local(): pl.pallas_call(functools.partial(table_kernel, groups), out_shape=b16((RO...  8.11 us
    ppermute x9, waiting for transfers between devices, moved(): lax.ppermute(block, axis, [(i, target_of(i) % count) for i in range(count)])  7.2 us
    all_to_all x1, starting transfers between devices, local(): lax.all_to_all(ids.reshape(devices, 1, LANES), ('blk', 'table'), split_ax...  5.95 us
    all_to_all x1, waiting for transfers between devices, local(): lax.all_to_all(ids.reshape(devices, 1, LANES), ('blk', 'table'), split_ax...  3.61 us
    all_to_all x1, starting transfers between devices, local(): lax.all_to_all(send_rows.reshape(devices, capacity, width), ('blk', 'tabl...  2.97 us
  transfers between devices with their start and end apart: 11, of which 4 were waited for; matrix products, arithmetic and copies ran while one was open for 0% of the time, Pallas kernels for 19%

profile of v1, /device:TPU:1, one launch (start us, length us, event | category | flops | bytes accessed | tf_op | source)
XLA Modules:
  0.0 67.5 jit_solution(14615157041761101152)
XLA Ops:
  0.6 2.1 %collective-permute-start.1 = (bf16[512,256]{1,0:T(8,128)(2,1)}, bf16[512,256]{1,0:T(8,128)(2,1)S(1)}, u32[]{:S(2)}, u32[]{:S(2)}) collective-permute-start(bf16[512,256]{1,0:T(8,128)(2,1)} %refs_2_.1), channel_id=1, source_target_pairs={{0,8},{4,12},{8,16},{12,20},{16,24},{20,28},{24,0},{28,4},{1,9},{5... | collective-permute-start | bytes 786440 | tf_op jit(solution)/shard_map/ppermute | solution.py:22
  2.7 1.0 %collective-permute-start.4 = (bf16[512,256]{1,0:T(8,128)(2,1)}, bf16[512,256]{1,0:T(8,128)(2,1)S(1)}, u32[]{:S(2)}, u32[]{:S(2)}) collective-permute-start(bf16[512,256]{1,0:T(8,128)(2,1)} %refs_3_.1), channel_id=1, source_target_pairs={{0,24},{4,28},{8,0},{12,4},{16,8},{20,12},{24,16},{28,20},{1,25},{... | collective-permute-start | bytes 786440 | tf_op jit(solution)/shard_map/ppermute | solution.py:22
  3.7 2.5 %collective-permute-start = (bf16[512,256]{1,0:T(8,128)(2,1)}, bf16[512,256]{1,0:T(8,128)(2,1)S(1)}, u32[]{:S(2)}, u32[]{:S(2)}) collective-permute-start(bf16[512,256]{1,0:T(8,128)(2,1)} %refs_2_.1), channel_id=1, source_target_pairs={{0,4},{4,16},{8,12},{12,24},{16,20},{20,0},{24,28},{28,8},{1,5},{5... | collective-permute-start | bytes 786440 | tf_op jit(solution)/shard_map/ppermute | solution.py:22
  6.2 3.7 %collective-permute-done.1.refs_2_ = bf16[512,256]{1,0:T(8,128)(2,1)S(1)} collective-permute-done((bf16[512,256]{1,0:T(8,128)(2,1)}, bf16[512,256]{1,0:T(8,128)(2,1)S(1)}, u32[]{:S(2)}, u32[]{:S(2)}) %collective-permute-start.1) | collective-permute-done | bytes 262176 | tf_op jit(solution)/shard_map/ppermute | solution.py:22
  9.9 2.1 %collective-permute-start.2 = (bf16[512,256]{1,0:T(8,128)(2,1)S(1)}, bf16[512,256]{1,0:T(8,128)(2,1)S(1)}, u32[]{:S(2)}, u32[]{:S(2)}) collective-permute-start(bf16[512,256]{1,0:T(8,128)(2,1)S(1)} %collective-permute-done.1.refs_2_), channel_id=1, source_target_pairs={{0,4},{4,0},{8,12},{12,8},{16,20},{20,16},{24,28},{28,24},{1,5},{5... | collective-permute-start | bytes 786440 | tf_op jit(solution)/shard_map/ppermute | solution.py:22
  12.0 0.0 collective-permute-start.3
  12.0 3.5 %collective-permute-done.4.refs_2_ = bf16[512,256]{1,0:T(8,128)(2,1)S(1)} collective-permute-done((bf16[512,256]{1,0:T(8,128)(2,1)}, bf16[512,256]{1,0:T(8,128)(2,1)S(1)}, u32[]{:S(2)}, u32[]{:S(2)}) %collective-permute-start.4) | collective-permute-done | bytes 262176 | tf_op jit(solution)/shard_map/ppermute | solution.py:22
  15.5 1.5 %collective-permute-start.5 = (bf16[512,256]{1,0:T(8,128)(2,1)S(1)}, bf16[512,256]{1,0:T(8,128)(2,1)S(1)}, u32[]{:S(2)}, u32[]{:S(2)}) collective-permute-start(bf16[512,256]{1,0:T(8,128)(2,1)S(1)} %collective-permute-done.4.refs_2_), channel_id=1, source_target_pairs={{0,4},{4,0},{8,12},{12,8},{16,20},{20,16},{24,28},{28,24},{1,5},{5... | collective-permute-start | bytes 786440 | tf_op jit(solution)/shard_map/ppermute | solution.py:22
  17.1 2.3 %shard_map.76 = (s32[1,512]{1,0:T(1,128)S(1)}, s32[32,128]{1,0:T(8,128)}, f32[1,512]{1,0:T(1,128)S(1)}, f32[1,512]{1,0:T(1,128)S(1)}, s32[1,512]{1,0:T(1,128)S(1...) custom-call(s32[1,512]{1,0:T(1,128)} %bitcast.13, s32[1,512]{1,0:T(1,128)} %bitcast.14, ...), custom_call_target="tpu_custom_call" | custom-call | flops 134217728 | bytes 524288 | tf_op jit(solution)/shard_map/pallas_call | solution.py:272
  19.3 0.0 collective-permute-done.refs_1_
  19.3 0.0 collective-permute-done.2.refs_3_
  19.3 1.6 %shard_map.77 = (f32[1,512]{1,0:T(1,128)S(1)}, f32[1,512]{1,0:T(1,128)}) custom-call(bf16[512,256]{1,0:T(8,128)(2,1)S(1)} %get-tuple-element.16.refs_0_.q_ref, bf16[512,256]{1,0:T(8,128)(2,1)S(1)} %collective-permute-done.refs_1_, bf16[512,256]{1,0:T(8,128)(2,1)S(1)} %collective-permute-done.1.refs_2_, bf16[512,256]{1,0:T(8,128)(2,1)S(1)} %collective-permute-done.2.refs_3_, ...), custom_call_target="tpu_custom_call" | custom-call | flops 402653184 | bytes 1056768 | tf_op jit(solution)/shard_map/pallas_call | solution.py:38
  21.0 1.1 %collective-permute-start.8 = (f32[1,512]{1,0:T(1,128)S(1)}, f32[1,512]{1,0:T(1,128)S(1)}, u32[]{:S(2)}, u32[]{:S(2)}) collective-permute-start(f32[1,512]{1,0:T(1,128)S(1)} %get-tuple-element.19.lse_ref.refs_4_), channel_id=1, source_target_pairs={{0,28},{4,24},{8,4},{12,0},{16,12},{20,8},{24,20},{28,16},{1,29},{... | collective-permute-start | bytes 6152 | tf_op jit(solution)/shard_map/ppermute | solution.py:22
  22.0 0.1 collective-permute-start.7
  22.1 0.7 %collective-permute-start.6 = (f32[1,512]{1,0:T(1,128)S(1)}, f32[1,512]{1,0:T(1,128)S(1)}, u32[]{:S(2)}, u32[]{:S(2)}) collective-permute-start(f32[1,512]{1,0:T(1,128)S(1)} %get-tuple-element.19.lse_ref.refs_4_), channel_id=1, source_target_pairs={{0,20},{4,0},{8,28},{12,8},{16,4},{20,16},{24,12},{28,24},{1,21},{... | collective-permute-start | bytes 6152 | tf_op jit(solution)/shard_map/ppermute | solution.py:22
  22.9 5.9 %all-to-all-start = ((s32[32,1,128]{2,1,0:T(1,128)}), s32[32,1,128]{2,1,0:T(1,128)S(1)}, u32[]{:S(2)}, u32[]{:S(2)}) async-start(s32[32,1,128]{2,1,0:T(1,128)} %bitcast.4), calls=%async_computation | async-start | bytes 32768 | tf_op jit(solution)/shard_map/all_to_all | solution.py:293
  28.8 0.0 collective-permute-done.3.refs_1_
  28.8 0.0 collective-permute-done.5.refs_3_
  28.8 0.0 collective-permute-done.8.refs_7_
  28.8 0.0 collective-permute-done.7.refs_6_
  28.9 0.0 collective-permute-done.6.refs_5_
  28.9 3.0 %shard_map.79 = (bf16[512,256]{1,0:T(8,128)(2,1)}, bf16[1536,256]{1,0:T(8,128)(2,1)}) custom-call(bf16[512,256]{1,0:T(8,128)(2,1)S(1)} %get-tuple-element.21.refs_0_.k_ref, s32[1,512]{1,0:T(1,128)S(1)} %get-tuple-element.22.slot_ref, s32[1,512]{1,0:T(1,128)S(1)} %get-tuple-element.20.pos_ref, bf16[512,256]{1,0:T(8,128)(2,1)S(1)} %get-tuple-element.16.refs_0_.q_ref, ...), custom_call_target="tpu_custom_call" | custom-call | flops 1476395008 | bytes 2371584 | tf_op jit(solution)/shard_map/pallas_call | solution.py:38
  31.8 3.6 %all-to-all-done = s32[32,1,128]{2,1,0:T(1,128)S(1)} async-done(((s32[32,1,128]{2,1,0:T(1,128)}), s32[32,1,128]{2,1,0:T(1,128)S(1)}, u32[]{:S(2)}, u32[]{:S(2)}) %all-to-all-start) | async-done | bytes 16416 | tf_op jit(solution)/shard_map/all_to_all | solution.py:293
  35.5 3.0 %all-to-all-start.1 = ((bf16[32,48,256]{2,1,0:T(8,128)(2,1)}), bf16[32,48,256]{2,1,0:T(8,128)(2,1)S(1)}, u32[]{:S(2)}, u32[]{:S(2)}) async-start(bf16[32,48,256]{2,1,0:T(8,128)(2,1)} %bitcast.7), calls=%async_computation.1 | async-start | bytes 1572864 | tf_op jit(solution)/shard_map/all_to_all | solution.py:333
  38.4 3.9 %shard_map.80 = (s32[1,1536]{1,0:T(1,128)S(1)}, s32[12,128]{1,0:T(8,128)S(1)}, s32[1,128]{1,0:T(1,128)S(1)}) custom-call(s32[32,128]{1,0:T(8,128)S(1)} %bitcast.11), custom_call_target="tpu_custom_call" | custom-call | flops 75497472 | bytes 29184 | tf_op jit(solution)/shard_map/pallas_call | solution.py:38
  42.3 2.4 %shard_map.78 = bf16[512,256]{1,0:T(8,128)(2,1)} custom-call(bf16[512,256]{1,0:T(8,128)(2,1)S(1)} %get-tuple-element.16.refs_0_.q_ref, f32[1,512]{1,0:T(1,128)S(1)} %get-tuple-element.19.lse_ref.refs_4_, s32[1,512]{1,0:T(1,128)S(1)} %get-tuple-element.20.pos_ref, bf16[512,256]{1,0:T(8,128)(2,1)S(1)} %get-tuple-element.21.refs_0_.k_ref, ...), custom_call_target="tpu_custom_call" | custom-call | flops 1073741824 | bytes 1576960 | tf_op jit(solution)/shard_map/pallas_call | solution.py:38
  44.7 14.7 %all-to-all-done.1 = bf16[32,48,256]{2,1,0:T(8,128)(2,1)S(1)} async-done(((bf16[32,48,256]{2,1,0:T(8,128)(2,1)}), bf16[32,48,256]{2,1,0:T(8,128)(2,1)S(1)}, u32[]{:S(2)}, u32[]{:S(2)}) %all-to-all-start.1) | async-done | bytes 786464 | tf_op jit(solution)/shard_map/all_to_all | solution.py:333
  59.4 8.1 %shard_map.81 = bf16[16384,256]{1,0:T(8,128)(2,1)} custom-call(s32[128]{0:T(128)S(1)} %bitcast.12, bf16[1536,256]{1,0:T(8,128)(2,1)S(1)} %bitcast.10, s32[1,1536]{1,0:T(1,128)S(1)} %get-tuple-element.27.rank_ref, s32[12,128]{1,0:T(8,128)S(1)} %get-tuple-element.28.sorted_ref), custom_call_target="tpu_custom_call" | custom-call | flops 1207959552 | bytes 8388608 | tf_op jit(solution)/shard_map/pallas_call | solution.py:337
Async XLA Ops:
  0.6 9.3 %collective-permute-start.1 = (bf16[512,256]{1,0:T(8,128)(2,1)}, bf16[512,256]{1,0:T(8,128)(2,1)S(1)}, u32[]{:S(2)}, u32[]{:S(2)}) collective-permute-start(bf16[512,256]{1,0:T(8,128)(2,1)} %refs_2_.1), channel_id=1, source_target_pairs={{0,8},{4,12},{8,16},{12,20},{16,24},{20,28},{24,0},{28,4},{1,9},{5... | collective-permute-start | bytes 786440 | tf_op jit(solution)/shard_map/ppermute | solution.py:22
  2.7 12.8 %collective-permute-start.4 = (bf16[512,256]{1,0:T(8,128)(2,1)}, bf16[512,256]{1,0:T(8,128)(2,1)S(1)}, u32[]{:S(2)}, u32[]{:S(2)}) collective-permute-start(bf16[512,256]{1,0:T(8,128)(2,1)} %refs_3_.1), channel_id=1, source_target_pairs={{0,24},{4,28},{8,0},{12,4},{16,8},{20,12},{24,16},{28,20},{1,25},{... | collective-permute-start | bytes 786440 | tf_op jit(solution)/shard_map/ppermute | solution.py:22
  3.7 15.6 %collective-permute-start = (bf16[512,256]{1,0:T(8,128)(2,1)}, bf16[512,256]{1,0:T(8,128)(2,1)S(1)}, u32[]{:S(2)}, u32[]{:S(2)}) collective-permute-start(bf16[512,256]{1,0:T(8,128)(2,1)} %refs_2_.1), channel_id=1, source_target_pairs={{0,4},{4,16},{8,12},{12,24},{16,20},{20,0},{24,28},{28,8},{1,5},{5... | collective-permute-start | bytes 786440 | tf_op jit(solution)/shard_map/ppermute | solution.py:22
  9.9 9.4 %collective-permute-start.2 = (bf16[512,256]{1,0:T(8,128)(2,1)S(1)}, bf16[512,256]{1,0:T(8,128)(2,1)S(1)}, u32[]{:S(2)}, u32[]{:S(2)}) collective-permute-start(bf16[512,256]{1,0:T(8,128)(2,1)S(1)} %collective-permute-done.1.refs_2_), channel_id=1, source_target_pairs={{0,4},{4,0},{8,12},{12,8},{16,20},{20,16},{24,28},{28,24},{1,5},{5... | collective-permute-start | bytes 786440 | tf_op jit(solution)/shard_map/ppermute | solution.py:22
  12.0 16.8 %collective-permute-start.3 = (bf16[512,256]{1,0:T(8,128)(2,1)}, bf16[512,256]{1,0:T(8,128)(2,1)S(1)}, u32[]{:S(2)}, u32[]{:S(2)}) collective-permute-start(bf16[512,256]{1,0:T(8,128)(2,1)} %refs_3_.1), channel_id=1, source_target_pairs={{0,20},{4,0},{8,28},{12,8},{16,4},{20,16},{24,12},{28,24},{1,21},{... | collective-permute-start | bytes 786440 | tf_op jit(solution)/shard_map/ppermute | solution.py:22
  15.5 13.3 %collective-permute-start.5 = (bf16[512,256]{1,0:T(8,128)(2,1)S(1)}, bf16[512,256]{1,0:T(8,128)(2,1)S(1)}, u32[]{:S(2)}, u32[]{:S(2)}) collective-permute-start(bf16[512,256]{1,0:T(8,128)(2,1)S(1)} %collective-permute-done.4.refs_2_), channel_id=1, source_target_pairs={{0,4},{4,0},{8,12},{12,8},{16,20},{20,16},{24,28},{28,24},{1,5},{5... | collective-permute-start | bytes 786440 | tf_op jit(solution)/shard_map/ppermute | solution.py:22
  21.0 7.9 %collective-permute-start.8 = (f32[1,512]{1,0:T(1,128)S(1)}, f32[1,512]{1,0:T(1,128)S(1)}, u32[]{:S(2)}, u32[]{:S(2)}) collective-permute-start(f32[1,512]{1,0:T(1,128)S(1)} %get-tuple-element.19.lse_ref.refs_4_), channel_id=1, source_target_pairs={{0,28},{4,24},{8,4},{12,0},{16,12},{20,8},{24,20},{28,16},{1,29},{... | collective-permute-start | bytes 6152 | tf_op jit(solution)/shard_map/ppermute | solution.py:22
  22.0 6.8 %collective-permute-start.7 = (f32[1,512]{1,0:T(1,128)S(1)}, f32[1,512]{1,0:T(1,128)S(1)}, u32[]{:S(2)}, u32[]{:S(2)}) collective-permute-start(f32[1,512]{1,0:T(1,128)S(1)} %get-tuple-element.19.lse_ref.refs_4_), channel_id=1, source_target_pairs={{0,24},{4,28},{8,0},{12,4},{16,8},{20,12},{24,16},{28,20},{1,25},{... | collective-permute-start | bytes 6152 | tf_op jit(solution)/shard_map/ppermute | solution.py:22
  22.1 6.7 %collective-permute-start.6 = (f32[1,512]{1,0:T(1,128)S(1)}, f32[1,512]{1,0:T(1,128)S(1)}, u32[]{:S(2)}, u32[]{:S(2)}) collective-permute-start(f32[1,512]{1,0:T(1,128)S(1)} %get-tuple-element.19.lse_ref.refs_4_), channel_id=1, source_target_pairs={{0,20},{4,0},{8,28},{12,8},{16,4},{20,16},{24,12},{28,24},{1,21},{... | collective-permute-start | bytes 6152 | tf_op jit(solution)/shard_map/ppermute | solution.py:22
  22.9 12.6 %all-to-all-start = ((s32[32,1,128]{2,1,0:T(1,128)}), s32[32,1,128]{2,1,0:T(1,128)S(1)}, u32[]{:S(2)}, u32[]{:S(2)}) async-start(s32[32,1,128]{2,1,0:T(1,128)} %bitcast.4), calls=%async_computation | async-start | bytes 32768 | tf_op jit(solution)/shard_map/all_to_all | solution.py:293
  35.5 23.9 %all-to-all-start.1 = ((bf16[32,48,256]{2,1,0:T(8,128)(2,1)}), bf16[32,48,256]{2,1,0:T(8,128)(2,1)S(1)}, u32[]{:S(2)}, u32[]{:S(2)}) async-start(bf16[32,48,256]{2,1,0:T(8,128)(2,1)} %bitcast.7), calls=%async_computation.1 | async-start | bytes 1572864 | tf_op jit(solution)/shard_map/all_to_all | solution.py:333

commit v2 on v1

--- a/solution.py
+++ b/solution.py
@@ -72,7 +72,7 @@
     route(devices, capacity, owner_ref, row_ref, slot_ref, ids_ref)
     copies[2].wait()
     copies[3].wait()
-    stats_kernel(scale, 1, 0, q_ref, k_ref, top_ref, total_ref)
+    stats_kernel(scale, 1, 0, False, q_ref, k_ref, top_ref, total_ref)
     copies[4].wait()
 
 
@@ -145,15 +145,15 @@
         sorted_ref[c : c + 1, :] = (up * 128.0 + down)[0:1, :].astype(jnp.int32)
 
 
-def stats_kernel(scale, blocks, olds, *refs):
+def stats_kernel(scale, blocks, olds, final, *refs):
     q_ref = refs[0]
     k_refs = refs[1 : 1 + blocks]
     old = refs[1 + blocks : 1 + blocks + olds]
-    top_ref, total_ref = refs[-2:]
+    outs = refs[1 + blocks + olds :]
     size = q_ref.shape[0]
     for base in range(0, size, SUB):
-        q = q_ref[base : base + SUB, :]
         at = slice(base, base + SUB)
+        q = q_ref[at, :]
         top = old[0][:, at] if old else None
         total = old[1][:, at] if old else None
         for k in k_refs:
@@ -163,8 +163,11 @@
             part = jnp.sum(jnp.exp2(scores - high), axis=0, keepdims=True)
             total = part if top is None else total * jnp.exp2(top - high) + part
             top = high
-        top_ref[:, at] = top + jnp.log2(total) if old else top
-        total_ref[:, at] = total
+        if final:
+            outs[0][:, at] = top + jnp.log2(total)
+        else:
+            outs[0][:, at] = top
+            outs[1][:, at] = total
 
 
 def query_kernel(scale, blocks, q_ref, lse_ref, pos_ref, *refs):
@@ -184,22 +187,25 @@
         out_ref[at, :] = (scale * total).astype(jnp.bfloat16)
 
 
-def item_kernel(scale, blocks, k_ref, slot_ref, pos_ref, *refs):
-    q_refs, lse_refs = refs[:blocks], refs[blocks : 2 * blocks]
-    out_ref, send_ref = refs[-2:]
+def item_kernel(scale, own, last, k_ref, q_ref, lse_ref, *refs):
+    refs = list(refs)
     size = k_ref.shape[0]
     keys = k_ref[...]
-    total = None
-    for m in range(blocks):
-        for base in range(0, size, SUB):
-            at = slice(base, base + SUB)
-            q = q_refs[m][at, :]
-            scores = (scale * LOG2E) * lax.dot_general(keys, q, NT, preferred_element_type=jnp.float32)
-            weights = jnp.exp2(scores - lse_refs[m][:, at])
-            if m == 0:
-                weights = weights - jnp.where(iota((size, SUB), 0) == pos_ref[:, at], 1.0, 0.0)
-            part = jnp.dot(weights.astype(jnp.bfloat16), q, preferred_element_type=jnp.float32)
-            total = part if total is None else total + part
+    pos = refs.pop(0)[...] if own else None
+    total = None if own else refs.pop(0)[...]
+    for base in range(0, size, SUB):
+        at = slice(base, base + SUB)
+        q = q_ref[at, :]
+        scores = (scale * LOG2E) * lax.dot_general(keys, q, NT, preferred_element_type=jnp.float32)
+        weights = jnp.exp2(scores - lse_ref[:, at])
+        if own:
+            weights = weights - jnp.where(iota((size, SUB), 0) == pos[:, at], 1.0, 0.0)
+        part = jnp.dot(weights.astype(jnp.bfloat16), q, preferred_element_type=jnp.float32)
+        total = part if total is None else total + part
+    if not last:
+        refs[0][...] = total
+        return
+    slot_ref, out_ref, send_ref = refs
     grad = (scale * total).astype(jnp.bfloat16)
     out_ref[...] = grad
     for base in range(0, send_ref.shape[0], SUB):
@@ -208,16 +214,13 @@
         send_ref[base : base + SUB, :] = part.astype(jnp.bfloat16)
 
 
-def table_kernel(groups, count_ref, rows_ref, rank_ref, sorted_ref, out_ref, pick, arranged, total):
-    step = pl.program_id(0)
+def table_kernel(groups, count_ref, rows_ref, rank_ref, sorted_ref, out_ref, pick, arranged, table, total, done):
     chunks = arranged.shape[0] // LANES
     width = rows_ref.shape[1]
-
-    @pl.when(step == 0)
-    def _():
-        for at in range(0, chunks * LANES, SUB):
-            pick[at : at + SUB, :] = one_hot((SUB, chunks * LANES), rank_ref[...], at)
-        arranged[...] = jnp.dot(pick[...], rows_ref[...], preferred_element_type=jnp.float32).astype(jnp.bfloat16)
+    steps = table.shape[0] // (groups * SUB)
+    for at in range(0, chunks * LANES, SUB):
+        pick[at : at + SUB, :] = one_hot((SUB, chunks * LANES), rank_ref[...], at)
+    arranged[...] = jnp.dot(pick[...], rows_ref[...], preferred_element_type=jnp.float32).astype(jnp.bfloat16)
 
     def spread(chunk, base):
         at = pl.multiple_of(chunk * LANES, LANES)
@@ -225,26 +228,44 @@
         hot = one_hot((SUB, 2 * LANES), ids - base, 0)
         return jnp.dot(hot, arranged[pl.ds(at, 2 * LANES), :], preferred_element_type=jnp.float32)
 
-    firsts = [jnp.minimum(count_ref[step * groups + g] // LANES, chunks - 2) for g in range(groups)]
-    overs = [count_ref[step * groups + g + 1] > (firsts[g] + 2) * LANES for g in range(groups)]
-    for g in range(groups):
-        out_ref[g * SUB : (g + 1) * SUB, :] = spread(firsts[g], (step * groups + g) * SUB).astype(jnp.bfloat16)
-
-    @pl.when(functools.reduce(jnp.logical_or, overs))
-    def _():
-        def group(g, carry):
+    def copy_out(step):
+        at = pl.ds(pl.multiple_of(step * (groups * SUB), groups * SUB), groups * SUB)
+        return pltpu.make_async_copy(table.at[at, :], out_ref.at[at, :], done.at[step])
+
+    def one_step(step, carry):
+        firsts = [jnp.minimum(count_ref[step * groups + g] // LANES, chunks - 2) for g in range(groups)]
+        overs = [count_ref[step * groups + g + 1] > (firsts[g] + 2) * LANES for g in range(groups)]
+        for g in range(groups):
             base = (step * groups + g) * SUB
-            total[...] = jnp.zeros((SUB, width), jnp.float32)
-
-            def more(pair, inner):
-                total[...] += spread(2 * pair, base)
+            at = pl.ds(pl.multiple_of(base, SUB), SUB)
+            table[at, :] = spread(firsts[g], base).astype(jnp.bfloat16)
+
+        @pl.when(functools.reduce(jnp.logical_or, overs))
+        def _():
+            def group(g, inner):
+                base = (step * groups + g) * SUB
+                total[...] = jnp.zeros((SUB, width), jnp.float32)
+
+                def more(pair, deeper):
+                    total[...] += spread(2 * pair, base)
+                    return deeper
+
+                lax.fori_loop(0, chunks // 2, more, 0)
+                table[pl.ds(pl.multiple_of(base, SUB), SUB), :] = total[...].astype(jnp.bfloat16)
                 return inner
 
-            lax.fori_loop(0, chunks // 2, more, 0)
-            out_ref[pl.ds(pl.multiple_of(g * SUB, SUB), SUB), :] = total[...].astype(jnp.bfloat16)
-            return carry
-
-        lax.fori_loop(0, groups, group, 0)
+            lax.fori_loop(0, groups, group, 0)
+
+        copy_out(step).start()
+        return carry
+
+    lax.fori_loop(0, steps, one_step, 0)
+
+    def finish(step, carry):
+        copy_out(step).wait()
+        return carry
+
+    lax.fori_loop(0, steps, finish, 0)
 
 
 def local(queries, items, positives, item_owner, item_row):
@@ -296,14 +317,22 @@
     k_swap = [moved(k, "blk", lambda i: i ^ 1) for k in k_two]
     q_swap = [moved(q, "blk", lambda i: i ^ 1) for q in q_two]
     k_all = [k_odd, *k_two, *k_swap]
-    q_all = [q_odd, *q_two, *q_swap]
+    q_all = [*q_two, q_odd, *q_swap]
     table_groups = ROWS_DEV // SUB
-    lse, _ = call(
-        functools.partial(stats_kernel, scale * LOG2E, len(k_all), 2),
+    early = [k_odd, *k_two]
+    top, total = call(
+        functools.partial(stats_kernel, scale * LOG2E, len(early), 2, False),
         (f32((1, size)), f32((1, size))),
-        (queries, *k_all, top, total),
-        flops=pair * len(k_all),
-        trans=size * size * len(k_all),
+        (queries, *early, top, total),
+        flops=pair * len(early),
+        trans=size * size * len(early),
+    )
+    lse = call(
+        functools.partial(stats_kernel, scale * LOG2E, len(k_swap), 2, True),
+        f32((1, size)),
+        (queries, *k_swap, top, total),
+        flops=pair * len(k_swap),
+        trans=size * size * len(k_swap),
     )
     got_rank, got_sorted, got_count = call(
         functools.partial(order_kernel, capacity, SUB),
@@ -314,7 +343,7 @@
     lse_odd = moved(lse, "blk", lambda i: i - 1 if i % 2 else i - (window - 1))
     lse_two = [moved(lse, "blk", lambda i, j=j: i - 2 * j) for j in twos]
     lse_swap = [moved(lse, "blk", lambda i, j=j: (i ^ 1) - 2 * j) for j in twos]
-    lse_all = [lse_odd, *lse_two, *lse_swap]
+    lse_all = [*lse_two, lse_odd, *lse_swap]
 
     query_grad = call(
         functools.partial(query_kernel, scale, window),
@@ -323,12 +352,27 @@
         flops=2 * pair * window,
         trans=size * size * window,
     )
+    item_sum = call(
+        functools.partial(item_kernel, scale, True, False),
+        f32((size, width)),
+        (items, queries, lse, pos_row),
+        flops=2 * pair,
+        trans=size * size,
+    )
+    for q, one in zip(q_all[:-1], lse_all[:-1]):
+        item_sum = call(
+            functools.partial(item_kernel, scale, False, False),
+            f32((size, width)),
+            (items, q, one, item_sum),
+            flops=2 * pair,
+            trans=size * size,
+        )
     item_grad, send_rows = call(
-        functools.partial(item_kernel, scale, window),
+        functools.partial(item_kernel, scale, False, True),
         (b16((size, width)), b16((slots, width))),
-        (items, slot, pos_row, queries, *q_all, lse, *lse_all),
-        flops=2 * pair * window + 2 * slots * size * width,
-        trans=size * size * window,
+        (items, q_all[-1], lse_all[-1], item_sum, slot),
+        flops=2 * pair + 2 * slots * size * width,
+        trans=size * size,
     )
     got_rows = lax.all_to_all(
         send_rows.reshape(devices, capacity, width), ("blk", "table"), split_axis=0, concat_axis=0, tiled=True
@@ -337,14 +381,16 @@
     table_grad = pl.pallas_call(
         functools.partial(table_kernel, groups),
         out_shape=b16((ROWS_DEV, width)),
-        grid_spec=pltpu.PrefetchScalarGridSpec(
-            num_scalar_prefetch=1,
-            grid=(table_groups // groups,),
-            in_specs=[vmem(), vmem(), vmem()],
-            out_specs=pl.BlockSpec((groups * SUB, width), lambda i, count: (i, 0)),
-            scratch_shapes=[pltpu.VMEM((slots, slots), jnp.bfloat16), pltpu.VMEM((slots, width), jnp.bfloat16), pltpu.VMEM((SUB, width), jnp.float32)],
-        ),
-        compiler_params=params(24),
+        in_specs=[pl.BlockSpec(memory_space=pltpu.SMEM), vmem(), vmem(), vmem()],
+        out_specs=pl.BlockSpec(memory_space=pltpu.HBM),
+        scratch_shapes=[
+            pltpu.VMEM((slots, slots), jnp.bfloat16),
+            pltpu.VMEM((slots, width), jnp.bfloat16),
+            pltpu.VMEM((ROWS_DEV, width), jnp.bfloat16),
+            pltpu.VMEM((SUB, width), jnp.float32),
+            pltpu.SemaphoreType.DMA((table_groups // groups,)),
+        ],
+        compiler_params=params(32),
         cost_estimate=pl.CostEstimate(
             flops=2 * slots * slots * width, bytes_accessed=2 * ROWS_DEV * width, transcendentals=0
         ),

time: 67.7 us -> 67.2 us (level)
  starting transfers between devices: 20 us -> 22.7 us
  waiting for transfers between devices: 25.5 us -> 22.8 us
    all_to_all x1, waiting for transfers between devices: 3.61 us -> 0.01 us  [local(): lax.all_to_all(ids.reshape(devices, 1, LANES), ('blk', 'table'), split_ax...]
    all_to_all x1, starting transfers between devices: 2.97 us -> 5.48 us  [local(): lax.all_to_all(send_rows.reshape(devices, capacity, width), ('blk', 'tabl...]
    pallas_call x1, Pallas kernels: 8.11 us -> 6.67 us  [local(): pl.pallas_call(functools.partial(table_kernel, groups), out_shape=b16((RO...]
    ppermute x9, starting transfers between devices: 11.1 us -> 12.4 us  [moved(): lax.ppermute(block, axis, [(i, target_of(i) % count) for i in range(count)])]
    all_to_all x1, starting transfers between devices: 5.95 us -> 4.81 us  [local(): lax.all_to_all(ids.reshape(devices, 1, LANES), ('blk', 'table'), split_ax...]
    ppermute x9, waiting for transfers between devices: 7.2 us -> 8.22 us  [moved(): lax.ppermute(block, axis, [(i, target_of(i) % count) for i in range(count)])]
    pallas_call x4 -> x8, Pallas kernels: 10.9 us -> 11.9 us  [call(): pl.pallas_call(body, out_shape=out_shape, in_specs=[vmem() for _ in args]...]
  transfers between devices with their start and end apart: 11 -> 11, of which waited for: 4 -> 4; matrix products, arithmetic and copies ran while one was open for 0% -> 0% of each run, Pallas kernels for 19% -> 21%
where the time goes in v2:
time: 67.2 us; the launch traced here: 67 us
  waiting for transfers between devices  22.8 us (34%)
  starting transfers between devices  22.7 us (34%)
  Pallas kernels  20.8 us (31%)
  between operations  0.74 us (1%)
    all_to_all x1, waiting for transfers between devices, local(): lax.all_to_all(send_rows.reshape(devices, capacity, width), ('blk', 'tabl...  14.5 us
    ppermute x9, starting transfers between devices, moved(): lax.ppermute(block, axis, [(i, target_of(i) % count) for i in range(count)])  12.4 us
    pallas_call x8, Pallas kernels, call(): pl.pallas_call(body, out_shape=out_shape, in_specs=[vmem() for _ in args]...  11.9 us
    ppermute x9, waiting for transfers between devices, moved(): lax.ppermute(block, axis, [(i, target_of(i) % count) for i in range(count)])  8.22 us
    pallas_call x1, Pallas kernels, local(): pl.pallas_call(functools.partial(table_kernel, groups), out_shape=b16((RO...  6.67 us
    all_to_all x1, starting transfers between devices, local(): lax.all_to_all(send_rows.reshape(devices, capacity, width), ('blk', 'tabl...  5.48 us
    all_to_all x1, starting transfers between devices, local(): lax.all_to_all(ids.reshape(devices, 1, LANES), ('blk', 'table'), split_ax...  4.81 us
    pallas_call x1, Pallas kernels, local(): pl.pallas_call(functools.partial(first_kernel, scale * LOG2E, devices, ca...  2.25 us
  transfers between devices with their start and end apart: 11, of which 4 were waited for; matrix products, arithmetic and copies ran while one was open for 0% of the time, Pallas kernels for 21%

profile of v2, /device:TPU:1, one launch (start us, length us, event | category | flops | bytes accessed | tf_op | source)
XLA Modules:
  0.0 67.0 jit_solution(7178389519436768216)
XLA Ops:
  0.6 2.1 %collective-permute-start = (bf16[512,256]{1,0:T(8,128)(2,1)}, bf16[512,256]{1,0:T(8,128)(2,1)S(1)}, u32[]{:S(2)}, u32[]{:S(2)}) collective-permute-start(bf16[512,256]{1,0:T(8,128)(2,1)} %refs_2_.1), channel_id=1, source_target_pairs={{0,8},{4,12},{8,16},{12,20},{16,24},{20,28},{24,0},{28,4},{1,9},{5... | collective-permute-start | bytes 786440 | tf_op jit(solution)/shard_map/ppermute | solution.py:22
  2.7 1.0 %collective-permute-start.3 = (bf16[512,256]{1,0:T(8,128)(2,1)}, bf16[512,256]{1,0:T(8,128)(2,1)S(1)}, u32[]{:S(2)}, u32[]{:S(2)}) collective-permute-start(bf16[512,256]{1,0:T(8,128)(2,1)} %refs_3_.1), channel_id=1, source_target_pairs={{0,24},{4,28},{8,0},{12,4},{16,8},{20,12},{24,16},{28,20},{1,25},{... | collective-permute-start | bytes 786440 | tf_op jit(solution)/shard_map/ppermute | solution.py:22
  3.7 2.5 %collective-permute-start.2 = (bf16[512,256]{1,0:T(8,128)(2,1)}, bf16[512,256]{1,0:T(8,128)(2,1)S(1)}, u32[]{:S(2)}, u32[]{:S(2)}) collective-permute-start(bf16[512,256]{1,0:T(8,128)(2,1)} %refs_2_.1), channel_id=1, source_target_pairs={{0,4},{4,16},{8,12},{12,24},{16,20},{20,0},{24,28},{28,8},{1,5},{5... | collective-permute-start | bytes 786440 | tf_op jit(solution)/shard_map/ppermute | solution.py:22
  6.2 3.7 %collective-permute-done.refs_2_ = bf16[512,256]{1,0:T(8,128)(2,1)S(1)} collective-permute-done((bf16[512,256]{1,0:T(8,128)(2,1)}, bf16[512,256]{1,0:T(8,128)(2,1)S(1)}, u32[]{:S(2)}, u32[]{:S(2)}) %collective-permute-start) | collective-permute-done | bytes 262176 | tf_op jit(solution)/shard_map/ppermute | solution.py:22
  9.9 2.1 %collective-permute-start.1 = (bf16[512,256]{1,0:T(8,128)(2,1)S(1)}, bf16[512,256]{1,0:T(8,128)(2,1)S(1)}, u32[]{:S(2)}, u32[]{:S(2)}) collective-permute-start(bf16[512,256]{1,0:T(8,128)(2,1)S(1)} %collective-permute-done.refs_2_), channel_id=1, source_target_pairs={{0,4},{4,0},{8,12},{12,8},{16,20},{20,16},{24,28},{28,24},{1,5},{5... | collective-permute-start | bytes 786440 | tf_op jit(solution)/shard_map/ppermute | solution.py:22
  12.0 0.0 collective-permute-start.6
  12.0 3.5 %collective-permute-done.3.q_ref = bf16[512,256]{1,0:T(8,128)(2,1)S(1)} collective-permute-done((bf16[512,256]{1,0:T(8,128)(2,1)}, bf16[512,256]{1,0:T(8,128)(2,1)S(1)}, u32[]{:S(2)}, u32[]{:S(2)}) %collective-permute-start.3) | collective-permute-done | bytes 262176 | tf_op jit(solution)/shard_map/ppermute | solution.py:22
  15.5 1.5 %collective-permute-start.4 = (bf16[512,256]{1,0:T(8,128)(2,1)S(1)}, bf16[512,256]{1,0:T(8,128)(2,1)S(1)}, u32[]{:S(2)}, u32[]{:S(2)}) collective-permute-start(bf16[512,256]{1,0:T(8,128)(2,1)S(1)} %collective-permute-done.3.q_ref), channel_id=1, source_target_pairs={{0,4},{4,0},{8,12},{12,8},{16,20},{20,16},{24,28},{28,24},{1,5},{5... | collective-permute-start | bytes 786440 | tf_op jit(solution)/shard_map/ppermute | solution.py:22
  17.1 2.3 %shard_map.76 = (s32[1,512]{1,0:T(1,128)S(1)}, s32[32,128]{1,0:T(8,128)}, f32[1,512]{1,0:T(1,128)S(1)}, f32[1,512]{1,0:T(1,128)S(1)}, s32[1,512]{1,0:T(1,128)S(1...) custom-call(s32[1,512]{1,0:T(1,128)} %bitcast.13, s32[1,512]{1,0:T(1,128)} %bitcast.14, ...), custom_call_target="tpu_custom_call" | custom-call | flops 134217728 | bytes 524288 | tf_op jit(solution)/shard_map/pallas_call | solution.py:293
  19.3 4.8 %all-to-all-start = ((s32[32,1,128]{2,1,0:T(1,128)}), s32[32,1,128]{2,1,0:T(1,128)S(1)}, u32[]{:S(2)}, u32[]{:S(2)}) async-start(s32[32,1,128]{2,1,0:T(1,128)} %bitcast.4), calls=%async_computation | async-start | bytes 32768 | tf_op jit(solution)/shard_map/all_to_all | solution.py:314
  24.1 0.0 collective-permute-done.2.refs_1_
  24.1 0.8 %shard_map.77 = (f32[1,512]{1,0:T(1,128)S(1)}, f32[1,512]{1,0:T(1,128)S(1)}) custom-call(bf16[512,256]{1,0:T(8,128)(2,1)S(1)} %get-tuple-element.17.refs_0_.q_ref, bf16[512,256]{1,0:T(8,128)(2,1)S(1)} %collective-permute-done.2.refs_1_, bf16[512,256]{1,0:T(8,128)(2,1)S(1)} %collective-permute-done.refs_2_, f32[1,512]{1,0:T(1,128)S(1)} %get-tuple-element.18.refs_3_, ...), custom_call_target="tpu_custom_call" | custom-call | flops 268435456 | bytes 794624 | tf_op jit(solution)/shard_map/pallas_call | solution.py:38
  24.9 0.0 collective-permute-done.1.refs_1_.refs_3_
  24.9 0.5 shard_map.78.lse_ref
  25.5 2.3 %collective-permute-start.8 = (f32[1,512]{1,0:T(1,128)S(1)}, f32[1,512]{1,0:T(1,128)S(1)}, u32[]{:S(2)}, u32[]{:S(2)}) collective-permute-start(f32[1,512]{1,0:T(1,128)S(1)} %shard_map.78.lse_ref), channel_id=1, source_target_pairs={{0,24},{4,28},{8,0},{12,4},{16,8},{20,12},{24,16},{28,20},{1,25},{... | collective-permute-start | bytes 6152 | tf_op jit(solution)/shard_map/ppermute | solution.py:22
  27.8 0.7 %collective-permute-start.7 = (f32[1,512]{1,0:T(1,128)S(1)}, f32[1,512]{1,0:T(1,128)S(1)}, u32[]{:S(2)}, u32[]{:S(2)}) collective-permute-start(f32[1,512]{1,0:T(1,128)S(1)} %shard_map.78.lse_ref), channel_id=1, source_target_pairs={{0,20},{4,0},{8,28},{12,8},{16,4},{20,16},{24,12},{28,24},{1,21},{... | collective-permute-start | bytes 6152 | tf_op jit(solution)/shard_map/ppermute | solution.py:22
  28.4 0.2 collective-permute-start.5
  28.6 0.7 %shard_map.80.refs_0_ = f32[512,256]{1,0:T(8,128)S(1)} custom-call(bf16[512,256]{1,0:T(8,128)(2,1)S(1)} %get-tuple-element.23.refs_0_.k_ref, bf16[512,256]{1,0:T(8,128)(2,1)S(1)} %get-tuple-element.17.refs_0_.q_ref, f32[1,512]{1,0:T(1,128)S(1)} %shard_map.78.lse_ref, s32[1,512]{1,0:T(1,128)S(1)} %get-tuple-element.22.pos_ref.refs_0_), custom_call_target="tpu_custom_call" | custom-call | flops 268435456 | bytes 1052672 | tf_op jit(solution)/shard_map/pallas_call | solution.py:38
  29.3 0.0 collective-permute-done.8.lse_ref
  29.3 0.7 %shard_map.81.refs_0_ = f32[512,256]{1,0:T(8,128)S(1)} custom-call(bf16[512,256]{1,0:T(8,128)(2,1)S(1)} %get-tuple-element.23.refs_0_.k_ref, bf16[512,256]{1,0:T(8,128)(2,1)S(1)} %collective-permute-done.3.q_ref, f32[1,512]{1,0:T(1,128)S(1)} %collective-permute-done.8.lse_ref, f32[512,256]{1,0:T(8,128)S(1)} %shard_map.80.refs_0_), custom_call_target="tpu_custom_call" | custom-call | flops 268435456 | bytes 1574912 | tf_op jit(solution)/shard_map/pallas_call | solution.py:38
  30.1 0.0 collective-permute-done.6.q_ref
  30.1 1.0 %collective-permute-done.7.lse_ref = f32[1,512]{1,0:T(1,128)S(1)} collective-permute-done((f32[1,512]{1,0:T(1,128)S(1)}, f32[1,512]{1,0:T(1,128)S(1)}, u32[]{:S(2)}, u32[]{:S(2)}) %collective-permute-start.7) | collective-permute-done | bytes 2080 | tf_op jit(solution)/shard_map/ppermute | solution.py:22
  31.1 0.7 %shard_map.82.refs_0_ = f32[512,256]{1,0:T(8,128)S(1)} custom-call(bf16[512,256]{1,0:T(8,128)(2,1)S(1)} %get-tuple-element.23.refs_0_.k_ref, bf16[512,256]{1,0:T(8,128)(2,1)S(1)} %collective-permute-done.6.q_ref, f32[1,512]{1,0:T(1,128)S(1)} %collective-permute-done.7.lse_ref, f32[512,256]{1,0:T(8,128)S(1)} %shard_map.81.refs_0_), custom_call_target="tpu_custom_call" | custom-call | flops 268435456 | bytes 1574912 | tf_op jit(solution)/shard_map/pallas_call | solution.py:38
  31.8 0.0 collective-permute-done.4.q_ref
  31.8 0.0 collective-permute-done.5.lse_ref
  31.8 2.2 %shard_map.83 = (bf16[512,256]{1,0:T(8,128)(2,1)}, bf16[1536,256]{1,0:T(8,128)(2,1)}) custom-call(bf16[512,256]{1,0:T(8,128)(2,1)S(1)} %get-tuple-element.23.refs_0_.k_ref, bf16[512,256]{1,0:T(8,128)(2,1)S(1)} %collective-permute-done.4.q_ref, f32[1,512]{1,0:T(1,128)S(1)} %collective-permute-done.5.lse_ref, f32[512,256]{1,0:T(8,128)S(1)} %shard_map.82.refs_0_, ...), custom_call_target="tpu_custom_call" | custom-call | flops 671088640 | bytes 2101248 | tf_op jit(solution)/shard_map/pallas_call | solution.py:38
  34.0 0.0 all-to-all-done
  34.0 5.5 %all-to-all-start.1 = ((bf16[32,48,256]{2,1,0:T(8,128)(2,1)}), bf16[32,48,256]{2,1,0:T(8,128)(2,1)S(1)}, u32[]{:S(2)}, u32[]{:S(2)}) async-start(bf16[32,48,256]{2,1,0:T(8,128)(2,1)} %bitcast.7), calls=%async_computation.1 | async-start | bytes 1572864 | tf_op jit(solution)/shard_map/all_to_all | solution.py:377
  39.5 3.9 %shard_map.84 = (s32[1,1536]{1,0:T(1,128)S(1)}, s32[12,128]{1,0:T(8,128)S(1)}, s32[1,128]{1,0:T(1,128)S(1)}) custom-call(s32[32,128]{1,0:T(8,128)S(1)} %bitcast.11), custom_call_target="tpu_custom_call" | custom-call | flops 75497472 | bytes 29184 | tf_op jit(solution)/shard_map/pallas_call | solution.py:38
  43.4 2.4 %shard_map.79 = bf16[512,256]{1,0:T(8,128)(2,1)} custom-call(bf16[512,256]{1,0:T(8,128)(2,1)S(1)} %get-tuple-element.17.refs_0_.q_ref, f32[1,512]{1,0:T(1,128)S(1)} %shard_map.78.lse_ref, s32[1,512]{1,0:T(1,128)S(1)} %get-tuple-element.22.pos_ref.refs_0_, bf16[512,256]{1,0:T(8,128)(2,1)S(1)} %get-tuple-element.23.refs_0_.k_ref, ...), custom_call_target="tpu_custom_call" | custom-call | flops 1073741824 | bytes 1576960 | tf_op jit(solution)/shard_map/pallas_call | solution.py:38
  45.8 14.5 %all-to-all-done.1 = bf16[32,48,256]{2,1,0:T(8,128)(2,1)S(1)} async-done(((bf16[32,48,256]{2,1,0:T(8,128)(2,1)}), bf16[32,48,256]{2,1,0:T(8,128)(2,1)S(1)}, u32[]{:S(2)}, u32[]{:S(2)}) %all-to-all-start.1) | async-done | bytes 786464 | tf_op jit(solution)/shard_map/all_to_all | solution.py:377
  60.3 6.7 %shard_map.85 = bf16[16384,256]{1,0:T(8,128)(2,1)} custom-call(s32[128]{0:T(128)S(1)} %bitcast.12, bf16[1536,256]{1,0:T(8,128)(2,1)S(1)} %bitcast.10, s32[1,1536]{1,0:T(1,128)S(1)} %get-tuple-element.29.rank_ref, s32[12,128]{1,0:T(8,128)S(1)} %get-tuple-element.30.sorted_ref), custom_call_target="tpu_custom_call" | custom-call | flops 1207959552 | bytes 8388608 | tf_op jit(solution)/shard_map/pallas_call | solution.py:381
Async XLA Ops:
  0.6 9.3 %collective-permute-start = (bf16[512,256]{1,0:T(8,128)(2,1)}, bf16[512,256]{1,0:T(8,128)(2,1)S(1)}, u32[]{:S(2)}, u32[]{:S(2)}) collective-permute-start(bf16[512,256]{1,0:T(8,128)(2,1)} %refs_2_.1), channel_id=1, source_target_pairs={{0,8},{4,12},{8,16},{12,20},{16,24},{20,28},{24,0},{28,4},{1,9},{5... | collective-permute-start | bytes 786440 | tf_op jit(solution)/shard_map/ppermute | solution.py:22
  2.7 12.8 %collective-permute-start.3 = (bf16[512,256]{1,0:T(8,128)(2,1)}, bf16[512,256]{1,0:T(8,128)(2,1)S(1)}, u32[]{:S(2)}, u32[]{:S(2)}) collective-permute-start(bf16[512,256]{1,0:T(8,128)(2,1)} %refs_3_.1), channel_id=1, source_target_pairs={{0,24},{4,28},{8,0},{12,4},{16,8},{20,12},{24,16},{28,20},{1,25},{... | collective-permute-start | bytes 786440 | tf_op jit(solution)/shard_map/ppermute | solution.py:22
  3.7 20.4 %collective-permute-start.2 = (bf16[512,256]{1,0:T(8,128)(2,1)}, bf16[512,256]{1,0:T(8,128)(2,1)S(1)}, u32[]{:S(2)}, u32[]{:S(2)}) collective-permute-start(bf16[512,256]{1,0:T(8,128)(2,1)} %refs_2_.1), channel_id=1, source_target_pairs={{0,4},{4,16},{8,12},{12,24},{16,20},{20,0},{24,28},{28,8},{1,5},{5... | collective-permute-start | bytes 786440 | tf_op jit(solution)/shard_map/ppermute | solution.py:22
  9.9 15.0 %collective-permute-start.1 = (bf16[512,256]{1,0:T(8,128)(2,1)S(1)}, bf16[512,256]{1,0:T(8,128)(2,1)S(1)}, u32[]{:S(2)}, u32[]{:S(2)}) collective-permute-start(bf16[512,256]{1,0:T(8,128)(2,1)S(1)} %collective-permute-done.refs_2_), channel_id=1, source_target_pairs={{0,4},{4,0},{8,12},{12,8},{16,20},{20,16},{24,28},{28,24},{1,5},{5... | collective-permute-start | bytes 786440 | tf_op jit(solution)/shard_map/ppermute | solution.py:22
  12.0 18.0 %collective-permute-start.6 = (bf16[512,256]{1,0:T(8,128)(2,1)}, bf16[512,256]{1,0:T(8,128)(2,1)S(1)}, u32[]{:S(2)}, u32[]{:S(2)}) collective-permute-start(bf16[512,256]{1,0:T(8,128)(2,1)} %refs_3_.1), channel_id=1, source_target_pairs={{0,20},{4,0},{8,28},{12,8},{16,4},{20,16},{24,12},{28,24},{1,21},{... | collective-permute-start | bytes 786440 | tf_op jit(solution)/shard_map/ppermute | solution.py:22
  15.5 16.3 %collective-permute-start.4 = (bf16[512,256]{1,0:T(8,128)(2,1)S(1)}, bf16[512,256]{1,0:T(8,128)(2,1)S(1)}, u32[]{:S(2)}, u32[]{:S(2)}) collective-permute-start(bf16[512,256]{1,0:T(8,128)(2,1)S(1)} %collective-permute-done.3.q_ref), channel_id=1, source_target_pairs={{0,4},{4,0},{8,12},{12,8},{16,20},{20,16},{24,28},{28,24},{1,5},{5... | collective-permute-start | bytes 786440 | tf_op jit(solution)/shard_map/ppermute | solution.py:22
  19.3 14.7 %all-to-all-start = ((s32[32,1,128]{2,1,0:T(1,128)}), s32[32,1,128]{2,1,0:T(1,128)S(1)}, u32[]{:S(2)}, u32[]{:S(2)}) async-start(s32[32,1,128]{2,1,0:T(1,128)} %bitcast.4), calls=%async_computation | async-start | bytes 32768 | tf_op jit(solution)/shard_map/all_to_all | solution.py:314
  25.5 3.9 %collective-permute-start.8 = (f32[1,512]{1,0:T(1,128)S(1)}, f32[1,512]{1,0:T(1,128)S(1)}, u32[]{:S(2)}, u32[]{:S(2)}) collective-permute-start(f32[1,512]{1,0:T(1,128)S(1)} %shard_map.78.lse_ref), channel_id=1, source_target_pairs={{0,24},{4,28},{8,0},{12,4},{16,8},{20,12},{24,16},{28,20},{1,25},{... | collective-permute-start | bytes 6152 | tf_op jit(solution)/shard_map/ppermute | solution.py:22
  27.8 3.3 %collective-permute-start.7 = (f32[1,512]{1,0:T(1,128)S(1)}, f32[1,512]{1,0:T(1,128)S(1)}, u32[]{:S(2)}, u32[]{:S(2)}) collective-permute-start(f32[1,512]{1,0:T(1,128)S(1)} %shard_map.78.lse_ref), channel_id=1, source_target_pairs={{0,20},{4,0},{8,28},{12,8},{16,4},{20,16},{24,12},{28,24},{1,21},{... | collective-permute-start | bytes 6152 | tf_op jit(solution)/shard_map/ppermute | solution.py:22
  28.4 3.4 %collective-permute-start.5 = (f32[1,512]{1,0:T(1,128)S(1)}, f32[1,512]{1,0:T(1,128)S(1)}, u32[]{:S(2)}, u32[]{:S(2)}) collective-permute-start(f32[1,512]{1,0:T(1,128)S(1)} %shard_map.78.lse_ref), channel_id=1, source_target_pairs={{0,28},{4,24},{8,4},{12,0},{16,12},{20,8},{24,20},{28,16},{1,29},{... | collective-permute-start | bytes 6152 | tf_op jit(solution)/shard_map/ppermute | solution.py:22
  34.0 26.3 %all-to-all-start.1 = ((bf16[32,48,256]{2,1,0:T(8,128)(2,1)}), bf16[32,48,256]{2,1,0:T(8,128)(2,1)S(1)}, u32[]{:S(2)}, u32[]{:S(2)}) async-start(bf16[32,48,256]{2,1,0:T(8,128)(2,1)} %bitcast.7), calls=%async_computation.1 | async-start | bytes 1572864 | tf_op jit(solution)/shard_map/all_to_all | solution.py:377

commit v3 on v2

--- a/solution.py
+++ b/solution.py
@@ -12,6 +12,7 @@
 ROWS_DEV = 16384
 LANES = 128
 SUB = 256
+PACK = 16
 LOG2E = math.log2(math.e)
 NT = (((1,), (1,)), ((), ()))
 TN = (((0,), (0,)), ((), ()))
@@ -101,7 +102,7 @@
     ids_ref[...] = value.astype(jnp.int32)
 
 
-def order_kernel(capacity, group, ids_ref, rank_ref, sorted_ref, count_ref):
+def order_kernel(capacity, group, groups, ids_ref, rank_ref, sorted_ref, count_ref):
     devices = ids_ref.shape[0]
     slots = devices * capacity
     chunks = slots // LANES
@@ -132,17 +133,32 @@
             else:
                 hit = (col < rows[i]) | ((col == rows[i]) & earlier)
             ranks[i] = ranks[i] + jnp.sum(jnp.where(hit, 1.0, 0.0), axis=0, keepdims=True)
-    count_ref[...] = count.astype(jnp.int32)
+    count = count.astype(jnp.int32)
+    covered = start_of(count, slots) + LANES
+    over = (pltpu.roll(count, LANES - 1, 1) > covered) & (lane < groups)
+    over = jnp.max(jnp.where(over, 1.0, 0.0), axis=1, keepdims=True).astype(jnp.int32)
+    count_ref[...] = jnp.where(lane == LANES - 1, over, count)
     rank = jnp.concatenate(ranks, axis=1).astype(jnp.int32)
     rank_ref[...] = rank
     row = jnp.concatenate(rows, axis=1)
     high = jnp.broadcast_to(lax.shift_right_logical(row, 7).astype(jnp.float32), (8, slots)).astype(jnp.bfloat16)
     low = jnp.broadcast_to((row & 127).astype(jnp.float32), (8, slots)).astype(jnp.bfloat16)
+    lines = []
     for c in range(chunks):
         pick = one_hot((LANES, slots), rank, c * LANES)
         up = lax.dot_general(high, pick, NT, preferred_element_type=jnp.float32)
         down = lax.dot_general(low, pick, NT, preferred_element_type=jnp.float32)
-        sorted_ref[c : c + 1, :] = (up * 128.0 + down)[0:1, :].astype(jnp.int32)
+        lines.append((up * 128.0 + down)[0:1, :].astype(jnp.int32))
+    for o in range(LANES // PACK):
+        turned = [pltpu.roll(line, LANES - o * PACK, 1) if o else line for line in lines]
+        for c in range(chunks):
+            after_it = turned[min(c + 1, chunks - 1)]
+            sorted_ref[o, c : c + 1, :] = jnp.where(lane < LANES - o * PACK, turned[c], after_it)
+
+
+def start_of(count, slots):
+    packs = lax.shift_right_logical(count, PACK.bit_length() - 1)
+    return jnp.minimum(packs * PACK, slots - LANES)
 
 
 def stats_kernel(scale, blocks, olds, final, *refs):
@@ -208,64 +224,63 @@
     slot_ref, out_ref, send_ref = refs
     grad = (scale * total).astype(jnp.bfloat16)
     out_ref[...] = grad
-    for base in range(0, send_ref.shape[0], SUB):
-        pick = one_hot((SUB, size), slot_ref[...], base)
-        part = jnp.dot(pick, grad, preferred_element_type=jnp.float32)
-        send_ref[base : base + SUB, :] = part.astype(jnp.bfloat16)
-
-
-def table_kernel(groups, count_ref, rows_ref, rank_ref, sorted_ref, out_ref, pick, arranged, table, total, done):
-    chunks = arranged.shape[0] // LANES
-    width = rows_ref.shape[1]
-    steps = table.shape[0] // (groups * SUB)
-    for at in range(0, chunks * LANES, SUB):
-        pick[at : at + SUB, :] = one_hot((SUB, chunks * LANES), rank_ref[...], at)
+    pick = one_hot((send_ref.shape[0], size), slot_ref[...], 0)
+    send_ref[...] = jnp.dot(pick, grad, preferred_element_type=jnp.float32).astype(jnp.bfloat16)
+
+
+def table_kernel(group, per_copy, count_ref, rows_ref, rank_ref, sorted_ref, out_ref, pick, arranged, table, total, done):
+    slots, width = arranged.shape
+    groups = table.shape[0] // group
+    copies = groups // per_copy
+    for at in range(0, slots, SUB):
+        pick[at : at + SUB, :] = one_hot((SUB, slots), rank_ref[...], at)
     arranged[...] = jnp.dot(pick[...], rows_ref[...], preferred_element_type=jnp.float32).astype(jnp.bfloat16)
 
-    def spread(chunk, base):
-        at = pl.multiple_of(chunk * LANES, LANES)
-        ids = jnp.concatenate([sorted_ref[pl.ds(chunk, 1), :], sorted_ref[pl.ds(chunk + 1, 1), :]], axis=1)
-        hot = one_hot((SUB, 2 * LANES), ids - base, 0)
-        return jnp.dot(hot, arranged[pl.ds(at, 2 * LANES), :], preferred_element_type=jnp.float32)
-
-    def copy_out(step):
-        at = pl.ds(pl.multiple_of(step * (groups * SUB), groups * SUB), groups * SUB)
-        return pltpu.make_async_copy(table.at[at, :], out_ref.at[at, :], done.at[step])
-
-    def one_step(step, carry):
-        firsts = [jnp.minimum(count_ref[step * groups + g] // LANES, chunks - 2) for g in range(groups)]
-        overs = [count_ref[step * groups + g + 1] > (firsts[g] + 2) * LANES for g in range(groups)]
-        for g in range(groups):
-            base = (step * groups + g) * SUB
-            at = pl.ds(pl.multiple_of(base, SUB), SUB)
-            table[at, :] = spread(firsts[g], base).astype(jnp.bfloat16)
-
-        @pl.when(functools.reduce(jnp.logical_or, overs))
-        def _():
-            def group(g, inner):
-                base = (step * groups + g) * SUB
-                total[...] = jnp.zeros((SUB, width), jnp.float32)
-
-                def more(pair, deeper):
-                    total[...] += spread(2 * pair, base)
+    def spread(start, base):
+        turn = lax.shift_right_logical(start, PACK.bit_length() - 1) & (LANES // PACK - 1)
+        ids = sorted_ref[turn, pl.ds(lax.shift_right_logical(start, 7), 1), :]
+        hot = one_hot((group, LANES), ids - base, 0)
+        at = pl.ds(pl.multiple_of(start, PACK), LANES)
+        return jnp.dot(hot, arranged[at, :], preferred_element_type=jnp.float32)
+
+    def copy_out(c):
+        size = per_copy * group
+        at = pl.ds(c * size if isinstance(c, int) else pl.multiple_of(c * size, size), size)
+        return pltpu.make_async_copy(table.at[at, :], out_ref.at[at, :], done.at[c])
+
+    over = count_ref[LANES - 1] > 0
+
+    @pl.when(jnp.logical_not(over))
+    def _():
+        for c in range(copies):
+            for number in range(c * per_copy, (c + 1) * per_copy):
+                start = start_of(count_ref[number], slots)
+                table[number * group : (number + 1) * group, :] = spread(start, number * group).astype(jnp.bfloat16)
+            copy_out(c).start()
+
+    @pl.when(over)
+    def _():
+        def one(c, carry):
+            def each(g, inner):
+                number = c * per_copy + g
+                total[...] = jnp.zeros((group, width), jnp.float32)
+
+                def more(chunk, deeper):
+                    total[...] += spread(chunk * LANES, number * group)
                     return deeper
 
-                lax.fori_loop(0, chunks // 2, more, 0)
-                table[pl.ds(pl.multiple_of(base, SUB), SUB), :] = total[...].astype(jnp.bfloat16)
+                lax.fori_loop(0, slots // LANES, more, 0)
+                table[pl.ds(pl.multiple_of(number * group, group), group), :] = total[...].astype(jnp.bfloat16)
                 return inner
 
-            lax.fori_loop(0, groups, group, 0)
-
-        copy_out(step).start()
-        return carry
-
-    lax.fori_loop(0, steps, one_step, 0)
-
-    def finish(step, carry):
-        copy_out(step).wait()
-        return carry
-
-    lax.fori_loop(0, steps, finish, 0)
+            lax.fori_loop(0, per_copy, each, 0)
+            copy_out(c).start()
+            return carry
+
+        lax.fori_loop(0, copies, one, 0)
+
+    for c in range(copies):
+        copy_out(c).wait()
 
 
 def local(queries, items, positives, item_owner, item_row):
@@ -318,7 +333,6 @@
     q_swap = [moved(q, "blk", lambda i: i ^ 1) for q in q_two]
     k_all = [k_odd, *k_two, *k_swap]
     q_all = [*q_two, q_odd, *q_swap]
-    table_groups = ROWS_DEV // SUB
     early = [k_odd, *k_two]
     top, total = call(
         functools.partial(stats_kernel, scale * LOG2E, len(early), 2, False),
@@ -334,9 +348,10 @@
         flops=pair * len(k_swap),
         trans=size * size * len(k_swap),
     )
+    group, per_copy = 512, 4
     got_rank, got_sorted, got_count = call(
-        functools.partial(order_kernel, capacity, SUB),
-        (i32((1, slots)), i32((slots // LANES, LANES)), i32((1, LANES))),
+        functools.partial(order_kernel, capacity, group, ROWS_DEV // group),
+        (i32((1, slots)), i32((LANES // PACK, slots // LANES, LANES)), i32((1, LANES))),
         (got_ids,),
         flops=32 * slots * slots,
     )
@@ -377,9 +392,8 @@
     got_rows = lax.all_to_all(
         send_rows.reshape(devices, capacity, width), ("blk", "table"), split_axis=0, concat_axis=0, tiled=True
     ).reshape(slots, width)
-    groups = 8
     table_grad = pl.pallas_call(
-        functools.partial(table_kernel, groups),
+        functools.partial(table_kernel, group, per_copy),
         out_shape=b16((ROWS_DEV, width)),
         in_specs=[pl.BlockSpec(memory_space=pltpu.SMEM), vmem(), vmem(), vmem()],
         out_specs=pl.BlockSpec(memory_space=pltpu.HBM),
@@ -387,8 +401,8 @@
             pltpu.VMEM((slots, slots), jnp.bfloat16),
             pltpu.VMEM((slots, width), jnp.bfloat16),
             pltpu.VMEM((ROWS_DEV, width), jnp.bfloat16),
-            pltpu.VMEM((SUB, width), jnp.float32),
-            pltpu.SemaphoreType.DMA((table_groups // groups,)),
+            pltpu.VMEM((group, width), jnp.float32),
+            pltpu.SemaphoreType.DMA((ROWS_DEV // (group * per_copy),)),
         ],
         compiler_params=params(32),
         cost_estimate=pl.CostEstimate(

time: 67.2 us -> 66.6 us (level)
  Pallas kernels: 20.8 us -> 20.1 us
    pallas_call x1, Pallas kernels: 6.67 us -> 5.91 us  [local(): pl.pallas_call(functools.partial(table_kernel, group, per_copy), out_shap...]
where the time goes in v3:
time: 66.6 us; the launch traced here: 66.3 us
  starting transfers between devices  22.7 us (34%)
  waiting for transfers between devices  22.7 us (34%)
  Pallas kernels  20.1 us (30%)
  between operations  0.91 us (1%)
    all_to_all x1, waiting for transfers between devices, local(): lax.all_to_all(send_rows.reshape(devices, capacity, width), ('blk', 'tabl...  14.5 us
    ppermute x9, starting transfers between devices, moved(): lax.ppermute(block, axis, [(i, target_of(i) % count) for i in range(count)])  12.4 us
    pallas_call x8, Pallas kernels, call(): pl.pallas_call(body, out_shape=out_shape, in_specs=[vmem() for _ in args]...  11.9 us
    ppermute x9, waiting for transfers between devices, moved(): lax.ppermute(block, axis, [(i, target_of(i) % count) for i in range(count)])  8.22 us
    pallas_call x1, Pallas kernels, local(): pl.pallas_call(functools.partial(table_kernel, group, per_copy), out_shap...  5.91 us
    all_to_all x1, starting transfers between devices, local(): lax.all_to_all(send_rows.reshape(devices, capacity, width), ('blk', 'tabl...  5.48 us
    all_to_all x1, starting transfers between devices, local(): lax.all_to_all(ids.reshape(devices, 1, LANES), ('blk', 'table'), split_ax...  4.81 us
    pallas_call x1, Pallas kernels, local(): pl.pallas_call(functools.partial(first_kernel, scale * LOG2E, devices, ca...  2.25 us
  transfers between devices with their start and end apart: 11, of which 4 were waited for; matrix products, arithmetic and copies ran while one was open for 0% of the time, Pallas kernels for 21%

profile of v3, /device:TPU:1, one launch (start us, length us, event | category | flops | bytes accessed | tf_op | source)
XLA Modules:
  0.0 66.3 jit_solution(10571408506669486332)
XLA Ops:
  0.6 2.1 %collective-permute-start = (bf16[512,256]{1,0:T(8,128)(2,1)}, bf16[512,256]{1,0:T(8,128)(2,1)S(1)}, u32[]{:S(2)}, u32[]{:S(2)}) collective-permute-start(bf16[512,256]{1,0:T(8,128)(2,1)} %refs_2_.1), channel_id=1, source_target_pairs={{0,8},{4,12},{8,16},{12,20},{16,24},{20,28},{24,0},{28,4},{1,9},{5... | collective-permute-start | bytes 786440 | tf_op jit(solution)/shard_map/ppermute | solution.py:23
  2.7 1.0 %collective-permute-start.3 = (bf16[512,256]{1,0:T(8,128)(2,1)}, bf16[512,256]{1,0:T(8,128)(2,1)S(1)}, u32[]{:S(2)}, u32[]{:S(2)}) collective-permute-start(bf16[512,256]{1,0:T(8,128)(2,1)} %refs_3_.1), channel_id=1, source_target_pairs={{0,24},{4,28},{8,0},{12,4},{16,8},{20,12},{24,16},{28,20},{1,25},{... | collective-permute-start | bytes 786440 | tf_op jit(solution)/shard_map/ppermute | solution.py:23
  3.7 2.5 %collective-permute-start.2 = (bf16[512,256]{1,0:T(8,128)(2,1)}, bf16[512,256]{1,0:T(8,128)(2,1)S(1)}, u32[]{:S(2)}, u32[]{:S(2)}) collective-permute-start(bf16[512,256]{1,0:T(8,128)(2,1)} %refs_2_.1), channel_id=1, source_target_pairs={{0,4},{4,16},{8,12},{12,24},{16,20},{20,0},{24,28},{28,8},{1,5},{5... | collective-permute-start | bytes 786440 | tf_op jit(solution)/shard_map/ppermute | solution.py:23
  6.2 3.7 %collective-permute-done.refs_2_ = bf16[512,256]{1,0:T(8,128)(2,1)S(1)} collective-permute-done((bf16[512,256]{1,0:T(8,128)(2,1)}, bf16[512,256]{1,0:T(8,128)(2,1)S(1)}, u32[]{:S(2)}, u32[]{:S(2)}) %collective-permute-start) | collective-permute-done | bytes 262176 | tf_op jit(solution)/shard_map/ppermute | solution.py:23
  9.9 2.1 %collective-permute-start.1 = (bf16[512,256]{1,0:T(8,128)(2,1)S(1)}, bf16[512,256]{1,0:T(8,128)(2,1)S(1)}, u32[]{:S(2)}, u32[]{:S(2)}) collective-permute-start(bf16[512,256]{1,0:T(8,128)(2,1)S(1)} %collective-permute-done.refs_2_), channel_id=1, source_target_pairs={{0,4},{4,0},{8,12},{12,8},{16,20},{20,16},{24,28},{28,24},{1,5},{5... | collective-permute-start | bytes 786440 | tf_op jit(solution)/shard_map/ppermute | solution.py:23
  12.0 0.0 collective-permute-start.6
  12.0 3.5 %collective-permute-done.3.q_ref = bf16[512,256]{1,0:T(8,128)(2,1)S(1)} collective-permute-done((bf16[512,256]{1,0:T(8,128)(2,1)}, bf16[512,256]{1,0:T(8,128)(2,1)S(1)}, u32[]{:S(2)}, u32[]{:S(2)}) %collective-permute-start.3) | collective-permute-done | bytes 262176 | tf_op jit(solution)/shard_map/ppermute | solution.py:23
  15.5 1.5 %collective-permute-start.4 = (bf16[512,256]{1,0:T(8,128)(2,1)S(1)}, bf16[512,256]{1,0:T(8,128)(2,1)S(1)}, u32[]{:S(2)}, u32[]{:S(2)}) collective-permute-start(bf16[512,256]{1,0:T(8,128)(2,1)S(1)} %collective-permute-done.3.q_ref), channel_id=1, source_target_pairs={{0,4},{4,0},{8,12},{12,8},{16,20},{20,16},{24,28},{28,24},{1,5},{5... | collective-permute-start | bytes 786440 | tf_op jit(solution)/shard_map/ppermute | solution.py:23
  17.1 2.3 %shard_map.76 = (s32[1,512]{1,0:T(1,128)S(1)}, s32[32,128]{1,0:T(8,128)}, f32[1,512]{1,0:T(1,128)S(1)}, f32[1,512]{1,0:T(1,128)S(1)}, s32[1,512]{1,0:T(1,128)S(1...) custom-call(s32[1,512]{1,0:T(1,128)} %bitcast.13, s32[1,512]{1,0:T(1,128)} %bitcast.14, ...), custom_call_target="tpu_custom_call" | custom-call | flops 134217728 | bytes 524288 | tf_op jit(solution)/shard_map/pallas_call | solution.py:308
  19.3 4.8 %all-to-all-start = ((s32[32,1,128]{2,1,0:T(1,128)}), s32[32,1,128]{2,1,0:T(1,128)S(1)}, u32[]{:S(2)}, u32[]{:S(2)}) async-start(s32[32,1,128]{2,1,0:T(1,128)} %bitcast.4), calls=%async_computation | async-start | bytes 32768 | tf_op jit(solution)/shard_map/all_to_all | solution.py:329
  24.1 0.0 collective-permute-done.2.refs_1_
  24.1 0.8 %shard_map.77 = (f32[1,512]{1,0:T(1,128)S(1)}, f32[1,512]{1,0:T(1,128)S(1)}) custom-call(bf16[512,256]{1,0:T(8,128)(2,1)S(1)} %get-tuple-element.17.refs_0_.q_ref, bf16[512,256]{1,0:T(8,128)(2,1)S(1)} %collective-permute-done.2.refs_1_, bf16[512,256]{1,0:T(8,128)(2,1)S(1)} %collective-permute-done.refs_2_, f32[1,512]{1,0:T(1,128)S(1)} %get-tuple-element.18.refs_3_, ...), custom_call_target="tpu_custom_call" | custom-call | flops 268435456 | bytes 794624 | tf_op jit(solution)/shard_map/pallas_call | solution.py:39
  24.9 0.0 collective-permute-done.1.refs_1_.refs_3_
  24.9 0.5 shard_map.78.lse_ref
  25.5 2.3 %collective-permute-start.8 = (f32[1,512]{1,0:T(1,128)S(1)}, f32[1,512]{1,0:T(1,128)S(1)}, u32[]{:S(2)}, u32[]{:S(2)}) collective-permute-start(f32[1,512]{1,0:T(1,128)S(1)} %shard_map.78.lse_ref), channel_id=1, source_target_pairs={{0,24},{4,28},{8,0},{12,4},{16,8},{20,12},{24,16},{28,20},{1,25},{... | collective-permute-start | bytes 6152 | tf_op jit(solution)/shard_map/ppermute | solution.py:23
  27.8 0.7 %collective-permute-start.7 = (f32[1,512]{1,0:T(1,128)S(1)}, f32[1,512]{1,0:T(1,128)S(1)}, u32[]{:S(2)}, u32[]{:S(2)}) collective-permute-start(f32[1,512]{1,0:T(1,128)S(1)} %shard_map.78.lse_ref), channel_id=1, source_target_pairs={{0,20},{4,0},{8,28},{12,8},{16,4},{20,16},{24,12},{28,24},{1,21},{... | collective-permute-start | bytes 6152 | tf_op jit(solution)/shard_map/ppermute | solution.py:23
  28.4 0.2 collective-permute-start.5
  28.6 0.7 %shard_map.80.refs_0_ = f32[512,256]{1,0:T(8,128)S(1)} custom-call(bf16[512,256]{1,0:T(8,128)(2,1)S(1)} %get-tuple-element.23.refs_0_.k_ref, bf16[512,256]{1,0:T(8,128)(2,1)S(1)} %get-tuple-element.17.refs_0_.q_ref, f32[1,512]{1,0:T(1,128)S(1)} %shard_map.78.lse_ref, s32[1,512]{1,0:T(1,128)S(1)} %get-tuple-element.22.pos_ref.refs_0_), custom_call_target="tpu_custom_call" | custom-call | flops 268435456 | bytes 1052672 | tf_op jit(solution)/shard_map/pallas_call | solution.py:39
  29.3 0.0 collective-permute-done.8.lse_ref
  29.3 0.7 %shard_map.81.refs_0_ = f32[512,256]{1,0:T(8,128)S(1)} custom-call(bf16[512,256]{1,0:T(8,128)(2,1)S(1)} %get-tuple-element.23.refs_0_.k_ref, bf16[512,256]{1,0:T(8,128)(2,1)S(1)} %collective-permute-done.3.q_ref, f32[1,512]{1,0:T(1,128)S(1)} %collective-permute-done.8.lse_ref, f32[512,256]{1,0:T(8,128)S(1)} %shard_map.80.refs_0_), custom_call_target="tpu_custom_call" | custom-call | flops 268435456 | bytes 1574912 | tf_op jit(solution)/shard_map/pallas_call | solution.py:39
  30.0 0.0 collective-permute-done.6.q_ref
  30.1 1.0 %collective-permute-done.7.lse_ref = f32[1,512]{1,0:T(1,128)S(1)} collective-permute-done((f32[1,512]{1,0:T(1,128)S(1)}, f32[1,512]{1,0:T(1,128)S(1)}, u32[]{:S(2)}, u32[]{:S(2)}) %collective-permute-start.7) | collective-permute-done | bytes 2080 | tf_op jit(solution)/shard_map/ppermute | solution.py:23
  31.1 0.7 %shard_map.82.refs_0_ = f32[512,256]{1,0:T(8,128)S(1)} custom-call(bf16[512,256]{1,0:T(8,128)(2,1)S(1)} %get-tuple-element.23.refs_0_.k_ref, bf16[512,256]{1,0:T(8,128)(2,1)S(1)} %collective-permute-done.6.q_ref, f32[1,512]{1,0:T(1,128)S(1)} %collective-permute-done.7.lse_ref, f32[512,256]{1,0:T(8,128)S(1)} %shard_map.81.refs_0_), custom_call_target="tpu_custom_call" | custom-call | flops 268435456 | bytes 1574912 | tf_op jit(solution)/shard_map/pallas_call | solution.py:39
  31.8 0.0 collective-permute-done.4.q_ref
  31.8 0.0 collective-permute-done.5.lse_ref
  31.8 2.2 %shard_map.83 = (bf16[512,256]{1,0:T(8,128)(2,1)}, bf16[1536,256]{1,0:T(8,128)(2,1)}) custom-call(bf16[512,256]{1,0:T(8,128)(2,1)S(1)} %get-tuple-element.23.refs_0_.k_ref, bf16[512,256]{1,0:T(8,128)(2,1)S(1)} %collective-permute-done.4.q_ref, f32[1,512]{1,0:T(1,128)S(1)} %collective-permute-done.5.lse_ref, f32[512,256]{1,0:T(8,128)S(1)} %shard_map.82.refs_0_, ...), custom_call_target="tpu_custom_call" | custom-call | flops 671088640 | bytes 2101248 | tf_op jit(solution)/shard_map/pallas_call | solution.py:39
  34.0 0.0 all-to-all-done
  34.0 5.5 %all-to-all-start.1 = ((bf16[32,48,256]{2,1,0:T(8,128)(2,1)}), bf16[32,48,256]{2,1,0:T(8,128)(2,1)S(1)}, u32[]{:S(2)}, u32[]{:S(2)}) async-start(bf16[32,48,256]{2,1,0:T(8,128)(2,1)} %bitcast.7), calls=%async_computation.1 | async-start | bytes 1572864 | tf_op jit(solution)/shard_map/all_to_all | solution.py:392
  39.5 4.0 %shard_map.84 = (s32[1,1536]{1,0:T(1,128)S(1)}, s32[8,12,128]{2,1,0:T(8,128)S(1)}, s32[1,128]{1,0:T(1,128)S(1)}) custom-call(s32[32,128]{1,0:T(8,128)S(1)} %bitcast.11), custom_call_target="tpu_custom_call" | custom-call | flops 75497472 | bytes 72192 | tf_op jit(solution)/shard_map/pallas_call | solution.py:39
  43.4 2.4 %shard_map.79 = bf16[512,256]{1,0:T(8,128)(2,1)} custom-call(bf16[512,256]{1,0:T(8,128)(2,1)S(1)} %get-tuple-element.17.refs_0_.q_ref, f32[1,512]{1,0:T(1,128)S(1)} %shard_map.78.lse_ref, s32[1,512]{1,0:T(1,128)S(1)} %get-tuple-element.22.pos_ref.refs_0_, bf16[512,256]{1,0:T(8,128)(2,1)S(1)} %get-tuple-element.23.refs_0_.k_ref, ...), custom_call_target="tpu_custom_call" | custom-call | flops 1073741824 | bytes 1576960 | tf_op jit(solution)/shard_map/pallas_call | solution.py:39
  45.8 14.5 %all-to-all-done.1 = bf16[32,48,256]{2,1,0:T(8,128)(2,1)S(1)} async-done(((bf16[32,48,256]{2,1,0:T(8,128)(2,1)}), bf16[32,48,256]{2,1,0:T(8,128)(2,1)S(1)}, u32[]{:S(2)}, u32[]{:S(2)}) %all-to-all-start.1) | async-done | bytes 786464 | tf_op jit(solution)/shard_map/all_to_all | solution.py:392
  60.3 5.9 %shard_map.85 = bf16[16384,256]{1,0:T(8,128)(2,1)} custom-call(s32[128]{0:T(128)S(1)} %bitcast.12, bf16[1536,256]{1,0:T(8,128)(2,1)S(1)} %bitcast.10, s32[1,1536]{1,0:T(1,128)S(1)} %get-tuple-element.29.rank_ref, s32[8,12,128]{2,1,0:T(8,128)S(1)} %get-tuple-element.30.sorted_ref), custom_call_target="tpu_custom_call" | custom-call | flops 1207959552 | bytes 8388608 | tf_op jit(solution)/shard_map/pallas_call | solution.py:395
Async XLA Ops:
  0.6 9.3 %collective-permute-start = (bf16[512,256]{1,0:T(8,128)(2,1)}, bf16[512,256]{1,0:T(8,128)(2,1)S(1)}, u32[]{:S(2)}, u32[]{:S(2)}) collective-permute-start(bf16[512,256]{1,0:T(8,128)(2,1)} %refs_2_.1), channel_id=1, source_target_pairs={{0,8},{4,12},{8,16},{12,20},{16,24},{20,28},{24,0},{28,4},{1,9},{5... | collective-permute-start | bytes 786440 | tf_op jit(solution)/shard_map/ppermute | solution.py:23
  2.7 12.8 %collective-permute-start.3 = (bf16[512,256]{1,0:T(8,128)(2,1)}, bf16[512,256]{1,0:T(8,128)(2,1)S(1)}, u32[]{:S(2)}, u32[]{:S(2)}) collective-permute-start(bf16[512,256]{1,0:T(8,128)(2,1)} %refs_3_.1), channel_id=1, source_target_pairs={{0,24},{4,28},{8,0},{12,4},{16,8},{20,12},{24,16},{28,20},{1,25},{... | collective-permute-start | bytes 786440 | tf_op jit(solution)/shard_map/ppermute | solution.py:23
  3.7 20.4 %collective-permute-start.2 = (bf16[512,256]{1,0:T(8,128)(2,1)}, bf16[512,256]{1,0:T(8,128)(2,1)S(1)}, u32[]{:S(2)}, u32[]{:S(2)}) collective-permute-start(bf16[512,256]{1,0:T(8,128)(2,1)} %refs_2_.1), channel_id=1, source_target_pairs={{0,4},{4,16},{8,12},{12,24},{16,20},{20,0},{24,28},{28,8},{1,5},{5... | collective-permute-start | bytes 786440 | tf_op jit(solution)/shard_map/ppermute | solution.py:23
  9.9 15.0 %collective-permute-start.1 = (bf16[512,256]{1,0:T(8,128)(2,1)S(1)}, bf16[512,256]{1,0:T(8,128)(2,1)S(1)}, u32[]{:S(2)}, u32[]{:S(2)}) collective-permute-start(bf16[512,256]{1,0:T(8,128)(2,1)S(1)} %collective-permute-done.refs_2_), channel_id=1, source_target_pairs={{0,4},{4,0},{8,12},{12,8},{16,20},{20,16},{24,28},{28,24},{1,5},{5... | collective-permute-start | bytes 786440 | tf_op jit(solution)/shard_map/ppermute | solution.py:23
  12.0 18.0 %collective-permute-start.6 = (bf16[512,256]{1,0:T(8,128)(2,1)}, bf16[512,256]{1,0:T(8,128)(2,1)S(1)}, u32[]{:S(2)}, u32[]{:S(2)}) collective-permute-start(bf16[512,256]{1,0:T(8,128)(2,1)} %refs_3_.1), channel_id=1, source_target_pairs={{0,20},{4,0},{8,28},{12,8},{16,4},{20,16},{24,12},{28,24},{1,21},{... | collective-permute-start | bytes 786440 | tf_op jit(solution)/shard_map/ppermute | solution.py:23
  15.5 16.3 %collective-permute-start.4 = (bf16[512,256]{1,0:T(8,128)(2,1)S(1)}, bf16[512,256]{1,0:T(8,128)(2,1)S(1)}, u32[]{:S(2)}, u32[]{:S(2)}) collective-permute-start(bf16[512,256]{1,0:T(8,128)(2,1)S(1)} %collective-permute-done.3.q_ref), channel_id=1, source_target_pairs={{0,4},{4,0},{8,12},{12,8},{16,20},{20,16},{24,28},{28,24},{1,5},{5... | collective-permute-start | bytes 786440 | tf_op jit(solution)/shard_map/ppermute | solution.py:23
  19.3 14.7 %all-to-all-start = ((s32[32,1,128]{2,1,0:T(1,128)}), s32[32,1,128]{2,1,0:T(1,128)S(1)}, u32[]{:S(2)}, u32[]{:S(2)}) async-start(s32[32,1,128]{2,1,0:T(1,128)} %bitcast.4), calls=%async_computation | async-start | bytes 32768 | tf_op jit(solution)/shard_map/all_to_all | solution.py:329
  25.5 3.9 %collective-permute-start.8 = (f32[1,512]{1,0:T(1,128)S(1)}, f32[1,512]{1,0:T(1,128)S(1)}, u32[]{:S(2)}, u32[]{:S(2)}) collective-permute-start(f32[1,512]{1,0:T(1,128)S(1)} %shard_map.78.lse_ref), channel_id=1, source_target_pairs={{0,24},{4,28},{8,0},{12,4},{16,8},{20,12},{24,16},{28,20},{1,25},{... | collective-permute-start | bytes 6152 | tf_op jit(solution)/shard_map/ppermute | solution.py:23
  27.8 3.3 %collective-permute-start.7 = (f32[1,512]{1,0:T(1,128)S(1)}, f32[1,512]{1,0:T(1,128)S(1)}, u32[]{:S(2)}, u32[]{:S(2)}) collective-permute-start(f32[1,512]{1,0:T(1,128)S(1)} %shard_map.78.lse_ref), channel_id=1, source_target_pairs={{0,20},{4,0},{8,28},{12,8},{16,4},{20,16},{24,12},{28,24},{1,21},{... | collective-permute-start | bytes 6152 | tf_op jit(solution)/shard_map/ppermute | solution.py:23
  28.4 3.4 %collective-permute-start.5 = (f32[1,512]{1,0:T(1,128)S(1)}, f32[1,512]{1,0:T(1,128)S(1)}, u32[]{:S(2)}, u32[]{:S(2)}) collective-permute-start(f32[1,512]{1,0:T(1,128)S(1)} %shard_map.78.lse_ref), channel_id=1, source_target_pairs={{0,28},{4,24},{8,4},{12,0},{16,12},{20,8},{24,20},{28,16},{1,29},{... | collective-permute-start | bytes 6152 | tf_op jit(solution)/shard_map/ppermute | solution.py:23
  34.0 26.3 %all-to-all-start.1 = ((bf16[32,48,256]{2,1,0:T(8,128)(2,1)}), bf16[32,48,256]{2,1,0:T(8,128)(2,1)S(1)}, u32[]{:S(2)}, u32[]{:S(2)}) async-start(bf16[32,48,256]{2,1,0:T(8,128)(2,1)} %bitcast.7), calls=%async_computation.1 | async-start | bytes 1572864 | tf_op jit(solution)/shard_map/all_to_all | solution.py:392

commit v4 on v3

--- a/solution.py
+++ b/solution.py
@@ -39,7 +39,7 @@
     return pl.pallas_call(
         body,
         out_shape=out_shape,
-        in_specs=[vmem() for _ in args],
+        in_specs=[pl.BlockSpec(memory_space=pltpu.SMEM) if a.size == 1 else vmem() for a in args],
         out_specs=specs if isinstance(out_shape, (tuple, list)) else specs[0],
         cost_estimate=pl.CostEstimate(flops=flops, bytes_accessed=moved_bytes, transcendentals=trans),
         compiler_params=params(mib),
@@ -61,9 +61,9 @@
     return jnp.where(there == row.astype(jnp.int16), jnp.bfloat16(1), jnp.bfloat16(0))
 
 
-def first_kernel(scale, devices, capacity, *refs):
-    sources, results, (owner_ref, row_ref, done) = refs[:5], refs[5:12], refs[12:]
-    slot_ref, ids_ref, top_ref, total_ref, pos_ref, q_ref, k_ref = results
+def first_kernel(devices, capacity, *refs):
+    sources, results, (owner_ref, row_ref, done) = refs[:5], refs[5:10], refs[10:]
+    slot_ref, ids_ref, pos_ref, q_ref, k_ref = results
     targets = (owner_ref, row_ref, k_ref, q_ref, pos_ref)
     copies = [pltpu.make_async_copy(a, b, done.at[i]) for i, (a, b) in enumerate(zip(sources, targets))]
     for copy in copies:
@@ -71,10 +71,8 @@
     copies[0].wait()
     copies[1].wait()
     route(devices, capacity, owner_ref, row_ref, slot_ref, ids_ref)
-    copies[2].wait()
-    copies[3].wait()
-    stats_kernel(scale, 1, 0, False, q_ref, k_ref, top_ref, total_ref)
-    copies[4].wait()
+    for copy in copies[2:]:
+        copy.wait()
 
 
 def route(devices, capacity, owner_ref, row_ref, slot_ref, ids_ref):
@@ -102,19 +100,27 @@
     ids_ref[...] = value.astype(jnp.int32)
 
 
-def order_kernel(capacity, group, groups, ids_ref, rank_ref, sorted_ref, count_ref):
-    devices = ids_ref.shape[0]
+def order_kernel(capacity, group, groups, tables, place_ref, *refs):
+    parts, (rank_ref, sorted_ref, count_ref) = refs[:tables], refs[tables:]
+    devices = tables * parts[0].shape[0]
     slots = devices * capacity
     chunks = slots // LANES
-    ids = ids_ref[...]
     lane = iota((1, LANES), 1)
+    place = place_ref[0, 0]
+    sources = []
+    for t in range(tables):
+        found = parts[0][...]
+        for d in range(1, tables):
+            found = jnp.where(lax.rem(place - d + tables, tables) == t, parts[d][...], found)
+        sources.append(found)
     rolled = {}
     rows = [jnp.zeros((1, LANES), jnp.int32) for _ in range(chunks)]
     for s in range(devices):
         at, off = divmod(s * capacity, LANES)
-        if off not in rolled:
-            rolled[off] = pltpu.roll(ids, off, 1) if off else ids
-        piece = rolled[off][s : s + 1, :]
+        block, table = divmod(s, tables)
+        if (off, table) not in rolled:
+            rolled[off, table] = pltpu.roll(sources[table], off, 1) if off else sources[table]
+        piece = rolled[off, table][block : block + 1, :]
         rows[at] = jnp.where((lane >= off) & (lane < off + capacity), piece, rows[at])
         if off + capacity > LANES:
             rows[at + 1] = jnp.where(lane < off + capacity - LANES, piece, rows[at + 1])
@@ -288,7 +294,8 @@
     scale = 3.0 / math.sqrt(width)
     blk_count = lax.axis_size("blk")
     window = blk_count // 2
-    devices = blk_count * lax.axis_size("table")
+    table_count = lax.axis_size("table")
+    devices = blk_count * table_count
     capacity = -(-(3 * size // devices) // 8) * 8
     slots = devices * capacity
     f32 = functools.partial(jax.ShapeDtypeStruct, dtype=jnp.float32)
@@ -305,39 +312,35 @@
     k_odd = moved(items, "blk", lambda i: i + window - 1 if i % 2 else i + 1)
     q_two = [moved(queries, "blk", lambda i, j=j: i - 2 * j) for j in twos]
     q_odd = moved(queries, "blk", lambda i: i - 1 if i % 2 else i - (window - 1))
-    slot, ids, top, total, pos_row, queries, items = pl.pallas_call(
-        functools.partial(first_kernel, scale * LOG2E, devices, capacity),
+    slot, ids, pos_row, queries, items = pl.pallas_call(
+        functools.partial(first_kernel, devices, capacity),
         out_shape=(
             i32((1, size)),
             i32((devices, LANES)),
-            f32((1, size)),
-            f32((1, size)),
             i32((1, size)),
             b16((size, width)),
             b16((size, width)),
         ),
         in_specs=[pl.BlockSpec(memory_space=pltpu.HBM) for _ in range(5)],
-        out_specs=tuple(vmem() for _ in range(7)),
+        out_specs=tuple(vmem() for _ in range(5)),
         scratch_shapes=[
             pltpu.VMEM((1, size), jnp.int32),
             pltpu.VMEM((1, size), jnp.int32),
             pltpu.SemaphoreType.DMA((5,)),
         ],
         compiler_params=params(12),
-        cost_estimate=pl.CostEstimate(flops=pair, bytes_accessed=4 * size * width, transcendentals=size * size),
+        cost_estimate=pl.CostEstimate(flops=size * size, bytes_accessed=4 * size * width, transcendentals=0),
     )(*[pltpu.with_memory_space_constraint(x, pltpu.HBM) for x in (owner_row, row_row, items, queries, pos_row)])
-    got_ids = lax.all_to_all(
-        ids.reshape(devices, 1, LANES), ("blk", "table"), split_axis=0, concat_axis=0, tiled=True
-    ).reshape(devices, LANES)
+    mine = lax.all_to_all(ids.reshape(blk_count, table_count, LANES), "blk", split_axis=0, concat_axis=0, tiled=True)
     k_swap = [moved(k, "blk", lambda i: i ^ 1) for k in k_two]
     q_swap = [moved(q, "blk", lambda i: i ^ 1) for q in q_two]
     k_all = [k_odd, *k_two, *k_swap]
     q_all = [*q_two, q_odd, *q_swap]
-    early = [k_odd, *k_two]
+    early = [items, k_odd, *k_two]
     top, total = call(
-        functools.partial(stats_kernel, scale * LOG2E, len(early), 2, False),
+        functools.partial(stats_kernel, scale * LOG2E, len(early), 0, False),
         (f32((1, size)), f32((1, size))),
-        (queries, *early, top, total),
+        (queries, *early),
         flops=pair * len(early),
         trans=size * size * len(early),
     )
@@ -347,13 +350,6 @@
         (queries, *k_swap, top, total),
         flops=pair * len(k_swap),
         trans=size * size * len(k_swap),
-    )
-    group, per_copy = 512, 4
-    got_rank, got_sorted, got_count = call(
-        functools.partial(order_kernel, capacity, group, ROWS_DEV // group),
-        (i32((1, slots)), i32((LANES // PACK, slots // LANES, LANES)), i32((1, LANES))),
-        (got_ids,),
-        flops=32 * slots * slots,
     )
     lse_odd = moved(lse, "blk", lambda i: i - 1 if i % 2 else i - (window - 1))
     lse_two = [moved(lse, "blk", lambda i, j=j: i - 2 * j) for j in twos]
@@ -392,6 +388,18 @@
     got_rows = lax.all_to_all(
         send_rows.reshape(devices, capacity, width), ("blk", "table"), split_axis=0, concat_axis=0, tiled=True
     ).reshape(slots, width)
+    place = lax.axis_index("table")
+    parts = [lax.dynamic_index_in_dim(mine, place, 1, keepdims=False)]
+    for d in range(1, table_count):
+        part = lax.dynamic_index_in_dim(mine, (place + d) % table_count, 1, keepdims=False)
+        parts.append(moved(part, "table", lambda i, d=d: i + d))
+    group, per_copy = 512, 4
+    got_rank, got_sorted, got_count = call(
+        functools.partial(order_kernel, capacity, group, ROWS_DEV // group, table_count),
+        (i32((1, slots)), i32((LANES // PACK, slots // LANES, LANES)), i32((1, LANES))),
+        (place.reshape(1, 1), *parts),
+        flops=32 * slots * slots,
+    )
     table_grad = pl.pallas_call(
         functools.partial(table_kernel, group, per_copy),
         out_shape=b16((ROWS_DEV, width)),

time: 66.6 us -> 71.8 us (1.078)
  the two profiles are of different devices: /device:TPU:1 before, /device:TPU:0 now
where the time goes in v4:
time: 71.8 us; the launch traced here: 71.5 us
  waiting for transfers between devices  26.5 us (37%)
  starting transfers between devices  24.2 us (34%)
  Pallas kernels  19.8 us (28%)
  between operations  0.95 us (1%)
    ppermute x12, waiting for transfers between devices, moved(): lax.ppermute(block, axis, [(i, target_of(i) % count) for i in range(count)])  26.5 us
    ppermute x12, starting transfers between devices, moved(): lax.ppermute(block, axis, [(i, target_of(i) % count) for i in range(count)])  14.5 us
    pallas_call x8, Pallas kernels, call(): pl.pallas_call(body, out_shape=out_shape, in_specs=[pl.BlockSpec(memory_s...  12.2 us
    all_to_all x1, starting transfers between devices, local(): lax.all_to_all(send_rows.reshape(devices, capacity, width), ('blk', 'tabl...  6.34 us
    pallas_call x1, Pallas kernels, local(): pl.pallas_call(functools.partial(table_kernel, group, per_copy), out_shap...  5.91 us
    all_to_all x1, starting transfers between devices, local(): lax.all_to_all(ids.reshape(blk_count, table_count, LANES), 'blk', split_a...  3.35 us
    pallas_call x1, Pallas kernels, local(): pl.pallas_call(functools.partial(first_kernel, devices, capacity), out_sh...  1.71 us
  transfers between devices with their start and end apart: 14, of which 4 were waited for; matrix products, arithmetic and copies ran while one was open for 0% of the time, Pallas kernels for 19%

profile of v4, /device:TPU:0, one launch (start us, length us, event | category | flops | bytes accessed | tf_op | source)
XLA Modules:
  0.0 71.5 jit_solution(5323250648283204391)
XLA Ops:
  0.6 3.0 %collective-permute-start = (bf16[512,256]{1,0:T(8,128)(2,1)}, bf16[512,256]{1,0:T(8,128)(2,1)S(1)}, u32[]{:S(2)}, u32[]{:S(2)}) collective-permute-start(bf16[512,256]{1,0:T(8,128)(2,1)} %refs_2_.1), channel_id=1, source_target_pairs={{0,8},{4,12},{8,16},{12,20},{16,24},{20,28},{24,0},{28,4},{1,9},{5... | collective-permute-start | bytes 786440 | tf_op jit(solution)/shard_map/ppermute | solution.py:23
  3.7 1.0 %collective-permute-start.3 = (bf16[512,256]{1,0:T(8,128)(2,1)}, bf16[512,256]{1,0:T(8,128)(2,1)S(1)}, u32[]{:S(2)}, u32[]{:S(2)}) collective-permute-start(bf16[512,256]{1,0:T(8,128)(2,1)} %refs_3_.1), channel_id=1, source_target_pairs={{0,24},{4,28},{8,0},{12,4},{16,8},{20,12},{24,16},{28,20},{1,25},{... | collective-permute-start | bytes 786440 | tf_op jit(solution)/shard_map/ppermute | solution.py:23
  4.7 0.0 collective-permute-start.2
  4.7 7.3 %collective-permute-done.refs_3_.refs_2_ = bf16[512,256]{1,0:T(8,128)(2,1)S(1)} collective-permute-done((bf16[512,256]{1,0:T(8,128)(2,1)}, bf16[512,256]{1,0:T(8,128)(2,1)S(1)}, u32[]{:S(2)}, u32[]{:S(2)}) %collective-permute-start) | collective-permute-done | bytes 262176 | tf_op jit(solution)/shard_map/ppermute | solution.py:23
  12.0 2.1 %collective-permute-start.6 = (bf16[512,256]{1,0:T(8,128)(2,1)}, bf16[512,256]{1,0:T(8,128)(2,1)S(1)}, u32[]{:S(2)}, u32[]{:S(2)}) collective-permute-start(bf16[512,256]{1,0:T(8,128)(2,1)} %refs_3_.1), channel_id=1, source_target_pairs={{0,20},{4,0},{8,28},{12,8},{16,4},{20,16},{24,12},{28,24},{1,21},{... | collective-permute-start | bytes 786440 | tf_op jit(solution)/shard_map/ppermute | solution.py:23
  14.1 2.9 %collective-permute-done.3.q_ref = bf16[512,256]{1,0:T(8,128)(2,1)S(1)} collective-permute-done((bf16[512,256]{1,0:T(8,128)(2,1)}, bf16[512,256]{1,0:T(8,128)(2,1)S(1)}, u32[]{:S(2)}, u32[]{:S(2)}) %collective-permute-start.3) | collective-permute-done | bytes 262176 | tf_op jit(solution)/shard_map/ppermute | solution.py:23
  17.0 0.0 collective-permute-start.4
  17.0 1.7 %shard_map.76 = (s32[1,512]{1,0:T(1,128)S(1)}, s32[32,128]{1,0:T(8,128)}, s32[1,512]{1,0:T(1,128)S(1)}, bf16[512,256]{1,0:T(8,128)(2,1)S(1)}, bf16[512,256]{1,0:T(8,128)(2,1)S(1)}) custom-call(s32[1,512]{1,0:T(1,128)} %bitcast.18, s32[1,512]{1,0:T(1,128)} %bitcast.19, bf16[512,256]{1,0:T(8,128)(2,1)} %refs_2_.1, bf16[512,256]{1,0:T(8,128)(2,1)} %refs_3_.1, ...), custom_call_target="tpu_custom_call" | custom-call | flops 262144 | bytes 524288 | tf_op jit(solution)/shard_map/pallas_call | solution.py:315
  18.8 3.3 %all-to-all-start = ((s32[8,4,128]{2,1,0:T(4,128)}), s32[8,4,128]{2,1,0:T(4,128)S(1)}, u32[]{:S(2)}, u32[]{:S(2)}) async-start(s32[8,4,128]{2,1,0:T(4,128)} %bitcast.4), calls=%async_computation | async-start | bytes 32768 | tf_op jit(solution)/shard_map/all_to_all | solution.py:334
  22.1 0.0 collective-permute-done.2.refs_2_.refs_1_
  22.1 1.1 %shard_map.77 = (f32[1,512]{1,0:T(1,128)S(1)}, f32[1,512]{1,0:T(1,128)S(1)}) custom-call(bf16[512,256]{1,0:T(8,128)(2,1)S(1)} %get-tuple-element.15.refs_0_.q_ref, bf16[512,256]{1,0:T(8,128)(2,1)S(1)} %get-tuple-element.16.refs_1_.refs_0_.k_ref, bf16[512,256]{1,0:T(8,128)(2,1)S(1)} %collective-permute-done.2.refs_2_.refs_1_, ...), custom_call_target="tpu_custom_call" | custom-call | flops 402653184 | bytes 1052672 | tf_op jit(solution)/shard_map/pallas_call | solution.py:39
  23.2 0.0 collective-permute-done.1.refs_1_.refs_3_
  23.2 0.5 shard_map.78.lse_ref
  23.8 2.9 %collective-permute-start.8 = (f32[1,512]{1,0:T(1,128)S(1)}, f32[1,512]{1,0:T(1,128)S(1)}, u32[]{:S(2)}, u32[]{:S(2)}) collective-permute-start(f32[1,512]{1,0:T(1,128)S(1)} %shard_map.78.lse_ref), channel_id=1, source_target_pairs={{0,24},{4,28},{8,0},{12,4},{16,8},{20,12},{24,16},{28,20},{1,25},{... | collective-permute-start | bytes 6152 | tf_op jit(solution)/shard_map/ppermute | solution.py:23
  26.6 0.7 collective-permute-start.5
  27.3 0.7 shard_map.80.refs_0_
  28.0 0.0 collective-permute-done.8.lse_ref
  28.0 0.7 shard_map.81.refs_0_
  28.8 0.0 collective-permute-done.7.lse_ref
  28.8 0.7 shard_map.82.refs_0_
  29.5 0.0 collective-permute-done.4.q_ref
  29.5 0.2 collective-permute-done.5.lse_ref
  29.7 2.2 %shard_map.83 = (bf16[512,256]{1,0:T(8,128)(2,1)}, bf16[1536,256]{1,0:T(8,128)(2,1)}) custom-call(bf16[512,256]{1,0:T(8,128)(2,1)S(1)} %get-tuple-element.16.refs_1_.refs_0_.k_ref, bf16[512,256]{1,0:T(8,128)(2,1)S(1)} %collective-permute-done.4.q_ref, f32[1,512]{1,0:T(1,128)S(1)} %collective-permute-done.5.lse_ref, f32[512,256]{1,0:T(8,128)S(1)} %shard_map.82.refs_0_, ...), custom_call_target="tpu_custom_call" | custom-call | flops 671088640 | bytes 2101248 | tf_op jit(solution)/shard_map/pallas_call | solution.py:39
  31.8 6.3 %all-to-all-start.1 = ((bf16[32,48,256]{2,1,0:T(8,128)(2,1)}), bf16[32,48,256]{2,1,0:T(8,128)(2,1)S(1)}, u32[]{:S(2)}, u32[]{:S(2)}) async-start(bf16[32,48,256]{2,1,0:T(8,128)(2,1)} %bitcast.10), calls=%async_computation.1 | async-start | bytes 1572864 | tf_op jit(solution)/shard_map/all_to_all | solution.py:388
  38.3 2.7 %collective-permute-start.10 = (s32[8,128]{1,0:T(8,128)S(1)}, s32[8,128]{1,0:T(8,128)S(1)}, u32[]{:S(2)}, u32[]{:S(2)}) collective-permute-start(s32[8,128]{1,0:T(8,128)S(1)} %bitcast.17), channel_id=1, source_target_pairs={{0,2},{1,3},{2,0},{3,1},{4,6},{5,7},{6,4},{7,5},{8,10},{9,11},{10,... | collective-permute-start | bytes 12296 | tf_op jit(solution)/shard_map/ppermute | solution.py:23
  41.0 1.5 %collective-permute-start.11 = (s32[8,128]{1,0:T(8,128)S(1)}, s32[8,128]{1,0:T(8,128)S(1)}, u32[]{:S(2)}, u32[]{:S(2)}) collective-permute-start(s32[8,128]{1,0:T(8,128)S(1)} %bitcast.16), channel_id=1, source_target_pairs={{0,3},{1,0},{2,1},{3,2},{4,7},{5,4},{6,5},{7,6},{8,11},{9,8},{10,9... | collective-permute-start | bytes 12296 | tf_op jit(solution)/shard_map/ppermute | solution.py:23
  42.5 0.6 collective-permute-start.9
  43.0 16.1 %collective-permute-done.10.refs_2_ = s32[8,128]{1,0:T(8,128)S(1)} collective-permute-done((s32[8,128]{1,0:T(8,128)S(1)}, s32[8,128]{1,0:T(8,128)S(1)}, u32[]{:S(2)}, u32[]{:S(2)}) %collective-permute-start.10) | collective-permute-done | bytes 4128 | tf_op jit(solution)/shard_map/ppermute | solution.py:23
  59.1 0.0 collective-permute-done.9.refs_1_
  59.1 4.0 %shard_map.84 = (s32[1,1536]{1,0:T(1,128)S(1)}, s32[8,12,128]{2,1,0:T(8,128)S(1)}, s32[1,128]{1,0:T(1,128)S(1)}) custom-call(s32[1,1]{1,0:T(1,128)} %bitcast.3.place_ref, s32[8,128]{1,0:T(8,128)S(1)} %bitcast.13, s32[8,128]{1,0:T(8,128)S(1)} %collective-permute-done.9.refs_1_, s32[8,128]{1,0:T(8,128)S(1)} %collective-permute-done.10.refs_2_, ...), custom_call_target="tpu_custom_call" | custom-call | flops 75497472 | bytes 72196 | tf_op jit(solution)/shard_map/pallas_call | solution.py:39
  63.1 2.4 %shard_map.79 = bf16[512,256]{1,0:T(8,128)(2,1)} custom-call(bf16[512,256]{1,0:T(8,128)(2,1)S(1)} %get-tuple-element.15.refs_0_.q_ref, f32[1,512]{1,0:T(1,128)S(1)} %shard_map.78.lse_ref, s32[1,512]{1,0:T(1,128)S(1)} %get-tuple-element.19.pos_ref.refs_0_, bf16[512,256]{1,0:T(8,128)(2,1)S(1)} %get-tuple-element.16.refs_1_.refs_0_.k_ref, ...), custom_call_target="tpu_custom_call" | custom-call | flops 1073741824 | bytes 1576960 | tf_op jit(solution)/shard_map/pallas_call | solution.py:39
  65.4 5.9 %shard_map.85 = bf16[16384,256]{1,0:T(8,128)(2,1)} custom-call(s32[128]{0:T(128)S(1)} %bitcast.14, bf16[1536,256]{1,0:T(8,128)(2,1)S(1)} %bitcast.12, s32[1,1536]{1,0:T(1,128)S(1)} %get-tuple-element.25.rank_ref, s32[8,12,128]{2,1,0:T(8,128)S(1)} %get-tuple-element.26.sorted_ref), custom_call_target="tpu_custom_call" | custom-call | flops 1207959552 | bytes 8388608 | tf_op jit(solution)/shard_map/pallas_call | solution.py:403
  (7 shorter events, 0.0 us)
Async XLA Ops:
  0.6 11.4 %collective-permute-start = (bf16[512,256]{1,0:T(8,128)(2,1)}, bf16[512,256]{1,0:T(8,128)(2,1)S(1)}, u32[]{:S(2)}, u32[]{:S(2)}) collective-permute-start(bf16[512,256]{1,0:T(8,128)(2,1)} %refs_2_.1), channel_id=1, source_target_pairs={{0,8},{4,12},{8,16},{12,20},{16,24},{20,28},{24,0},{28,4},{1,9},{5... | collective-permute-start | bytes 786440 | tf_op jit(solution)/shard_map/ppermute | solution.py:23
  3.7 13.4 %collective-permute-start.3 = (bf16[512,256]{1,0:T(8,128)(2,1)}, bf16[512,256]{1,0:T(8,128)(2,1)S(1)}, u32[]{:S(2)}, u32[]{:S(2)}) collective-permute-start(bf16[512,256]{1,0:T(8,128)(2,1)} %refs_3_.1), channel_id=1, source_target_pairs={{0,24},{4,28},{8,0},{12,4},{16,8},{20,12},{24,16},{28,20},{1,25},{... | collective-permute-start | bytes 786440 | tf_op jit(solution)/shard_map/ppermute | solution.py:23
  4.7 17.4 %collective-permute-start.2 = (bf16[512,256]{1,0:T(8,128)(2,1)}, bf16[512,256]{1,0:T(8,128)(2,1)S(1)}, u32[]{:S(2)}, u32[]{:S(2)}) collective-permute-start(bf16[512,256]{1,0:T(8,128)(2,1)} %refs_2_.1), channel_id=1, source_target_pairs={{0,4},{4,16},{8,12},{12,24},{16,20},{20,0},{24,28},{28,8},{1,5},{5... | collective-permute-start | bytes 786440 | tf_op jit(solution)/shard_map/ppermute | solution.py:23
  12.0 11.2 %collective-permute-start.1 = (bf16[512,256]{1,0:T(8,128)(2,1)S(1)}, bf16[512,256]{1,0:T(8,128)(2,1)S(1)}, u32[]{:S(2)}, u32[]{:S(2)}) collective-permute-start(bf16[512,256]{1,0:T(8,128)(2,1)S(1)} %collective-permute-done.refs_3_.refs_2_), channel_id=1, source_target_pairs={{0,4},{4,0},{8,12},{12,8},{16,20},{20,16},{24,28},{28,24},{1,5},{5... | collective-permute-start | bytes 786440 | tf_op jit(solution)/shard_map/ppermute | solution.py:23
  12.0 16.7 %collective-permute-start.6 = (bf16[512,256]{1,0:T(8,128)(2,1)}, bf16[512,256]{1,0:T(8,128)(2,1)S(1)}, u32[]{:S(2)}, u32[]{:S(2)}) collective-permute-start(bf16[512,256]{1,0:T(8,128)(2,1)} %refs_3_.1), channel_id=1, source_target_pairs={{0,20},{4,0},{8,28},{12,8},{16,4},{20,16},{24,12},{28,24},{1,21},{... | collective-permute-start | bytes 786440 | tf_op jit(solution)/shard_map/ppermute | solution.py:23
  17.0 12.4 %collective-permute-start.4 = (bf16[512,256]{1,0:T(8,128)(2,1)S(1)}, bf16[512,256]{1,0:T(8,128)(2,1)S(1)}, u32[]{:S(2)}, u32[]{:S(2)}) collective-permute-start(bf16[512,256]{1,0:T(8,128)(2,1)S(1)} %collective-permute-done.3.q_ref), channel_id=1, source_target_pairs={{0,4},{4,0},{8,12},{12,8},{16,20},{20,16},{24,28},{28,24},{1,5},{5... | collective-permute-start | bytes 786440 | tf_op jit(solution)/shard_map/ppermute | solution.py:23
  18.8 13.1 %all-to-all-start = ((s32[8,4,128]{2,1,0:T(4,128)}), s32[8,4,128]{2,1,0:T(4,128)S(1)}, u32[]{:S(2)}, u32[]{:S(2)}) async-start(s32[8,4,128]{2,1,0:T(4,128)} %bitcast.4), calls=%async_computation | async-start | bytes 32768 | tf_op jit(solution)/shard_map/all_to_all | solution.py:334
  23.8 4.3 %collective-permute-start.8 = (f32[1,512]{1,0:T(1,128)S(1)}, f32[1,512]{1,0:T(1,128)S(1)}, u32[]{:S(2)}, u32[]{:S(2)}) collective-permute-start(f32[1,512]{1,0:T(1,128)S(1)} %shard_map.78.lse_ref), channel_id=1, source_target_pairs={{0,24},{4,28},{8,0},{12,4},{16,8},{20,12},{24,16},{28,20},{1,25},{... | collective-permute-start | bytes 6152 | tf_op jit(solution)/shard_map/ppermute | solution.py:23
  26.6 2.1 %collective-permute-start.7 = (f32[1,512]{1,0:T(1,128)S(1)}, f32[1,512]{1,0:T(1,128)S(1)}, u32[]{:S(2)}, u32[]{:S(2)}) collective-permute-start(f32[1,512]{1,0:T(1,128)S(1)} %shard_map.78.lse_ref), channel_id=1, source_target_pairs={{0,20},{4,0},{8,28},{12,8},{16,4},{20,16},{24,12},{28,24},{1,21},{... | collective-permute-start | bytes 6152 | tf_op jit(solution)/shard_map/ppermute | solution.py:23
  26.6 3.0 %collective-permute-start.5 = (f32[1,512]{1,0:T(1,128)S(1)}, f32[1,512]{1,0:T(1,128)S(1)}, u32[]{:S(2)}, u32[]{:S(2)}) collective-permute-start(f32[1,512]{1,0:T(1,128)S(1)} %shard_map.78.lse_ref), channel_id=1, source_target_pairs={{0,28},{4,24},{8,4},{12,0},{16,12},{20,8},{24,20},{28,16},{1,29},{... | collective-permute-start | bytes 6152 | tf_op jit(solution)/shard_map/ppermute | solution.py:23
  31.8 33.6 %all-to-all-start.1 = ((bf16[32,48,256]{2,1,0:T(8,128)(2,1)}), bf16[32,48,256]{2,1,0:T(8,128)(2,1)S(1)}, u32[]{:S(2)}, u32[]{:S(2)}) async-start(bf16[32,48,256]{2,1,0:T(8,128)(2,1)} %bitcast.10), calls=%async_computation.1 | async-start | bytes 1572864 | tf_op jit(solution)/shard_map/all_to_all | solution.py:388
  38.3 20.8 %collective-permute-start.10 = (s32[8,128]{1,0:T(8,128)S(1)}, s32[8,128]{1,0:T(8,128)S(1)}, u32[]{:S(2)}, u32[]{:S(2)}) collective-permute-start(s32[8,128]{1,0:T(8,128)S(1)} %bitcast.17), channel_id=1, source_target_pairs={{0,2},{1,3},{2,0},{3,1},{4,6},{5,7},{6,4},{7,5},{8,10},{9,11},{10,... | collective-permute-start | bytes 12296 | tf_op jit(solution)/shard_map/ppermute | solution.py:23
  41.0 18.1 %collective-permute-start.11 = (s32[8,128]{1,0:T(8,128)S(1)}, s32[8,128]{1,0:T(8,128)S(1)}, u32[]{:S(2)}, u32[]{:S(2)}) collective-permute-start(s32[8,128]{1,0:T(8,128)S(1)} %bitcast.16), channel_id=1, source_target_pairs={{0,3},{1,0},{2,1},{3,2},{4,7},{5,4},{6,5},{7,6},{8,11},{9,8},{10,9... | collective-permute-start | bytes 12296 | tf_op jit(solution)/shard_map/ppermute | solution.py:23
  42.5 16.6 %collective-permute-start.9 = (s32[8,128]{1,0:T(8,128)S(1)}, s32[8,128]{1,0:T(8,128)S(1)}, u32[]{:S(2)}, u32[]{:S(2)}) collective-permute-start(s32[8,128]{1,0:T(8,128)S(1)} %bitcast.15), channel_id=1, source_target_pairs={{0,1},{1,2},{2,3},{3,0},{4,5},{5,6},{6,7},{7,4},{8,9},{9,10},{10,1... | collective-permute-start | bytes 12296 | tf_op jit(solution)/shard_map/ppermute | solution.py:23

commit v5 on v3

--- a/solution.py
+++ b/solution.py
@@ -13,6 +13,8 @@
 LANES = 128
 SUB = 256
 PACK = 16
+RUN = 512
+VIEW = 64
 LOG2E = math.log2(math.e)
 NT = (((1,), (1,)), ((), ()))
 TN = (((0,), (0,)), ((), ()))
@@ -31,11 +33,11 @@
     return pltpu.CompilerParams(vmem_limit_bytes=mib * 2**20)
 
 
-def call(body, out_shape, args, flops=0, trans=0, mib=12):
+def call(body, out_shape, args, flops=0, trans=0, mib=12, scratch=()):
     moved_bytes = sum(a.size * a.dtype.itemsize for a in args)
     outs = out_shape if isinstance(out_shape, (tuple, list)) else (out_shape,)
     moved_bytes += sum(math.prod(o.shape) * o.dtype.itemsize for o in outs)
-    specs = [vmem() for _ in outs]
+    specs = [pl.BlockSpec(memory_space=pltpu.HBM) if scratch else vmem() for _ in outs]
     return pl.pallas_call(
         body,
         out_shape=out_shape,
@@ -43,6 +45,7 @@
         out_specs=specs if isinstance(out_shape, (tuple, list)) else specs[0],
         cost_estimate=pl.CostEstimate(flops=flops, bytes_accessed=moved_bytes, transcendentals=trans),
         compiler_params=params(mib),
+        scratch_shapes=scratch,
     )(*args)
 
 
@@ -61,9 +64,9 @@
     return jnp.where(there == row.astype(jnp.int16), jnp.bfloat16(1), jnp.bfloat16(0))
 
 
-def first_kernel(scale, devices, capacity, *refs):
-    sources, results, (owner_ref, row_ref, done) = refs[:5], refs[5:12], refs[12:]
-    slot_ref, ids_ref, top_ref, total_ref, pos_ref, q_ref, k_ref = results
+def first_kernel(devices, capacity, *refs):
+    sources, results, (owner_ref, row_ref, done) = refs[:5], refs[5:10], refs[10:]
+    slot_ref, ids_ref, pos_ref, q_ref, k_ref = results
     targets = (owner_ref, row_ref, k_ref, q_ref, pos_ref)
     copies = [pltpu.make_async_copy(a, b, done.at[i]) for i, (a, b) in enumerate(zip(sources, targets))]
     for copy in copies:
@@ -71,10 +74,8 @@
     copies[0].wait()
     copies[1].wait()
     route(devices, capacity, owner_ref, row_ref, slot_ref, ids_ref)
-    copies[2].wait()
-    copies[3].wait()
-    stats_kernel(scale, 1, 0, False, q_ref, k_ref, top_ref, total_ref)
-    copies[4].wait()
+    for copy in copies[2:]:
+        copy.wait()
 
 
 def route(devices, capacity, owner_ref, row_ref, slot_ref, ids_ref):
@@ -105,11 +106,11 @@
 def order_kernel(capacity, group, groups, ids_ref, rank_ref, sorted_ref, count_ref):
     devices = ids_ref.shape[0]
     slots = devices * capacity
-    chunks = slots // LANES
+    chunks = RUN // LANES
     ids = ids_ref[...]
     lane = iota((1, LANES), 1)
     rolled = {}
-    rows = [jnp.zeros((1, LANES), jnp.int32) for _ in range(chunks)]
+    rows = [jnp.zeros((1, LANES), jnp.int32) for _ in range(slots // LANES)]
     for s in range(devices):
         at, off = divmod(s * capacity, LANES)
         if off not in rolled:
@@ -119,46 +120,53 @@
         if off + capacity > LANES:
             rows[at + 1] = jnp.where(lane < off + capacity - LANES, piece, rows[at + 1])
     edges = lane * group
-    count = jnp.zeros((1, LANES), jnp.float32)
-    ranks = [jnp.zeros((1, LANES), jnp.float32) for _ in range(chunks)]
     earlier = iota((LANES, LANES), 0) < iota((LANES, LANES), 1)
-    for j in range(chunks):
-        col = column(rows[j])
-        count = count + jnp.sum(jnp.where(col < edges, 1.0, 0.0), axis=0, keepdims=True)
-        for i in range(chunks):
-            if j < i:
-                hit = col <= rows[i]
-            elif j > i:
-                hit = col < rows[i]
-            else:
-                hit = (col < rows[i]) | ((col == rows[i]) & earlier)
-            ranks[i] = ranks[i] + jnp.sum(jnp.where(hit, 1.0, 0.0), axis=0, keepdims=True)
-    count = count.astype(jnp.int32)
-    covered = start_of(count, slots) + LANES
-    over = (pltpu.roll(count, LANES - 1, 1) > covered) & (lane < groups)
-    over = jnp.max(jnp.where(over, 1.0, 0.0), axis=1, keepdims=True).astype(jnp.int32)
-    count_ref[...] = jnp.where(lane == LANES - 1, over, count)
-    rank = jnp.concatenate(ranks, axis=1).astype(jnp.int32)
-    rank_ref[...] = rank
-    row = jnp.concatenate(rows, axis=1)
-    high = jnp.broadcast_to(lax.shift_right_logical(row, 7).astype(jnp.float32), (8, slots)).astype(jnp.bfloat16)
-    low = jnp.broadcast_to((row & 127).astype(jnp.float32), (8, slots)).astype(jnp.bfloat16)
-    lines = []
-    for c in range(chunks):
-        pick = one_hot((LANES, slots), rank, c * LANES)
-        up = lax.dot_general(high, pick, NT, preferred_element_type=jnp.float32)
-        down = lax.dot_general(low, pick, NT, preferred_element_type=jnp.float32)
-        lines.append((up * 128.0 + down)[0:1, :].astype(jnp.int32))
-    for o in range(LANES // PACK):
-        turned = [pltpu.roll(line, LANES - o * PACK, 1) if o else line for line in lines]
+    over = jnp.zeros((1, LANES), jnp.float32)
+    count_ref[...] = jnp.zeros_like(count_ref)
+    for run in range(slots // RUN):
+        mine = rows[run * chunks : (run + 1) * chunks]
+        count = jnp.zeros((1, LANES), jnp.float32)
+        ranks = [jnp.zeros((1, LANES), jnp.float32) for _ in range(chunks)]
+        for j in range(chunks):
+            col = column(mine[j])
+            count = count + jnp.sum(jnp.where(col < edges, 1.0, 0.0), axis=0, keepdims=True)
+            for i in range(chunks):
+                if j < i:
+                    hit = col <= mine[i]
+                elif j > i:
+                    hit = col < mine[i]
+                else:
+                    hit = (col < mine[i]) | ((col == mine[i]) & earlier)
+                ranks[i] = ranks[i] + jnp.sum(jnp.where(hit, 1.0, 0.0), axis=0, keepdims=True)
+        count = count.astype(jnp.int32)
+        past = (pltpu.roll(count, LANES - 1, 1) > start_of(count) + VIEW) & (lane < groups)
+        over = jnp.maximum(over, jnp.where(past, 1.0, 0.0))
+        count_ref[run : run + 1, :] = count
+        rank = jnp.concatenate(ranks, axis=1).astype(jnp.int32)
+        rank_ref[:, run * RUN : (run + 1) * RUN] = rank
+        row = jnp.concatenate(mine, axis=1)
+        high = jnp.broadcast_to(lax.shift_right_logical(row, 7).astype(jnp.float32), (8, RUN)).astype(jnp.bfloat16)
+        low = jnp.broadcast_to((row & 127).astype(jnp.float32), (8, RUN)).astype(jnp.bfloat16)
+        lines = []
         for c in range(chunks):
-            after_it = turned[min(c + 1, chunks - 1)]
-            sorted_ref[o, c : c + 1, :] = jnp.where(lane < LANES - o * PACK, turned[c], after_it)
-
-
-def start_of(count, slots):
+            pick = one_hot((LANES, RUN), rank, c * LANES)
+            up = lax.dot_general(high, pick, NT, preferred_element_type=jnp.float32)
+            down = lax.dot_general(low, pick, NT, preferred_element_type=jnp.float32)
+            lines.append((up * 128.0 + down)[0:1, :].astype(jnp.int32))
+        for o in range(LANES // PACK):
+            turned = [pltpu.roll(line, LANES - o * PACK, 1) if o else line for line in lines]
+            for c in range(chunks):
+                view = jnp.where(lane < LANES - o * PACK, turned[c], turned[min(c + 1, chunks - 1)])
+                if run % 2:
+                    view = pltpu.roll(view, VIEW, 1)
+                sorted_ref[run, o, c : c + 1, :] = view
+    over = jnp.max(over, axis=1, keepdims=True).astype(jnp.int32)
+    count_ref[0:1, :] = jnp.where(lane == LANES - 1, over, count_ref[0:1, :])
+
+
+def start_of(count):
     packs = lax.shift_right_logical(count, PACK.bit_length() - 1)
-    return jnp.minimum(packs * PACK, slots - LANES)
+    return jnp.minimum(packs * PACK, RUN - VIEW)
 
 
 def stats_kernel(scale, blocks, olds, final, *refs):
@@ -221,41 +229,63 @@
     if not last:
         refs[0][...] = total
         return
-    slot_ref, out_ref, send_ref = refs
+    slot_ref, out_ref, send_ref, grad_ref, stage_ref, done = refs
     grad = (scale * total).astype(jnp.bfloat16)
-    out_ref[...] = grad
-    pick = one_hot((send_ref.shape[0], size), slot_ref[...], 0)
-    send_ref[...] = jnp.dot(pick, grad, preferred_element_type=jnp.float32).astype(jnp.bfloat16)
-
-
-def table_kernel(group, per_copy, count_ref, rows_ref, rank_ref, sorted_ref, out_ref, pick, arranged, table, total, done):
+    grad_ref[...] = grad
+    copies = [pltpu.make_async_copy(grad_ref, out_ref, done.at[0])]
+    copies[0].start()
+    slots = send_ref.shape[0]
+    part = slots // 3 if slots % (3 * SUB) == 0 else slots // 2
+    for i, base in enumerate(range(0, slots, part)):
+        at = pl.ds(base, part)
+        pick = one_hot((part, size), slot_ref[...], base)
+        stage_ref[at, :] = jnp.dot(pick, grad, preferred_element_type=jnp.float32).astype(jnp.bfloat16)
+        copies.append(pltpu.make_async_copy(stage_ref.at[at, :], send_ref.at[at, :], done.at[1 + i]))
+        copies[-1].start()
+    for copy in copies:
+        copy.wait()
+
+
+def table_kernel(group, per_copy, count_ref, rows_ref, rank_ref, sorted_ref, out_ref, arranged, table, total, done):
     slots, width = arranged.shape
     groups = table.shape[0] // group
     copies = groups // per_copy
-    for at in range(0, slots, SUB):
-        pick[at : at + SUB, :] = one_hot((SUB, slots), rank_ref[...], at)
-    arranged[...] = jnp.dot(pick[...], rows_ref[...], preferred_element_type=jnp.float32).astype(jnp.bfloat16)
-
-    def spread(start, base):
-        turn = lax.shift_right_logical(start, PACK.bit_length() - 1) & (LANES // PACK - 1)
-        ids = sorted_ref[turn, pl.ds(lax.shift_right_logical(start, 7), 1), :]
-        hot = one_hot((group, LANES), ids - base, 0)
-        at = pl.ds(pl.multiple_of(start, PACK), LANES)
-        return jnp.dot(hot, arranged[at, :], preferred_element_type=jnp.float32)
+    runs = slots // RUN
+    for run in range(runs):
+        at = slice(run * RUN, (run + 1) * RUN)
+        pick = one_hot((RUN, RUN), rank_ref[:, at], 0)
+        arranged[at, :] = jnp.dot(pick, rows_ref[at, :], preferred_element_type=jnp.float32).astype(jnp.bfloat16)
+
+    lane = iota((1, LANES), 1)
+
+    def spread(starts, base):
+        views, blocks = [], []
+        for run in range(runs):
+            start = starts[run]
+            turn = lax.shift_right_logical(start, PACK.bit_length() - 1) & (LANES // PACK - 1)
+            views.append(sorted_ref[run, turn, pl.ds(lax.shift_right_logical(start, 7), 1), :])
+            blocks.append(arranged[pl.ds(pl.multiple_of(run * RUN + start, PACK), VIEW), :])
+        if runs % 2:
+            views.append(jnp.full((1, LANES), -1, jnp.int32))
+            blocks.append(blocks[-1])
+        ids = [jnp.where(lane < VIEW, a, b) for a, b in zip(views[::2], views[1::2])]
+        ids = jnp.concatenate(ids, axis=1)
+        hot = one_hot((group, ids.shape[1]), ids - base, 0)
+        return jnp.dot(hot, jnp.concatenate(blocks, axis=0), preferred_element_type=jnp.float32)
 
     def copy_out(c):
         size = per_copy * group
         at = pl.ds(c * size if isinstance(c, int) else pl.multiple_of(c * size, size), size)
         return pltpu.make_async_copy(table.at[at, :], out_ref.at[at, :], done.at[c])
 
-    over = count_ref[LANES - 1] > 0
+    over = count_ref[0, LANES - 1] > 0
 
     @pl.when(jnp.logical_not(over))
     def _():
         for c in range(copies):
             for number in range(c * per_copy, (c + 1) * per_copy):
-                start = start_of(count_ref[number], slots)
-                table[number * group : (number + 1) * group, :] = spread(start, number * group).astype(jnp.bfloat16)
+                starts = [start_of(count_ref[run, number]) for run in range(runs)]
+                table[number * group : (number + 1) * group, :] = spread(starts, number * group).astype(jnp.bfloat16)
             copy_out(c).start()
 
     @pl.when(over)
@@ -265,11 +295,11 @@
                 number = c * per_copy + g
                 total[...] = jnp.zeros((group, width), jnp.float32)
 
-                def more(chunk, deeper):
-                    total[...] += spread(chunk * LANES, number * group)
+                def more(part, deeper):
+                    total[...] += spread([part * VIEW] * runs, number * group)
                     return deeper
 
-                lax.fori_loop(0, slots // LANES, more, 0)
+                lax.fori_loop(0, RUN // VIEW, more, 0)
                 table[pl.ds(pl.multiple_of(number * group, group), group), :] = total[...].astype(jnp.bfloat16)
                 return inner
 
@@ -305,19 +335,17 @@
     k_odd = moved(items, "blk", lambda i: i + window - 1 if i % 2 else i + 1)
     q_two = [moved(queries, "blk", lambda i, j=j: i - 2 * j) for j in twos]
     q_odd = moved(queries, "blk", lambda i: i - 1 if i % 2 else i - (window - 1))
-    slot, ids, top, total, pos_row, queries, items = pl.pallas_call(
-        functools.partial(first_kernel, scale * LOG2E, devices, capacity),
+    slot, ids, pos_row, queries, items = pl.pallas_call(
+        functools.partial(first_kernel, devices, capacity),
         out_shape=(
             i32((1, size)),
             i32((devices, LANES)),
-            f32((1, size)),
-            f32((1, size)),
             i32((1, size)),
             b16((size, width)),
             b16((size, width)),
         ),
         in_specs=[pl.BlockSpec(memory_space=pltpu.HBM) for _ in range(5)],
-        out_specs=tuple(vmem() for _ in range(7)),
+        out_specs=tuple(vmem() for _ in range(5)),
         scratch_shapes=[
             pltpu.VMEM((1, size), jnp.int32),
             pltpu.VMEM((1, size), jnp.int32),
@@ -333,11 +361,11 @@
     q_swap = [moved(q, "blk", lambda i: i ^ 1) for q in q_two]
     k_all = [k_odd, *k_two, *k_swap]
     q_all = [*q_two, q_odd, *q_swap]
-    early = [k_odd, *k_two]
+    early = [items, k_odd, *k_two]
     top, total = call(
-        functools.partial(stats_kernel, scale * LOG2E, len(early), 2, False),
+        functools.partial(stats_kernel, scale * LOG2E, len(early), 0, False),
         (f32((1, size)), f32((1, size))),
-        (queries, *early, top, total),
+        (queries, *early),
         flops=pair * len(early),
         trans=size * size * len(early),
     )
@@ -351,7 +379,7 @@
     group, per_copy = 512, 4
     got_rank, got_sorted, got_count = call(
         functools.partial(order_kernel, capacity, group, ROWS_DEV // group),
-        (i32((1, slots)), i32((LANES // PACK, slots // LANES, LANES)), i32((1, LANES))),
+        (i32((1, slots)), i32((slots // RUN, LANES // PACK, RUN // LANES, LANES)), i32((8, LANES))),
         (got_ids,),
         flops=32 * slots * slots,
     )
@@ -388,6 +416,11 @@
         (items, q_all[-1], lse_all[-1], item_sum, slot),
         flops=2 * pair + 2 * slots * size * width,
         trans=size * size,
+        scratch=[
+            pltpu.VMEM((size, width), jnp.bfloat16),
+            pltpu.VMEM((slots, width), jnp.bfloat16),
+            pltpu.SemaphoreType.DMA((4,)),
+        ],
     )
     got_rows = lax.all_to_all(
         send_rows.reshape(devices, capacity, width), ("blk", "table"), split_axis=0, concat_axis=0, tiled=True
@@ -398,7 +431,6 @@
         in_specs=[pl.BlockSpec(memory_space=pltpu.SMEM), vmem(), vmem(), vmem()],
         out_specs=pl.BlockSpec(memory_space=pltpu.HBM),
         scratch_shapes=[
-            pltpu.VMEM((slots, slots), jnp.bfloat16),
             pltpu.VMEM((slots, width), jnp.bfloat16),
             pltpu.VMEM((ROWS_DEV, width), jnp.bfloat16),
             pltpu.VMEM((group, width), jnp.float32),
@@ -408,7 +440,7 @@
         cost_estimate=pl.CostEstimate(
             flops=2 * slots * slots * width, bytes_accessed=2 * ROWS_DEV * width, transcendentals=0
         ),
-    )(got_count.reshape(LANES), got_rows, got_rank, got_sorted)
+    )(got_count, got_rows, got_rank, got_sorted)
     return (query_grad, item_grad, table_grad)
 
 

time: 66.6 us -> 65.2 us (0.979)
  Pallas kernels: 20.1 us -> 16.3 us
  waiting for transfers between devices: 22.7 us -> 25.2 us
    all_to_all x1, waiting for transfers between devices: 14.5 us -> 17 us  [local(): lax.all_to_all(send_rows.reshape(devices, capacity, width), ('blk', 'tabl...]
    pallas_call x8, Pallas kernels: 11.9 us -> 9.6 us  [call(): pl.pallas_call(body, out_shape=out_shape, in_specs=[vmem() for _ in args]...]
    pallas_call x1, Pallas kernels: 5.91 us -> 4.98 us  [local(): pl.pallas_call(functools.partial(table_kernel, group, per_copy), out_shap...]
  transfers between devices with their start and end apart: 11 -> 11, of which waited for: 4 -> 4; matrix products, arithmetic and copies ran while one was open for 0% -> 0% of each run, Pallas kernels for 21% -> 17%
where the time goes in v5:
time: 65.2 us; the launch traced here: 64.9 us
  waiting for transfers between devices  25.2 us (39%)
  starting transfers between devices  22.7 us (35%)
  Pallas kernels  16.3 us (25%)
  between operations  0.75 us (1%)
    all_to_all x1, waiting for transfers between devices, local(): lax.all_to_all(send_rows.reshape(devices, capacity, width), ('blk', 'tabl...  17 us
    ppermute x9, starting transfers between devices, moved(): lax.ppermute(block, axis, [(i, target_of(i) % count) for i in range(count)])  12.4 us
    pallas_call x8, Pallas kernels, call(): pl.pallas_call(body, out_shape=out_shape, in_specs=[vmem() for _ in args]...  9.6 us
    ppermute x9, waiting for transfers between devices, moved(): lax.ppermute(block, axis, [(i, target_of(i) % count) for i in range(count)])  8.2 us
    all_to_all x1, starting transfers between devices, local(): lax.all_to_all(send_rows.reshape(devices, capacity, width), ('blk', 'tabl...  5.5 us
    pallas_call x1, Pallas kernels, local(): pl.pallas_call(functools.partial(table_kernel, group, per_copy), out_shap...  4.98 us
    all_to_all x1, starting transfers between devices, local(): lax.all_to_all(ids.reshape(devices, 1, LANES), ('blk', 'table'), split_ax...  4.81 us
    pallas_call x1, Pallas kernels, local(): pl.pallas_call(functools.partial(first_kernel, devices, capacity), out_sh...  1.71 us
  transfers between devices with their start and end apart: 11, of which 4 were waited for; matrix products, arithmetic and copies ran while one was open for 0% of the time, Pallas kernels for 17%

profile of v5, /device:TPU:1, one launch (start us, length us, event | category | flops | bytes accessed | tf_op | source)
XLA Modules:
  0.0 64.9 jit_solution(5984186849546856006)
XLA Ops:
  0.6 2.1 %collective-permute-start = (bf16[512,256]{1,0:T(8,128)(2,1)}, bf16[512,256]{1,0:T(8,128)(2,1)S(1)}, u32[]{:S(2)}, u32[]{:S(2)}) collective-permute-start(bf16[512,256]{1,0:T(8,128)(2,1)} %refs_2_.1), channel_id=1, source_target_pairs={{0,8},{4,12},{8,16},{12,20},{16,24},{20,28},{24,0},{28,4},{1,9},{5... | collective-permute-start | bytes 786440 | tf_op jit(solution)/shard_map/ppermute | solution.py:25
  2.7 1.0 %collective-permute-start.3 = (bf16[512,256]{1,0:T(8,128)(2,1)}, bf16[512,256]{1,0:T(8,128)(2,1)S(1)}, u32[]{:S(2)}, u32[]{:S(2)}) collective-permute-start(bf16[512,256]{1,0:T(8,128)(2,1)} %refs_3_.1), channel_id=1, source_target_pairs={{0,24},{4,28},{8,0},{12,4},{16,8},{20,12},{24,16},{28,20},{1,25},{... | collective-permute-start | bytes 786440 | tf_op jit(solution)/shard_map/ppermute | solution.py:25
  3.7 2.5 %collective-permute-start.2 = (bf16[512,256]{1,0:T(8,128)(2,1)}, bf16[512,256]{1,0:T(8,128)(2,1)S(1)}, u32[]{:S(2)}, u32[]{:S(2)}) collective-permute-start(bf16[512,256]{1,0:T(8,128)(2,1)} %refs_2_.1), channel_id=1, source_target_pairs={{0,4},{4,16},{8,12},{12,24},{16,20},{20,0},{24,28},{28,8},{1,5},{5... | collective-permute-start | bytes 786440 | tf_op jit(solution)/shard_map/ppermute | solution.py:25
  6.2 3.7 %collective-permute-done.refs_3_.refs_2_ = bf16[512,256]{1,0:T(8,128)(2,1)S(1)} collective-permute-done((bf16[512,256]{1,0:T(8,128)(2,1)}, bf16[512,256]{1,0:T(8,128)(2,1)S(1)}, u32[]{:S(2)}, u32[]{:S(2)}) %collective-permute-start) | collective-permute-done | bytes 262176 | tf_op jit(solution)/shard_map/ppermute | solution.py:25
  9.9 2.1 %collective-permute-start.1 = (bf16[512,256]{1,0:T(8,128)(2,1)S(1)}, bf16[512,256]{1,0:T(8,128)(2,1)S(1)}, u32[]{:S(2)}, u32[]{:S(2)}) collective-permute-start(bf16[512,256]{1,0:T(8,128)(2,1)S(1)} %collective-permute-done.refs_3_.refs_2_), channel_id=1, source_target_pairs={{0,4},{4,0},{8,12},{12,8},{16,20},{20,16},{24,28},{28,24},{1,5},{5... | collective-permute-start | bytes 786440 | tf_op jit(solution)/shard_map/ppermute | solution.py:25
  12.0 0.0 collective-permute-start.6
  12.0 3.5 %collective-permute-done.3.q_ref = bf16[512,256]{1,0:T(8,128)(2,1)S(1)} collective-permute-done((bf16[512,256]{1,0:T(8,128)(2,1)}, bf16[512,256]{1,0:T(8,128)(2,1)S(1)}, u32[]{:S(2)}, u32[]{:S(2)}) %collective-permute-start.3) | collective-permute-done | bytes 262176 | tf_op jit(solution)/shard_map/ppermute | solution.py:25
  15.5 1.5 %collective-permute-start.4 = (bf16[512,256]{1,0:T(8,128)(2,1)S(1)}, bf16[512,256]{1,0:T(8,128)(2,1)S(1)}, u32[]{:S(2)}, u32[]{:S(2)}) collective-permute-start(bf16[512,256]{1,0:T(8,128)(2,1)S(1)} %collective-permute-done.3.q_ref), channel_id=1, source_target_pairs={{0,4},{4,0},{8,12},{12,8},{16,20},{20,16},{24,28},{28,24},{1,5},{5... | collective-permute-start | bytes 786440 | tf_op jit(solution)/shard_map/ppermute | solution.py:25
  17.1 1.7 %shard_map.76 = (s32[1,512]{1,0:T(1,128)S(1)}, s32[32,128]{1,0:T(8,128)}, s32[1,512]{1,0:T(1,128)S(1)}, bf16[512,256]{1,0:T(8,128)(2,1)S(1)}, bf16[512,256]{1,0:T(8,128)(2,1)S(1)}) custom-call(s32[1,512]{1,0:T(1,128)} %bitcast.11, s32[1,512]{1,0:T(1,128)} %bitcast.12, bf16[512,256]{1,0:T(8,128)(2,1)} %refs_2_.1, bf16[512,256]{1,0:T(8,128)(2,1)} %refs_3_.1, ...), custom_call_target="tpu_custom_call" | custom-call | flops 134217728 | bytes 524288 | tf_op jit(solution)/shard_map/pallas_call | solution.py:338
  18.8 4.8 %all-to-all-start = ((s32[32,1,128]{2,1,0:T(1,128)}), s32[32,1,128]{2,1,0:T(1,128)S(1)}, u32[]{:S(2)}, u32[]{:S(2)}) async-start(s32[32,1,128]{2,1,0:T(1,128)} %bitcast.4), calls=%async_computation | async-start | bytes 32768 | tf_op jit(solution)/shard_map/all_to_all | solution.py:357
  23.6 0.0 collective-permute-done.2.refs_2_.refs_1_
  23.6 1.1 %shard_map.77 = (f32[1,512]{1,0:T(1,128)S(1)}, f32[1,512]{1,0:T(1,128)S(1)}) custom-call(bf16[512,256]{1,0:T(8,128)(2,1)S(1)} %get-tuple-element.15.refs_0_.q_ref, bf16[512,256]{1,0:T(8,128)(2,1)S(1)} %get-tuple-element.16.refs_1_.refs_0_.k_ref, bf16[512,256]{1,0:T(8,128)(2,1)S(1)} %collective-permute-done.2.refs_2_.refs_1_, ...), custom_call_target="tpu_custom_call" | custom-call | flops 402653184 | bytes 1052672 | tf_op jit(solution)/shard_map/pallas_call | solution.py:41
  24.7 0.0 collective-permute-done.1.refs_1_.refs_3_
  24.7 0.5 shard_map.78.lse_ref
  25.2 2.3 %collective-permute-start.8 = (f32[1,512]{1,0:T(1,128)S(1)}, f32[1,512]{1,0:T(1,128)S(1)}, u32[]{:S(2)}, u32[]{:S(2)}) collective-permute-start(f32[1,512]{1,0:T(1,128)S(1)} %shard_map.78.lse_ref), channel_id=1, source_target_pairs={{0,24},{4,28},{8,0},{12,4},{16,8},{20,12},{24,16},{28,20},{1,25},{... | collective-permute-start | bytes 6152 | tf_op jit(solution)/shard_map/ppermute | solution.py:25
  27.5 0.7 %collective-permute-start.7 = (f32[1,512]{1,0:T(1,128)S(1)}, f32[1,512]{1,0:T(1,128)S(1)}, u32[]{:S(2)}, u32[]{:S(2)}) collective-permute-start(f32[1,512]{1,0:T(1,128)S(1)} %shard_map.78.lse_ref), channel_id=1, source_target_pairs={{0,20},{4,0},{8,28},{12,8},{16,4},{20,16},{24,12},{28,24},{1,21},{... | collective-permute-start | bytes 6152 | tf_op jit(solution)/shard_map/ppermute | solution.py:25
  28.2 0.2 collective-permute-start.5
  28.4 0.7 %shard_map.80.refs_0_ = f32[512,256]{1,0:T(8,128)S(1)} custom-call(bf16[512,256]{1,0:T(8,128)(2,1)S(1)} %get-tuple-element.16.refs_1_.refs_0_.k_ref, bf16[512,256]{1,0:T(8,128)(2,1)S(1)} %get-tuple-element.15.refs_0_.q_ref, f32[1,512]{1,0:T(1,128)S(1)} %shard_map.78.lse_ref, s32[1,512]{1,0:T(1,128)S(1)} %get-tuple-element.19.pos_ref.refs_0_), custom_call_target="tpu_custom_call" | custom-call | flops 268435456 | bytes 1052672 | tf_op jit(solution)/shard_map/pallas_call | solution.py:41
  29.1 0.0 collective-permute-done.8.lse_ref
  29.1 0.7 %shard_map.81.refs_0_ = f32[512,256]{1,0:T(8,128)S(1)} custom-call(bf16[512,256]{1,0:T(8,128)(2,1)S(1)} %get-tuple-element.16.refs_1_.refs_0_.k_ref, bf16[512,256]{1,0:T(8,128)(2,1)S(1)} %collective-permute-done.3.q_ref, f32[1,512]{1,0:T(1,128)S(1)} %collective-permute-done.8.lse_ref, f32[512,256]{1,0:T(8,128)S(1)} %shard_map.80.refs_0_), custom_call_target="tpu_custom_call" | custom-call | flops 268435456 | bytes 1574912 | tf_op jit(solution)/shard_map/pallas_call | solution.py:41
  29.8 0.0 collective-permute-done.6.q_ref
  29.8 1.0 %collective-permute-done.7.lse_ref = f32[1,512]{1,0:T(1,128)S(1)} collective-permute-done((f32[1,512]{1,0:T(1,128)S(1)}, f32[1,512]{1,0:T(1,128)S(1)}, u32[]{:S(2)}, u32[]{:S(2)}) %collective-permute-start.7) | collective-permute-done | bytes 2080 | tf_op jit(solution)/shard_map/ppermute | solution.py:25
  30.8 0.7 %shard_map.82.refs_0_ = f32[512,256]{1,0:T(8,128)S(1)} custom-call(bf16[512,256]{1,0:T(8,128)(2,1)S(1)} %get-tuple-element.16.refs_1_.refs_0_.k_ref, bf16[512,256]{1,0:T(8,128)(2,1)S(1)} %collective-permute-done.6.q_ref, f32[1,512]{1,0:T(1,128)S(1)} %collective-permute-done.7.lse_ref, f32[512,256]{1,0:T(8,128)S(1)} %shard_map.81.refs_0_), custom_call_target="tpu_custom_call" | custom-call | flops 268435456 | bytes 1574912 | tf_op jit(solution)/shard_map/pallas_call | solution.py:41
  31.5 0.0 collective-permute-done.4.q_ref
  31.5 0.0 collective-permute-done.5.lse_ref
  31.6 2.1 %shard_map.83 = (bf16[512,256]{1,0:T(8,128)(2,1)}, bf16[1536,256]{1,0:T(8,128)(2,1)}) custom-call(bf16[512,256]{1,0:T(8,128)(2,1)S(1)} %get-tuple-element.16.refs_1_.refs_0_.k_ref, bf16[512,256]{1,0:T(8,128)(2,1)S(1)} %collective-permute-done.4.q_ref, f32[1,512]{1,0:T(1,128)S(1)} %collective-permute-done.5.lse_ref, f32[512,256]{1,0:T(8,128)S(1)} %shard_map.82.refs_0_, ...), custom_call_target="tpu_custom_call" | custom-call | flops 671088640 | bytes 2101248 | tf_op jit(solution)/shard_map/pallas_call | solution.py:41
  33.6 0.0 all-to-all-done
  33.6 5.5 %all-to-all-start.1 = ((bf16[32,48,256]{2,1,0:T(8,128)(2,1)}), bf16[32,48,256]{2,1,0:T(8,128)(2,1)S(1)}, u32[]{:S(2)}, u32[]{:S(2)}) async-start(bf16[32,48,256]{2,1,0:T(8,128)(2,1)} %bitcast.6), calls=%async_computation.1 | async-start | bytes 1572864 | tf_op jit(solution)/shard_map/all_to_all | solution.py:425
  39.1 1.4 %shard_map.84 = (s32[1,1536]{1,0:T(1,128)S(1)}, s32[3,8,4,128]{3,2,1,0:T(4,128)S(1)}, s32[8,128]{1,0:T(8,128)S(1)}) custom-call(s32[32,128]{1,0:T(8,128)S(1)} %bitcast.10), custom_call_target="tpu_custom_call" | custom-call | flops 75497472 | bytes 75776 | tf_op jit(solution)/shard_map/pallas_call | solution.py:41
  40.6 2.4 %shard_map.79 = bf16[512,256]{1,0:T(8,128)(2,1)} custom-call(bf16[512,256]{1,0:T(8,128)(2,1)S(1)} %get-tuple-element.15.refs_0_.q_ref, f32[1,512]{1,0:T(1,128)S(1)} %shard_map.78.lse_ref, s32[1,512]{1,0:T(1,128)S(1)} %get-tuple-element.19.pos_ref.refs_0_, bf16[512,256]{1,0:T(8,128)(2,1)S(1)} %get-tuple-element.16.refs_1_.refs_0_.k_ref, ...), custom_call_target="tpu_custom_call" | custom-call | flops 1073741824 | bytes 1576960 | tf_op jit(solution)/shard_map/pallas_call | solution.py:41
  42.9 17.0 %all-to-all-done.1 = bf16[32,48,256]{2,1,0:T(8,128)(2,1)S(1)} async-done(((bf16[32,48,256]{2,1,0:T(8,128)(2,1)}), bf16[32,48,256]{2,1,0:T(8,128)(2,1)S(1)}, u32[]{:S(2)}, u32[]{:S(2)}) %all-to-all-start.1) | async-done | bytes 786464 | tf_op jit(solution)/shard_map/all_to_all | solution.py:425
  59.9 5.0 %shard_map.85 = bf16[16384,256]{1,0:T(8,128)(2,1)} custom-call(s32[8,128]{1,0:T(8,128)S(1)} %get-tuple-element.23.count_ref, bf16[1536,256]{1,0:T(8,128)(2,1)S(1)} %bitcast.9, s32[1,1536]{1,0:T(1,128)S(1)} %get-tuple-element.25.rank_ref, s32[3,8,4,128]{3,2,1,0:T(4,128)S(1)} %get-tuple-element.26.sorted_ref), custom_call_target="tpu_custom_call" | custom-call | flops 1207959552 | bytes 8388608 | tf_op jit(solution)/shard_map/pallas_call | solution.py:428
Async XLA Ops:
  0.6 9.3 %collective-permute-start = (bf16[512,256]{1,0:T(8,128)(2,1)}, bf16[512,256]{1,0:T(8,128)(2,1)S(1)}, u32[]{:S(2)}, u32[]{:S(2)}) collective-permute-start(bf16[512,256]{1,0:T(8,128)(2,1)} %refs_2_.1), channel_id=1, source_target_pairs={{0,8},{4,12},{8,16},{12,20},{16,24},{20,28},{24,0},{28,4},{1,9},{5... | collective-permute-start | bytes 786440 | tf_op jit(solution)/shard_map/ppermute | solution.py:25
  2.7 12.8 %collective-permute-start.3 = (bf16[512,256]{1,0:T(8,128)(2,1)}, bf16[512,256]{1,0:T(8,128)(2,1)S(1)}, u32[]{:S(2)}, u32[]{:S(2)}) collective-permute-start(bf16[512,256]{1,0:T(8,128)(2,1)} %refs_3_.1), channel_id=1, source_target_pairs={{0,24},{4,28},{8,0},{12,4},{16,8},{20,12},{24,16},{28,20},{1,25},{... | collective-permute-start | bytes 786440 | tf_op jit(solution)/shard_map/ppermute | solution.py:25
  3.7 19.9 %collective-permute-start.2 = (bf16[512,256]{1,0:T(8,128)(2,1)}, bf16[512,256]{1,0:T(8,128)(2,1)S(1)}, u32[]{:S(2)}, u32[]{:S(2)}) collective-permute-start(bf16[512,256]{1,0:T(8,128)(2,1)} %refs_2_.1), channel_id=1, source_target_pairs={{0,4},{4,16},{8,12},{12,24},{16,20},{20,0},{24,28},{28,8},{1,5},{5... | collective-permute-start | bytes 786440 | tf_op jit(solution)/shard_map/ppermute | solution.py:25
  9.9 14.8 %collective-permute-start.1 = (bf16[512,256]{1,0:T(8,128)(2,1)S(1)}, bf16[512,256]{1,0:T(8,128)(2,1)S(1)}, u32[]{:S(2)}, u32[]{:S(2)}) collective-permute-start(bf16[512,256]{1,0:T(8,128)(2,1)S(1)} %collective-permute-done.refs_3_.refs_2_), channel_id=1, source_target_pairs={{0,4},{4,0},{8,12},{12,8},{16,20},{20,16},{24,28},{28,24},{1,5},{5... | collective-permute-start | bytes 786440 | tf_op jit(solution)/shard_map/ppermute | solution.py:25
  12.0 17.8 %collective-permute-start.6 = (bf16[512,256]{1,0:T(8,128)(2,1)}, bf16[512,256]{1,0:T(8,128)(2,1)S(1)}, u32[]{:S(2)}, u32[]{:S(2)}) collective-permute-start(bf16[512,256]{1,0:T(8,128)(2,1)} %refs_3_.1), channel_id=1, source_target_pairs={{0,20},{4,0},{8,28},{12,8},{16,4},{20,16},{24,12},{28,24},{1,21},{... | collective-permute-start | bytes 786440 | tf_op jit(solution)/shard_map/ppermute | solution.py:25
  15.5 16.0 %collective-permute-start.4 = (bf16[512,256]{1,0:T(8,128)(2,1)S(1)}, bf16[512,256]{1,0:T(8,128)(2,1)S(1)}, u32[]{:S(2)}, u32[]{:S(2)}) collective-permute-start(bf16[512,256]{1,0:T(8,128)(2,1)S(1)} %collective-permute-done.3.q_ref), channel_id=1, source_target_pairs={{0,4},{4,0},{8,12},{12,8},{16,20},{20,16},{24,28},{28,24},{1,5},{5... | collective-permute-start | bytes 786440 | tf_op jit(solution)/shard_map/ppermute | solution.py:25
  18.8 14.9 %all-to-all-start = ((s32[32,1,128]{2,1,0:T(1,128)}), s32[32,1,128]{2,1,0:T(1,128)S(1)}, u32[]{:S(2)}, u32[]{:S(2)}) async-start(s32[32,1,128]{2,1,0:T(1,128)} %bitcast.4), calls=%async_computation | async-start | bytes 32768 | tf_op jit(solution)/shard_map/all_to_all | solution.py:357
  25.2 3.9 %collective-permute-start.8 = (f32[1,512]{1,0:T(1,128)S(1)}, f32[1,512]{1,0:T(1,128)S(1)}, u32[]{:S(2)}, u32[]{:S(2)}) collective-permute-start(f32[1,512]{1,0:T(1,128)S(1)} %shard_map.78.lse_ref), channel_id=1, source_target_pairs={{0,24},{4,28},{8,0},{12,4},{16,8},{20,12},{24,16},{28,20},{1,25},{... | collective-permute-start | bytes 6152 | tf_op jit(solution)/shard_map/ppermute | solution.py:25
  27.5 3.3 %collective-permute-start.7 = (f32[1,512]{1,0:T(1,128)S(1)}, f32[1,512]{1,0:T(1,128)S(1)}, u32[]{:S(2)}, u32[]{:S(2)}) collective-permute-start(f32[1,512]{1,0:T(1,128)S(1)} %shard_map.78.lse_ref), channel_id=1, source_target_pairs={{0,20},{4,0},{8,28},{12,8},{16,4},{20,16},{24,12},{28,24},{1,21},{... | collective-permute-start | bytes 6152 | tf_op jit(solution)/shard_map/ppermute | solution.py:25
  28.2 3.3 %collective-permute-start.5 = (f32[1,512]{1,0:T(1,128)S(1)}, f32[1,512]{1,0:T(1,128)S(1)}, u32[]{:S(2)}, u32[]{:S(2)}) collective-permute-start(f32[1,512]{1,0:T(1,128)S(1)} %shard_map.78.lse_ref), channel_id=1, source_target_pairs={{0,28},{4,24},{8,4},{12,0},{16,12},{20,8},{24,20},{28,16},{1,29},{... | collective-permute-start | bytes 6152 | tf_op jit(solution)/shard_map/ppermute | solution.py:25
  33.6 26.3 %all-to-all-start.1 = ((bf16[32,48,256]{2,1,0:T(8,128)(2,1)}), bf16[32,48,256]{2,1,0:T(8,128)(2,1)S(1)}, u32[]{:S(2)}, u32[]{:S(2)}) async-start(bf16[32,48,256]{2,1,0:T(8,128)(2,1)} %bitcast.6), calls=%async_computation.1 | async-start | bytes 1572864 | tf_op jit(solution)/shard_map/all_to_all | solution.py:425

commit v6 on v5

--- a/solution.py
+++ b/solution.py
@@ -211,25 +211,34 @@
         out_ref[at, :] = (scale * total).astype(jnp.bfloat16)
 
 
-def item_kernel(scale, own, last, k_ref, q_ref, lse_ref, *refs):
-    refs = list(refs)
+def item_terms(scale, keys, q_refs, lse_refs, total, pos=None):
+    size = keys.shape[0]
+    for q_ref, lse_ref in zip(q_refs, lse_refs):
+        for base in range(0, size, SUB):
+            at = slice(base, base + SUB)
+            q = q_ref[at, :]
+            scores = (scale * LOG2E) * lax.dot_general(keys, q, NT, preferred_element_type=jnp.float32)
+            weights = jnp.exp2(scores - lse_ref[:, at])
+            if pos is not None:
+                weights = weights - jnp.where(iota((size, SUB), 0) == pos[:, at], 1.0, 0.0)
+            part = jnp.dot(weights.astype(jnp.bfloat16), q, preferred_element_type=jnp.float32)
+            total = part if total is None else total + part
+    return total
+
+
+def own_kernel(scale, k_ref, q_ref, lse_ref, pos_ref, out_ref):
+    out_ref[...] = item_terms(scale, k_ref[...], [q_ref], [lse_ref], None, pos_ref[...])
+
+
+def more_kernel(scale, blocks, k_ref, sum_ref, *refs):
+    refs[-1][...] = item_terms(scale, k_ref[...], refs[:blocks], refs[blocks : 2 * blocks], sum_ref[...])
+
+
+def item_kernel(scale, blocks, k_ref, slot_ref, sum_ref, *refs):
+    q_refs, lse_refs = refs[:blocks], refs[blocks : 2 * blocks]
+    out_ref, send_ref, grad_ref, stage_ref, done = refs[2 * blocks :]
     size = k_ref.shape[0]
-    keys = k_ref[...]
-    pos = refs.pop(0)[...] if own else None
-    total = None if own else refs.pop(0)[...]
-    for base in range(0, size, SUB):
-        at = slice(base, base + SUB)
-        q = q_ref[at, :]
-        scores = (scale * LOG2E) * lax.dot_general(keys, q, NT, preferred_element_type=jnp.float32)
-        weights = jnp.exp2(scores - lse_ref[:, at])
-        if own:
-            weights = weights - jnp.where(iota((size, SUB), 0) == pos[:, at], 1.0, 0.0)
-        part = jnp.dot(weights.astype(jnp.bfloat16), q, preferred_element_type=jnp.float32)
-        total = part if total is None else total + part
-    if not last:
-        refs[0][...] = total
-        return
-    slot_ref, out_ref, send_ref, grad_ref, stage_ref, done = refs
+    total = item_terms(scale, k_ref[...], q_refs, lse_refs, sum_ref[...])
     grad = (scale * total).astype(jnp.bfloat16)
     grad_ref[...] = grad
     copies = [pltpu.make_async_copy(grad_ref, out_ref, done.at[0])]
@@ -376,7 +385,7 @@
         flops=pair * len(k_swap),
         trans=size * size * len(k_swap),
     )
-    group, per_copy = 512, 4
+    group, per_copy = 512, 2
     got_rank, got_sorted, got_count = call(
         functools.partial(order_kernel, capacity, group, ROWS_DEV // group),
         (i32((1, slots)), i32((slots // RUN, LANES // PACK, RUN // LANES, LANES)), i32((8, LANES))),
@@ -385,7 +394,7 @@
     )
     lse_odd = moved(lse, "blk", lambda i: i - 1 if i % 2 else i - (window - 1))
     lse_two = [moved(lse, "blk", lambda i, j=j: i - 2 * j) for j in twos]
-    lse_swap = [moved(lse, "blk", lambda i, j=j: (i ^ 1) - 2 * j) for j in twos]
+    lse_swap = [moved(one, "blk", lambda i: i ^ 1) for one in lse_two]
     lse_all = [*lse_two, lse_odd, *lse_swap]
 
     query_grad = call(
@@ -396,26 +405,26 @@
         trans=size * size * window,
     )
     item_sum = call(
-        functools.partial(item_kernel, scale, True, False),
+        functools.partial(own_kernel, scale),
         f32((size, width)),
         (items, queries, lse, pos_row),
         flops=2 * pair,
         trans=size * size,
     )
-    for q, one in zip(q_all[:-1], lse_all[:-1]):
-        item_sum = call(
-            functools.partial(item_kernel, scale, False, False),
-            f32((size, width)),
-            (items, q, one, item_sum),
-            flops=2 * pair,
-            trans=size * size,
-        )
+    cut = len(q_all) - len(q_swap)
+    item_sum = call(
+        functools.partial(more_kernel, scale, cut),
+        f32((size, width)),
+        (items, item_sum, *q_all[:cut], *lse_all[:cut]),
+        flops=2 * pair * cut,
+        trans=size * size * cut,
+    )
     item_grad, send_rows = call(
-        functools.partial(item_kernel, scale, False, True),
+        functools.partial(item_kernel, scale, len(q_swap)),
         (b16((size, width)), b16((slots, width))),
-        (items, q_all[-1], lse_all[-1], item_sum, slot),
-        flops=2 * pair + 2 * slots * size * width,
-        trans=size * size,
+        (items, slot, item_sum, *q_all[cut:], *lse_all[cut:]),
+        flops=2 * pair * len(q_swap) + 2 * slots * size * width,
+        trans=size * size * len(q_swap),
         scratch=[
             pltpu.VMEM((size, width), jnp.bfloat16),
             pltpu.VMEM((slots, width), jnp.bfloat16),

time: 65.2 us -> 65.1 us (level)
  starting transfers between devices: 22.7 us -> 24.2 us
  waiting for transfers between devices: 25.2 us -> 24.2 us
    ppermute x9, starting transfers between devices: 12.4 us -> 13.9 us  [moved(): lax.ppermute(block, axis, [(i, target_of(i) % count) for i in range(count)])]
    ppermute x9, waiting for transfers between devices: 8.2 us -> 7.22 us  [moved(): lax.ppermute(block, axis, [(i, target_of(i) % count) for i in range(count)])]
    pallas_call x8 -> x7, Pallas kernels: 9.6 us -> 9.08 us  [call(): pl.pallas_call(body, out_shape=out_shape, in_specs=[vmem() for _ in args]...]
  transfers between devices with their start and end apart: 11 -> 11, of which waited for: 4 -> 3; matrix products, arithmetic and copies ran while one was open for 0% -> 0% of each run, Pallas kernels for 17% -> 17%
where the time goes in v6:
time: 65.1 us; the launch traced here: 64.8 us
  starting transfers between devices  24.2 us (37%)
  waiting for transfers between devices  24.2 us (37%)
  Pallas kernels  15.7 us (24%)
  between operations  0.72 us (1%)
    all_to_all x1, waiting for transfers between devices, local(): lax.all_to_all(send_rows.reshape(devices, capacity, width), ('blk', 'tabl...  17 us
    ppermute x9, starting transfers between devices, moved(): lax.ppermute(block, axis, [(i, target_of(i) % count) for i in range(count)])  13.9 us
    pallas_call x7, Pallas kernels, call(): pl.pallas_call(body, out_shape=out_shape, in_specs=[vmem() for _ in args]...  9.08 us
    ppermute x9, waiting for transfers between devices, moved(): lax.ppermute(block, axis, [(i, target_of(i) % count) for i in range(count)])  7.22 us
    all_to_all x1, starting transfers between devices, local(): lax.all_to_all(send_rows.reshape(devices, capacity, width), ('blk', 'tabl...  5.54 us
    pallas_call x1, Pallas kernels, local(): pl.pallas_call(functools.partial(table_kernel, group, per_copy), out_shap...  4.9 us
    all_to_all x1, starting transfers between devices, local(): lax.all_to_all(ids.reshape(devices, 1, LANES), ('blk', 'table'), split_ax...  4.81 us
    pallas_call x1, Pallas kernels, local(): pl.pallas_call(functools.partial(first_kernel, devices, capacity), out_sh...  1.71 us
  transfers between devices with their start and end apart: 11, of which 3 were waited for; matrix products, arithmetic and copies ran while one was open for 0% of the time, Pallas kernels for 17%

profile of v6, /device:TPU:1, one launch (start us, length us, event | category | flops | bytes accessed | tf_op | source)
XLA Modules:
  0.0 64.8 jit_solution(3918406679137661538)
XLA Ops:
  0.6 2.1 %collective-permute-start = (bf16[512,256]{1,0:T(8,128)(2,1)}, bf16[512,256]{1,0:T(8,128)(2,1)S(1)}, u32[]{:S(2)}, u32[]{:S(2)}) collective-permute-start(bf16[512,256]{1,0:T(8,128)(2,1)} %refs_2_.1), channel_id=1, source_target_pairs={{0,8},{4,12},{8,16},{12,20},{16,24},{20,28},{24,0},{28,4},{1,9},{5... | collective-permute-start | bytes 786440 | tf_op jit(solution)/shard_map/ppermute | solution.py:25
  2.7 1.0 %collective-permute-start.3 = (bf16[512,256]{1,0:T(8,128)(2,1)}, bf16[512,256]{1,0:T(8,128)(2,1)S(1)}, u32[]{:S(2)}, u32[]{:S(2)}) collective-permute-start(bf16[512,256]{1,0:T(8,128)(2,1)} %refs_3_.1), channel_id=1, source_target_pairs={{0,24},{4,28},{8,0},{12,4},{16,8},{20,12},{24,16},{28,20},{1,25},{... | collective-permute-start | bytes 786440 | tf_op jit(solution)/shard_map/ppermute | solution.py:25
  3.7 2.5 %collective-permute-start.2 = (bf16[512,256]{1,0:T(8,128)(2,1)}, bf16[512,256]{1,0:T(8,128)(2,1)S(1)}, u32[]{:S(2)}, u32[]{:S(2)}) collective-permute-start(bf16[512,256]{1,0:T(8,128)(2,1)} %refs_2_.1), channel_id=1, source_target_pairs={{0,4},{4,16},{8,12},{12,24},{16,20},{20,0},{24,28},{28,8},{1,5},{5... | collective-permute-start | bytes 786440 | tf_op jit(solution)/shard_map/ppermute | solution.py:25
  6.2 3.7 %collective-permute-done.refs_3_.refs_2_ = bf16[512,256]{1,0:T(8,128)(2,1)S(1)} collective-permute-done((bf16[512,256]{1,0:T(8,128)(2,1)}, bf16[512,256]{1,0:T(8,128)(2,1)S(1)}, u32[]{:S(2)}, u32[]{:S(2)}) %collective-permute-start) | collective-permute-done | bytes 262176 | tf_op jit(solution)/shard_map/ppermute | solution.py:25
  9.9 2.1 %collective-permute-start.1 = (bf16[512,256]{1,0:T(8,128)(2,1)S(1)}, bf16[512,256]{1,0:T(8,128)(2,1)S(1)}, u32[]{:S(2)}, u32[]{:S(2)}) collective-permute-start(bf16[512,256]{1,0:T(8,128)(2,1)S(1)} %collective-permute-done.refs_3_.refs_2_), channel_id=1, source_target_pairs={{0,4},{4,0},{8,12},{12,8},{16,20},{20,16},{24,28},{28,24},{1,5},{5... | collective-permute-start | bytes 786440 | tf_op jit(solution)/shard_map/ppermute | solution.py:25
  12.0 0.0 collective-permute-start.4
  12.0 3.5 %collective-permute-done.3.refs_0_ = bf16[512,256]{1,0:T(8,128)(2,1)S(1)} collective-permute-done((bf16[512,256]{1,0:T(8,128)(2,1)}, bf16[512,256]{1,0:T(8,128)(2,1)S(1)}, u32[]{:S(2)}, u32[]{:S(2)}) %collective-permute-start.3) | collective-permute-done | bytes 262176 | tf_op jit(solution)/shard_map/ppermute | solution.py:25
  15.5 1.5 %collective-permute-start.7 = (bf16[512,256]{1,0:T(8,128)(2,1)S(1)}, bf16[512,256]{1,0:T(8,128)(2,1)S(1)}, u32[]{:S(2)}, u32[]{:S(2)}) collective-permute-start(bf16[512,256]{1,0:T(8,128)(2,1)S(1)} %collective-permute-done.3.refs_0_), channel_id=1, source_target_pairs={{0,4},{4,0},{8,12},{12,8},{16,20},{20,16},{24,28},{28,24},{1,5},{5... | collective-permute-start | bytes 786440 | tf_op jit(solution)/shard_map/ppermute | solution.py:25
  17.1 1.7 %shard_map.76 = (s32[1,512]{1,0:T(1,128)S(1)}, s32[32,128]{1,0:T(8,128)}, s32[1,512]{1,0:T(1,128)S(1)}, bf16[512,256]{1,0:T(8,128)(2,1)S(1)}, bf16[512,256]{1,0:T(8,128)(2,1)S(1)}) custom-call(s32[1,512]{1,0:T(1,128)} %bitcast.11, s32[1,512]{1,0:T(1,128)} %bitcast.12, bf16[512,256]{1,0:T(8,128)(2,1)} %refs_2_.1, bf16[512,256]{1,0:T(8,128)(2,1)} %refs_3_.1, ...), custom_call_target="tpu_custom_call" | custom-call | flops 134217728 | bytes 524288 | tf_op jit(solution)/shard_map/pallas_call | solution.py:347
  18.8 4.8 %all-to-all-start = ((s32[32,1,128]{2,1,0:T(1,128)}), s32[32,1,128]{2,1,0:T(1,128)S(1)}, u32[]{:S(2)}, u32[]{:S(2)}) async-start(s32[32,1,128]{2,1,0:T(1,128)} %bitcast.4), calls=%async_computation | async-start | bytes 32768 | tf_op jit(solution)/shard_map/all_to_all | solution.py:366
  23.6 0.0 collective-permute-done.2.refs_2_.refs_1_
  23.6 1.1 %shard_map.77 = (f32[1,512]{1,0:T(1,128)S(1)}, f32[1,512]{1,0:T(1,128)S(1)}) custom-call(bf16[512,256]{1,0:T(8,128)(2,1)S(1)} %get-tuple-element.15.refs_0_.q_ref, bf16[512,256]{1,0:T(8,128)(2,1)S(1)} %get-tuple-element.16.refs_1_.refs_0_.k_ref, bf16[512,256]{1,0:T(8,128)(2,1)S(1)} %collective-permute-done.2.refs_2_.refs_1_, ...), custom_call_target="tpu_custom_call" | custom-call | flops 402653184 | bytes 1052672 | tf_op jit(solution)/shard_map/pallas_call | solution.py:41
  24.7 0.0 collective-permute-done.1.refs_1_.refs_3_
  24.7 0.5 shard_map.78.lse_ref
  25.2 0.3 collective-permute-start.6
  25.5 2.4 %collective-permute-start.5 = (f32[1,512]{1,0:T(1,128)S(1)}, f32[1,512]{1,0:T(1,128)S(1)}, u32[]{:S(2)}, u32[]{:S(2)}) collective-permute-start(f32[1,512]{1,0:T(1,128)S(1)} %shard_map.78.lse_ref), channel_id=1, source_target_pairs={{0,24},{4,28},{8,0},{12,4},{16,8},{20,12},{24,16},{28,20},{1,25},{... | collective-permute-start | bytes 6152 | tf_op jit(solution)/shard_map/ppermute | solution.py:25
  27.9 0.7 %shard_map.80.sum_ref = f32[512,256]{1,0:T(8,128)S(1)} custom-call(bf16[512,256]{1,0:T(8,128)(2,1)S(1)} %get-tuple-element.16.refs_1_.refs_0_.k_ref, bf16[512,256]{1,0:T(8,128)(2,1)S(1)} %get-tuple-element.15.refs_0_.q_ref, f32[1,512]{1,0:T(1,128)S(1)} %shard_map.78.lse_ref, s32[1,512]{1,0:T(1,128)S(1)} %get-tuple-element.19.pos_ref), custom_call_target="tpu_custom_call" | custom-call | flops 268435456 | bytes 1052672 | tf_op jit(solution)/shard_map/pallas_call | solution.py:41
  28.6 0.0 collective-permute-done.5.refs_2_
  28.7 1.9 %collective-permute-start.8 = (f32[1,512]{1,0:T(1,128)S(1)}, f32[1,512]{1,0:T(1,128)S(1)}, u32[]{:S(2)}, u32[]{:S(2)}) collective-permute-start(f32[1,512]{1,0:T(1,128)S(1)} %collective-permute-done.5.refs_2_), channel_id=1, source_target_pairs={{0,4},{4,0},{8,12},{12,8},{16,20},{20,16},{24,28},{28,24},{1,5},{5... | collective-permute-start | bytes 6152 | tf_op jit(solution)/shard_map/ppermute | solution.py:25
  30.6 0.0 collective-permute-done.4.refs_1_
  30.6 0.0 collective-permute-done.6.refs_3_
  30.6 0.9 %shard_map.81.sum_ref = f32[512,256]{1,0:T(8,128)S(1)} custom-call(bf16[512,256]{1,0:T(8,128)(2,1)S(1)} %get-tuple-element.16.refs_1_.refs_0_.k_ref, f32[512,256]{1,0:T(8,128)S(1)} %shard_map.80.sum_ref, bf16[512,256]{1,0:T(8,128)(2,1)S(1)} %collective-permute-done.3.refs_0_, bf16[512,256]{1,0:T(8,128)(2,1)S(1)} %collective-permute-done.4.refs_1_, ...), custom_call_target="tpu_custom_call" | custom-call | flops 536870912 | bytes 1839104 | tf_op jit(solution)/shard_map/pallas_call | solution.py:41
  31.5 0.0 collective-permute-done.7.refs_0_
  31.5 0.0 collective-permute-done.8.refs_1_
  31.5 2.1 %shard_map.82 = (bf16[512,256]{1,0:T(8,128)(2,1)}, bf16[1536,256]{1,0:T(8,128)(2,1)}) custom-call(bf16[512,256]{1,0:T(8,128)(2,1)S(1)} %get-tuple-element.16.refs_1_.refs_0_.k_ref, s32[1,512]{1,0:T(1,128)S(1)} %get-tuple-element.20.slot_ref, f32[512,256]{1,0:T(8,128)S(1)} %shard_map.81.sum_ref, bf16[512,256]{1,0:T(8,128)(2,1)S(1)} %collective-permute-done.7.refs_0_, ...), custom_call_target="tpu_custom_call" | custom-call | flops 671088640 | bytes 2101248 | tf_op jit(solution)/shard_map/pallas_call | solution.py:41
  33.6 0.0 all-to-all-done
  33.6 5.5 %all-to-all-start.1 = ((bf16[32,48,256]{2,1,0:T(8,128)(2,1)}), bf16[32,48,256]{2,1,0:T(8,128)(2,1)S(1)}, u32[]{:S(2)}, u32[]{:S(2)}) async-start(bf16[32,48,256]{2,1,0:T(8,128)(2,1)} %bitcast.6), calls=%async_computation.1 | async-start | bytes 1572864 | tf_op jit(solution)/shard_map/all_to_all | solution.py:434
  39.1 1.4 %shard_map.83 = (s32[1,1536]{1,0:T(1,128)S(1)}, s32[3,8,4,128]{3,2,1,0:T(4,128)S(1)}, s32[8,128]{1,0:T(8,128)S(1)}) custom-call(s32[32,128]{1,0:T(8,128)S(1)} %bitcast.10), custom_call_target="tpu_custom_call" | custom-call | flops 75497472 | bytes 75776 | tf_op jit(solution)/shard_map/pallas_call | solution.py:41
  40.6 2.4 %shard_map.79 = bf16[512,256]{1,0:T(8,128)(2,1)} custom-call(bf16[512,256]{1,0:T(8,128)(2,1)S(1)} %get-tuple-element.15.refs_0_.q_ref, f32[1,512]{1,0:T(1,128)S(1)} %shard_map.78.lse_ref, s32[1,512]{1,0:T(1,128)S(1)} %get-tuple-element.19.pos_ref, bf16[512,256]{1,0:T(8,128)(2,1)S(1)} %get-tuple-element.16.refs_1_.refs_0_.k_ref, ...), custom_call_target="tpu_custom_call" | custom-call | flops 1073741824 | bytes 1576960 | tf_op jit(solution)/shard_map/pallas_call | solution.py:41
  42.9 17.0 %all-to-all-done.1 = bf16[32,48,256]{2,1,0:T(8,128)(2,1)S(1)} async-done(((bf16[32,48,256]{2,1,0:T(8,128)(2,1)}), bf16[32,48,256]{2,1,0:T(8,128)(2,1)S(1)}, u32[]{:S(2)}, u32[]{:S(2)}) %all-to-all-start.1) | async-done | bytes 786464 | tf_op jit(solution)/shard_map/all_to_all | solution.py:434
  59.9 4.9 %shard_map.84 = bf16[16384,256]{1,0:T(8,128)(2,1)} custom-call(s32[8,128]{1,0:T(8,128)S(1)} %get-tuple-element.23.count_ref, bf16[1536,256]{1,0:T(8,128)(2,1)S(1)} %bitcast.9, s32[1,1536]{1,0:T(1,128)S(1)} %get-tuple-element.25.rank_ref, s32[3,8,4,128]{3,2,1,0:T(4,128)S(1)} %get-tuple-element.26.sorted_ref), custom_call_target="tpu_custom_call" | custom-call | flops 1207959552 | bytes 8388608 | tf_op jit(solution)/shard_map/pallas_call | solution.py:437
Async XLA Ops:
  0.6 9.3 %collective-permute-start = (bf16[512,256]{1,0:T(8,128)(2,1)}, bf16[512,256]{1,0:T(8,128)(2,1)S(1)}, u32[]{:S(2)}, u32[]{:S(2)}) collective-permute-start(bf16[512,256]{1,0:T(8,128)(2,1)} %refs_2_.1), channel_id=1, source_target_pairs={{0,8},{4,12},{8,16},{12,20},{16,24},{20,28},{24,0},{28,4},{1,9},{5... | collective-permute-start | bytes 786440 | tf_op jit(solution)/shard_map/ppermute | solution.py:25
  2.7 12.8 %collective-permute-start.3 = (bf16[512,256]{1,0:T(8,128)(2,1)}, bf16[512,256]{1,0:T(8,128)(2,1)S(1)}, u32[]{:S(2)}, u32[]{:S(2)}) collective-permute-start(bf16[512,256]{1,0:T(8,128)(2,1)} %refs_3_.1), channel_id=1, source_target_pairs={{0,24},{4,28},{8,0},{12,4},{16,8},{20,12},{24,16},{28,20},{1,25},{... | collective-permute-start | bytes 786440 | tf_op jit(solution)/shard_map/ppermute | solution.py:25
  3.7 19.9 %collective-permute-start.2 = (bf16[512,256]{1,0:T(8,128)(2,1)}, bf16[512,256]{1,0:T(8,128)(2,1)S(1)}, u32[]{:S(2)}, u32[]{:S(2)}) collective-permute-start(bf16[512,256]{1,0:T(8,128)(2,1)} %refs_2_.1), channel_id=1, source_target_pairs={{0,4},{4,16},{8,12},{12,24},{16,20},{20,0},{24,28},{28,8},{1,5},{5... | collective-permute-start | bytes 786440 | tf_op jit(solution)/shard_map/ppermute | solution.py:25
  9.9 14.8 %collective-permute-start.1 = (bf16[512,256]{1,0:T(8,128)(2,1)S(1)}, bf16[512,256]{1,0:T(8,128)(2,1)S(1)}, u32[]{:S(2)}, u32[]{:S(2)}) collective-permute-start(bf16[512,256]{1,0:T(8,128)(2,1)S(1)} %collective-permute-done.refs_3_.refs_2_), channel_id=1, source_target_pairs={{0,4},{4,0},{8,12},{12,8},{16,20},{20,16},{24,28},{28,24},{1,5},{5... | collective-permute-start | bytes 786440 | tf_op jit(solution)/shard_map/ppermute | solution.py:25
  12.0 18.6 %collective-permute-start.4 = (bf16[512,256]{1,0:T(8,128)(2,1)}, bf16[512,256]{1,0:T(8,128)(2,1)S(1)}, u32[]{:S(2)}, u32[]{:S(2)}) collective-permute-start(bf16[512,256]{1,0:T(8,128)(2,1)} %refs_3_.1), channel_id=1, source_target_pairs={{0,20},{4,0},{8,28},{12,8},{16,4},{20,16},{24,12},{28,24},{1,21},{... | collective-permute-start | bytes 786440 | tf_op jit(solution)/shard_map/ppermute | solution.py:25
  15.5 16.0 %collective-permute-start.7 = (bf16[512,256]{1,0:T(8,128)(2,1)S(1)}, bf16[512,256]{1,0:T(8,128)(2,1)S(1)}, u32[]{:S(2)}, u32[]{:S(2)}) collective-permute-start(bf16[512,256]{1,0:T(8,128)(2,1)S(1)} %collective-permute-done.3.refs_0_), channel_id=1, source_target_pairs={{0,4},{4,0},{8,12},{12,8},{16,20},{20,16},{24,28},{28,24},{1,5},{5... | collective-permute-start | bytes 786440 | tf_op jit(solution)/shard_map/ppermute | solution.py:25
  18.8 14.8 %all-to-all-start = ((s32[32,1,128]{2,1,0:T(1,128)}), s32[32,1,128]{2,1,0:T(1,128)S(1)}, u32[]{:S(2)}, u32[]{:S(2)}) async-start(s32[32,1,128]{2,1,0:T(1,128)} %bitcast.4), calls=%async_computation | async-start | bytes 32768 | tf_op jit(solution)/shard_map/all_to_all | solution.py:366
  25.2 5.4 %collective-permute-start.6 = (f32[1,512]{1,0:T(1,128)S(1)}, f32[1,512]{1,0:T(1,128)S(1)}, u32[]{:S(2)}, u32[]{:S(2)}) collective-permute-start(f32[1,512]{1,0:T(1,128)S(1)} %shard_map.78.lse_ref), channel_id=1, source_target_pairs={{0,20},{4,0},{8,28},{12,8},{16,4},{20,16},{24,12},{28,24},{1,21},{... | collective-permute-start | bytes 6152 | tf_op jit(solution)/shard_map/ppermute | solution.py:25
  25.5 3.1 %collective-permute-start.5 = (f32[1,512]{1,0:T(1,128)S(1)}, f32[1,512]{1,0:T(1,128)S(1)}, u32[]{:S(2)}, u32[]{:S(2)}) collective-permute-start(f32[1,512]{1,0:T(1,128)S(1)} %shard_map.78.lse_ref), channel_id=1, source_target_pairs={{0,24},{4,28},{8,0},{12,4},{16,8},{20,12},{24,16},{28,20},{1,25},{... | collective-permute-start | bytes 6152 | tf_op jit(solution)/shard_map/ppermute | solution.py:25
  28.7 2.8 %collective-permute-start.8 = (f32[1,512]{1,0:T(1,128)S(1)}, f32[1,512]{1,0:T(1,128)S(1)}, u32[]{:S(2)}, u32[]{:S(2)}) collective-permute-start(f32[1,512]{1,0:T(1,128)S(1)} %collective-permute-done.5.refs_2_), channel_id=1, source_target_pairs={{0,4},{4,0},{8,12},{12,8},{16,20},{20,16},{24,28},{28,24},{1,5},{5... | collective-permute-start | bytes 6152 | tf_op jit(solution)/shard_map/ppermute | solution.py:25
  33.6 26.3 %all-to-all-start.1 = ((bf16[32,48,256]{2,1,0:T(8,128)(2,1)}), bf16[32,48,256]{2,1,0:T(8,128)(2,1)S(1)}, u32[]{:S(2)}, u32[]{:S(2)}) async-start(bf16[32,48,256]{2,1,0:T(8,128)(2,1)} %bitcast.6), calls=%async_computation.1 | async-start | bytes 1572864 | tf_op jit(solution)/shard_map/all_to_all | solution.py:434

commit v7 on v6

--- a/solution.py
+++ b/solution.py
@@ -64,7 +64,7 @@
     return jnp.where(there == row.astype(jnp.int16), jnp.bfloat16(1), jnp.bfloat16(0))
 
 
-def first_kernel(devices, capacity, *refs):
+def first_kernel(devices, tables, capacity, *refs):
     sources, results, (owner_ref, row_ref, done) = refs[:5], refs[5:10], refs[10:]
     slot_ref, ids_ref, pos_ref, q_ref, k_ref = results
     targets = (owner_ref, row_ref, k_ref, q_ref, pos_ref)
@@ -73,14 +73,15 @@
         copy.start()
     copies[0].wait()
     copies[1].wait()
-    route(devices, capacity, owner_ref, row_ref, slot_ref, ids_ref)
+    route(devices, tables, capacity, owner_ref, row_ref, slot_ref, ids_ref)
     for copy in copies[2:]:
         copy.wait()
 
 
-def route(devices, capacity, owner_ref, row_ref, slot_ref, ids_ref):
+def route(devices, tables, capacity, owner_ref, row_ref, slot_ref, ids_ref):
     size = owner_ref.shape[1]
     owner = owner_ref[...]
+    owner = lax.rem(owner, tables) * (devices // tables) + lax.div(owner, tables)
     rank = jnp.zeros((1, size), jnp.float32)
     for base in range(0, size, LANES):
         col = column(owner[:, base : base + LANES])
@@ -345,7 +346,7 @@
     q_two = [moved(queries, "blk", lambda i, j=j: i - 2 * j) for j in twos]
     q_odd = moved(queries, "blk", lambda i: i - 1 if i % 2 else i - (window - 1))
     slot, ids, pos_row, queries, items = pl.pallas_call(
-        functools.partial(first_kernel, devices, capacity),
+        functools.partial(first_kernel, devices, lax.axis_size("table"), capacity),
         out_shape=(
             i32((1, size)),
             i32((devices, LANES)),
@@ -364,7 +365,7 @@
         cost_estimate=pl.CostEstimate(flops=pair, bytes_accessed=4 * size * width, transcendentals=size * size),
     )(*[pltpu.with_memory_space_constraint(x, pltpu.HBM) for x in (owner_row, row_row, items, queries, pos_row)])
     got_ids = lax.all_to_all(
-        ids.reshape(devices, 1, LANES), ("blk", "table"), split_axis=0, concat_axis=0, tiled=True
+        ids.reshape(devices, 1, LANES), ("table", "blk"), split_axis=0, concat_axis=0, tiled=True
     ).reshape(devices, LANES)
     k_swap = [moved(k, "blk", lambda i: i ^ 1) for k in k_two]
     q_swap = [moved(q, "blk", lambda i: i ^ 1) for q in q_two]
@@ -432,7 +433,7 @@
         ],
     )
     got_rows = lax.all_to_all(
-        send_rows.reshape(devices, capacity, width), ("blk", "table"), split_axis=0, concat_axis=0, tiled=True
+        send_rows.reshape(devices, capacity, width), ("table", "blk"), split_axis=0, concat_axis=0, tiled=True
     ).reshape(slots, width)
     table_grad = pl.pallas_call(
         functools.partial(table_kernel, group, per_copy),

time: 65.1 us -> 65.1 us (level)
  no operation moved by 1% of the time
where the time goes in v7:
time: 65.1 us; the launch traced here: 64.2 us
  starting transfers between devices  24.2 us (37%)
  waiting for transfers between devices  23.6 us (36%)
  Pallas kernels  15.7 us (24%)
  between operations  0.72 us (1%)
    all_to_all x1, waiting for transfers between devices, local(): lax.all_to_all(send_rows.reshape(devices, capacity, width), ('table', 'bl...  16.4 us
    ppermute x9, starting transfers between devices, moved(): lax.ppermute(block, axis, [(i, target_of(i) % count) for i in range(count)])  13.9 us
    pallas_call x7, Pallas kernels, call(): pl.pallas_call(body, out_shape=out_shape, in_specs=[vmem() for _ in args]...  9.08 us
    ppermute x9, waiting for transfers between devices, moved(): lax.ppermute(block, axis, [(i, target_of(i) % count) for i in range(count)])  7.22 us
    all_to_all x1, starting transfers between devices, local(): lax.all_to_all(send_rows.reshape(devices, capacity, width), ('table', 'bl...  5.54 us
    pallas_call x1, Pallas kernels, local(): pl.pallas_call(functools.partial(table_kernel, group, per_copy), out_shap...  4.89 us
    all_to_all x1, starting transfers between devices, local(): lax.all_to_all(ids.reshape(devices, 1, LANES), ('table', 'blk'), split_ax...  4.81 us
    pallas_call x1, Pallas kernels, local(): pl.pallas_call(functools.partial(first_kernel, devices, lax.axis_size('ta...  1.71 us
  transfers between devices with their start and end apart: 11, of which 3 were waited for; matrix products, arithmetic and copies ran while one was open for 0% of the time, Pallas kernels for 17%

profile of v7, /device:TPU:1, one launch (start us, length us, event | category | flops | bytes accessed | tf_op | source)
XLA Modules:
  0.0 64.2 jit_solution(16238349613901930431)
XLA Ops:
  0.6 2.1 %collective-permute-start = (bf16[512,256]{1,0:T(8,128)(2,1)}, bf16[512,256]{1,0:T(8,128)(2,1)S(1)}, u32[]{:S(2)}, u32[]{:S(2)}) collective-permute-start(bf16[512,256]{1,0:T(8,128)(2,1)} %refs_2_.1), channel_id=1, source_target_pairs={{0,8},{4,12},{8,16},{12,20},{16,24},{20,28},{24,0},{28,4},{1,9},{5... | collective-permute-start | bytes 786440 | tf_op jit(solution)/shard_map/ppermute | solution.py:25
  2.7 1.0 %collective-permute-start.3 = (bf16[512,256]{1,0:T(8,128)(2,1)}, bf16[512,256]{1,0:T(8,128)(2,1)S(1)}, u32[]{:S(2)}, u32[]{:S(2)}) collective-permute-start(bf16[512,256]{1,0:T(8,128)(2,1)} %refs_3_.1), channel_id=1, source_target_pairs={{0,24},{4,28},{8,0},{12,4},{16,8},{20,12},{24,16},{28,20},{1,25},{... | collective-permute-start | bytes 786440 | tf_op jit(solution)/shard_map/ppermute | solution.py:25
  3.7 2.5 %collective-permute-start.2 = (bf16[512,256]{1,0:T(8,128)(2,1)}, bf16[512,256]{1,0:T(8,128)(2,1)S(1)}, u32[]{:S(2)}, u32[]{:S(2)}) collective-permute-start(bf16[512,256]{1,0:T(8,128)(2,1)} %refs_2_.1), channel_id=1, source_target_pairs={{0,4},{4,16},{8,12},{12,24},{16,20},{20,0},{24,28},{28,8},{1,5},{5... | collective-permute-start | bytes 786440 | tf_op jit(solution)/shard_map/ppermute | solution.py:25
  6.2 3.7 %collective-permute-done.refs_3_.refs_2_ = bf16[512,256]{1,0:T(8,128)(2,1)S(1)} collective-permute-done((bf16[512,256]{1,0:T(8,128)(2,1)}, bf16[512,256]{1,0:T(8,128)(2,1)S(1)}, u32[]{:S(2)}, u32[]{:S(2)}) %collective-permute-start) | collective-permute-done | bytes 262176 | tf_op jit(solution)/shard_map/ppermute | solution.py:25
  9.9 2.1 %collective-permute-start.1 = (bf16[512,256]{1,0:T(8,128)(2,1)S(1)}, bf16[512,256]{1,0:T(8,128)(2,1)S(1)}, u32[]{:S(2)}, u32[]{:S(2)}) collective-permute-start(bf16[512,256]{1,0:T(8,128)(2,1)S(1)} %collective-permute-done.refs_3_.refs_2_), channel_id=1, source_target_pairs={{0,4},{4,0},{8,12},{12,8},{16,20},{20,16},{24,28},{28,24},{1,5},{5... | collective-permute-start | bytes 786440 | tf_op jit(solution)/shard_map/ppermute | solution.py:25
  12.0 0.0 collective-permute-start.4
  12.0 3.5 %collective-permute-done.3.refs_0_ = bf16[512,256]{1,0:T(8,128)(2,1)S(1)} collective-permute-done((bf16[512,256]{1,0:T(8,128)(2,1)}, bf16[512,256]{1,0:T(8,128)(2,1)S(1)}, u32[]{:S(2)}, u32[]{:S(2)}) %collective-permute-start.3) | collective-permute-done | bytes 262176 | tf_op jit(solution)/shard_map/ppermute | solution.py:25
  15.5 1.5 %collective-permute-start.7 = (bf16[512,256]{1,0:T(8,128)(2,1)S(1)}, bf16[512,256]{1,0:T(8,128)(2,1)S(1)}, u32[]{:S(2)}, u32[]{:S(2)}) collective-permute-start(bf16[512,256]{1,0:T(8,128)(2,1)S(1)} %collective-permute-done.3.refs_0_), channel_id=1, source_target_pairs={{0,4},{4,0},{8,12},{12,8},{16,20},{20,16},{24,28},{28,24},{1,5},{5... | collective-permute-start | bytes 786440 | tf_op jit(solution)/shard_map/ppermute | solution.py:25
  17.1 1.7 %shard_map.76 = (s32[1,512]{1,0:T(1,128)S(1)}, s32[32,128]{1,0:T(8,128)}, s32[1,512]{1,0:T(1,128)S(1)}, bf16[512,256]{1,0:T(8,128)(2,1)S(1)}, bf16[512,256]{1,0:T(8,128)(2,1)S(1)}) custom-call(s32[1,512]{1,0:T(1,128)} %bitcast.11, s32[1,512]{1,0:T(1,128)} %bitcast.12, bf16[512,256]{1,0:T(8,128)(2,1)} %refs_2_.1, bf16[512,256]{1,0:T(8,128)(2,1)} %refs_3_.1, ...), custom_call_target="tpu_custom_call" | custom-call | flops 134217728 | bytes 524288 | tf_op jit(solution)/shard_map/pallas_call | solution.py:348
  18.8 4.8 %all-to-all-start = ((s32[32,1,128]{2,1,0:T(1,128)}), s32[32,1,128]{2,1,0:T(1,128)S(1)}, u32[]{:S(2)}, u32[]{:S(2)}) async-start(s32[32,1,128]{2,1,0:T(1,128)} %bitcast.4), calls=%async_computation | async-start | bytes 32768 | tf_op jit(solution)/shard_map/all_to_all | solution.py:367
  23.6 0.0 collective-permute-done.2.refs_2_.refs_1_
  23.6 1.1 %shard_map.77 = (f32[1,512]{1,0:T(1,128)S(1)}, f32[1,512]{1,0:T(1,128)S(1)}) custom-call(bf16[512,256]{1,0:T(8,128)(2,1)S(1)} %get-tuple-element.15.refs_0_.q_ref, bf16[512,256]{1,0:T(8,128)(2,1)S(1)} %get-tuple-element.16.refs_1_.refs_0_.k_ref, bf16[512,256]{1,0:T(8,128)(2,1)S(1)} %collective-permute-done.2.refs_2_.refs_1_, ...), custom_call_target="tpu_custom_call" | custom-call | flops 402653184 | bytes 1052672 | tf_op jit(solution)/shard_map/pallas_call | solution.py:41
  24.7 0.0 collective-permute-done.1.refs_1_.refs_3_
  24.7 0.5 shard_map.78.lse_ref
  25.2 0.3 collective-permute-start.6
  25.5 2.4 %collective-permute-start.5 = (f32[1,512]{1,0:T(1,128)S(1)}, f32[1,512]{1,0:T(1,128)S(1)}, u32[]{:S(2)}, u32[]{:S(2)}) collective-permute-start(f32[1,512]{1,0:T(1,128)S(1)} %shard_map.78.lse_ref), channel_id=1, source_target_pairs={{0,24},{4,28},{8,0},{12,4},{16,8},{20,12},{24,16},{28,20},{1,25},{... | collective-permute-start | bytes 6152 | tf_op jit(solution)/shard_map/ppermute | solution.py:25
  27.9 0.7 %shard_map.80.sum_ref = f32[512,256]{1,0:T(8,128)S(1)} custom-call(bf16[512,256]{1,0:T(8,128)(2,1)S(1)} %get-tuple-element.16.refs_1_.refs_0_.k_ref, bf16[512,256]{1,0:T(8,128)(2,1)S(1)} %get-tuple-element.15.refs_0_.q_ref, f32[1,512]{1,0:T(1,128)S(1)} %shard_map.78.lse_ref, s32[1,512]{1,0:T(1,128)S(1)} %get-tuple-element.19.pos_ref), custom_call_target="tpu_custom_call" | custom-call | flops 268435456 | bytes 1052672 | tf_op jit(solution)/shard_map/pallas_call | solution.py:41
  28.6 0.0 collective-permute-done.5.refs_2_
  28.7 1.9 %collective-permute-start.8 = (f32[1,512]{1,0:T(1,128)S(1)}, f32[1,512]{1,0:T(1,128)S(1)}, u32[]{:S(2)}, u32[]{:S(2)}) collective-permute-start(f32[1,512]{1,0:T(1,128)S(1)} %collective-permute-done.5.refs_2_), channel_id=1, source_target_pairs={{0,4},{4,0},{8,12},{12,8},{16,20},{20,16},{24,28},{28,24},{1,5},{5... | collective-permute-start | bytes 6152 | tf_op jit(solution)/shard_map/ppermute | solution.py:25
  30.6 0.0 collective-permute-done.4.refs_1_
  30.6 0.0 collective-permute-done.6.refs_3_
  30.6 0.9 %shard_map.81.sum_ref = f32[512,256]{1,0:T(8,128)S(1)} custom-call(bf16[512,256]{1,0:T(8,128)(2,1)S(1)} %get-tuple-element.16.refs_1_.refs_0_.k_ref, f32[512,256]{1,0:T(8,128)S(1)} %shard_map.80.sum_ref, bf16[512,256]{1,0:T(8,128)(2,1)S(1)} %collective-permute-done.3.refs_0_, bf16[512,256]{1,0:T(8,128)(2,1)S(1)} %collective-permute-done.4.refs_1_, ...), custom_call_target="tpu_custom_call" | custom-call | flops 536870912 | bytes 1839104 | tf_op jit(solution)/shard_map/pallas_call | solution.py:41
  31.5 0.0 collective-permute-done.7.refs_0_
  31.5 0.0 collective-permute-done.8.refs_1_
  31.5 2.1 %shard_map.82 = (bf16[512,256]{1,0:T(8,128)(2,1)}, bf16[1536,256]{1,0:T(8,128)(2,1)}) custom-call(bf16[512,256]{1,0:T(8,128)(2,1)S(1)} %get-tuple-element.16.refs_1_.refs_0_.k_ref, s32[1,512]{1,0:T(1,128)S(1)} %get-tuple-element.20.slot_ref, f32[512,256]{1,0:T(8,128)S(1)} %shard_map.81.sum_ref, bf16[512,256]{1,0:T(8,128)(2,1)S(1)} %collective-permute-done.7.refs_0_, ...), custom_call_target="tpu_custom_call" | custom-call | flops 671088640 | bytes 2101248 | tf_op jit(solution)/shard_map/pallas_call | solution.py:41
  33.6 0.0 all-to-all-done
  33.6 5.5 %all-to-all-start.1 = ((bf16[32,48,256]{2,1,0:T(8,128)(2,1)}), bf16[32,48,256]{2,1,0:T(8,128)(2,1)S(1)}, u32[]{:S(2)}, u32[]{:S(2)}) async-start(bf16[32,48,256]{2,1,0:T(8,128)(2,1)} %bitcast.6), calls=%async_computation.1 | async-start | bytes 1572864 | tf_op jit(solution)/shard_map/all_to_all | solution.py:435
  39.1 1.4 %shard_map.83 = (s32[1,1536]{1,0:T(1,128)S(1)}, s32[3,8,4,128]{3,2,1,0:T(4,128)S(1)}, s32[8,128]{1,0:T(8,128)S(1)}) custom-call(s32[32,128]{1,0:T(8,128)S(1)} %bitcast.10), custom_call_target="tpu_custom_call" | custom-call | flops 75497472 | bytes 75776 | tf_op jit(solution)/shard_map/pallas_call | solution.py:41
  40.6 2.4 %shard_map.79 = bf16[512,256]{1,0:T(8,128)(2,1)} custom-call(bf16[512,256]{1,0:T(8,128)(2,1)S(1)} %get-tuple-element.15.refs_0_.q_ref, f32[1,512]{1,0:T(1,128)S(1)} %shard_map.78.lse_ref, s32[1,512]{1,0:T(1,128)S(1)} %get-tuple-element.19.pos_ref, bf16[512,256]{1,0:T(8,128)(2,1)S(1)} %get-tuple-element.16.refs_1_.refs_0_.k_ref, ...), custom_call_target="tpu_custom_call" | custom-call | flops 1073741824 | bytes 1576960 | tf_op jit(solution)/shard_map/pallas_call | solution.py:41
  42.9 16.4 %all-to-all-done.1 = bf16[32,48,256]{2,1,0:T(8,128)(2,1)S(1)} async-done(((bf16[32,48,256]{2,1,0:T(8,128)(2,1)}), bf16[32,48,256]{2,1,0:T(8,128)(2,1)S(1)}, u32[]{:S(2)}, u32[]{:S(2)}) %all-to-all-start.1) | async-done | bytes 786464 | tf_op jit(solution)/shard_map/all_to_all | solution.py:435
  59.4 4.9 %shard_map.84 = bf16[16384,256]{1,0:T(8,128)(2,1)} custom-call(s32[8,128]{1,0:T(8,128)S(1)} %get-tuple-element.23.count_ref, bf16[1536,256]{1,0:T(8,128)(2,1)S(1)} %bitcast.9, s32[1,1536]{1,0:T(1,128)S(1)} %get-tuple-element.25.rank_ref, s32[3,8,4,128]{3,2,1,0:T(4,128)S(1)} %get-tuple-element.26.sorted_ref), custom_call_target="tpu_custom_call" | custom-call | flops 1207959552 | bytes 8388608 | tf_op jit(solution)/shard_map/pallas_call | solution.py:438
Async XLA Ops:
  0.6 9.3 %collective-permute-start = (bf16[512,256]{1,0:T(8,128)(2,1)}, bf16[512,256]{1,0:T(8,128)(2,1)S(1)}, u32[]{:S(2)}, u32[]{:S(2)}) collective-permute-start(bf16[512,256]{1,0:T(8,128)(2,1)} %refs_2_.1), channel_id=1, source_target_pairs={{0,8},{4,12},{8,16},{12,20},{16,24},{20,28},{24,0},{28,4},{1,9},{5... | collective-permute-start | bytes 786440 | tf_op jit(solution)/shard_map/ppermute | solution.py:25
  2.7 12.8 %collective-permute-start.3 = (bf16[512,256]{1,0:T(8,128)(2,1)}, bf16[512,256]{1,0:T(8,128)(2,1)S(1)}, u32[]{:S(2)}, u32[]{:S(2)}) collective-permute-start(bf16[512,256]{1,0:T(8,128)(2,1)} %refs_3_.1), channel_id=1, source_target_pairs={{0,24},{4,28},{8,0},{12,4},{16,8},{20,12},{24,16},{28,20},{1,25},{... | collective-permute-start | bytes 786440 | tf_op jit(solution)/shard_map/ppermute | solution.py:25
  3.7 19.9 %collective-permute-start.2 = (bf16[512,256]{1,0:T(8,128)(2,1)}, bf16[512,256]{1,0:T(8,128)(2,1)S(1)}, u32[]{:S(2)}, u32[]{:S(2)}) collective-permute-start(bf16[512,256]{1,0:T(8,128)(2,1)} %refs_2_.1), channel_id=1, source_target_pairs={{0,4},{4,16},{8,12},{12,24},{16,20},{20,0},{24,28},{28,8},{1,5},{5... | collective-permute-start | bytes 786440 | tf_op jit(solution)/shard_map/ppermute | solution.py:25
  9.9 14.8 %collective-permute-start.1 = (bf16[512,256]{1,0:T(8,128)(2,1)S(1)}, bf16[512,256]{1,0:T(8,128)(2,1)S(1)}, u32[]{:S(2)}, u32[]{:S(2)}) collective-permute-start(bf16[512,256]{1,0:T(8,128)(2,1)S(1)} %collective-permute-done.refs_3_.refs_2_), channel_id=1, source_target_pairs={{0,4},{4,0},{8,12},{12,8},{16,20},{20,16},{24,28},{28,24},{1,5},{5... | collective-permute-start | bytes 786440 | tf_op jit(solution)/shard_map/ppermute | solution.py:25
  12.0 18.6 %collective-permute-start.4 = (bf16[512,256]{1,0:T(8,128)(2,1)}, bf16[512,256]{1,0:T(8,128)(2,1)S(1)}, u32[]{:S(2)}, u32[]{:S(2)}) collective-permute-start(bf16[512,256]{1,0:T(8,128)(2,1)} %refs_3_.1), channel_id=1, source_target_pairs={{0,20},{4,0},{8,28},{12,8},{16,4},{20,16},{24,12},{28,24},{1,21},{... | collective-permute-start | bytes 786440 | tf_op jit(solution)/shard_map/ppermute | solution.py:25
  15.5 16.0 %collective-permute-start.7 = (bf16[512,256]{1,0:T(8,128)(2,1)S(1)}, bf16[512,256]{1,0:T(8,128)(2,1)S(1)}, u32[]{:S(2)}, u32[]{:S(2)}) collective-permute-start(bf16[512,256]{1,0:T(8,128)(2,1)S(1)} %collective-permute-done.3.refs_0_), channel_id=1, source_target_pairs={{0,4},{4,0},{8,12},{12,8},{16,20},{20,16},{24,28},{28,24},{1,5},{5... | collective-permute-start | bytes 786440 | tf_op jit(solution)/shard_map/ppermute | solution.py:25
  18.8 14.8 %all-to-all-start = ((s32[32,1,128]{2,1,0:T(1,128)}), s32[32,1,128]{2,1,0:T(1,128)S(1)}, u32[]{:S(2)}, u32[]{:S(2)}) async-start(s32[32,1,128]{2,1,0:T(1,128)} %bitcast.4), calls=%async_computation | async-start | bytes 32768 | tf_op jit(solution)/shard_map/all_to_all | solution.py:367
  25.2 5.4 %collective-permute-start.6 = (f32[1,512]{1,0:T(1,128)S(1)}, f32[1,512]{1,0:T(1,128)S(1)}, u32[]{:S(2)}, u32[]{:S(2)}) collective-permute-start(f32[1,512]{1,0:T(1,128)S(1)} %shard_map.78.lse_ref), channel_id=1, source_target_pairs={{0,20},{4,0},{8,28},{12,8},{16,4},{20,16},{24,12},{28,24},{1,21},{... | collective-permute-start | bytes 6152 | tf_op jit(solution)/shard_map/ppermute | solution.py:25
  25.5 3.1 %collective-permute-start.5 = (f32[1,512]{1,0:T(1,128)S(1)}, f32[1,512]{1,0:T(1,128)S(1)}, u32[]{:S(2)}, u32[]{:S(2)}) collective-permute-start(f32[1,512]{1,0:T(1,128)S(1)} %shard_map.78.lse_ref), channel_id=1, source_target_pairs={{0,24},{4,28},{8,0},{12,4},{16,8},{20,12},{24,16},{28,20},{1,25},{... | collective-permute-start | bytes 6152 | tf_op jit(solution)/shard_map/ppermute | solution.py:25
  28.7 2.8 %collective-permute-start.8 = (f32[1,512]{1,0:T(1,128)S(1)}, f32[1,512]{1,0:T(1,128)S(1)}, u32[]{:S(2)}, u32[]{:S(2)}) collective-permute-start(f32[1,512]{1,0:T(1,128)S(1)} %collective-permute-done.5.refs_2_), channel_id=1, source_target_pairs={{0,4},{4,0},{8,12},{12,8},{16,20},{20,16},{24,28},{28,24},{1,5},{5... | collective-permute-start | bytes 6152 | tf_op jit(solution)/shard_map/ppermute | solution.py:25
  33.6 25.8 %all-to-all-start.1 = ((bf16[32,48,256]{2,1,0:T(8,128)(2,1)}), bf16[32,48,256]{2,1,0:T(8,128)(2,1)S(1)}, u32[]{:S(2)}, u32[]{:S(2)}) async-start(bf16[32,48,256]{2,1,0:T(8,128)(2,1)} %bitcast.6), calls=%async_computation.1 | async-start | bytes 1572864 | tf_op jit(solution)/shard_map/all_to_all | solution.py:435
